TPU v7x, 32 devices: a whole 2x2x4 slice. The times are simulated.
32 devices in a mesh: tm: 4 (over y, x), rows: 8 (over z, core).
Axes of the slice: x: 2, y: 2, z: 4, core: 2. Of those that a mesh axis runs over, the one named last changes fastest.
Arguments:
- features: bfloat16 [48, 1280, 512], P('rows', 'tm'), may hold values from -6 to 6
- cotangent: bfloat16 [48, 1280, 512], P('rows', 'tm'), may hold values from -6 to 6
- state_bank: float32 [48, 512, 32], P('rows', 'tm'), may hold values from -6 to 6
- state_source: int32 [48], P('rows'), may hold values from 0 to 5, as said below
- master: float32 [88, 256, 256], P('tm', 'rows'), may hold values from -0.13258252 to 0.13258252
- left_stats: float32 [88, 256, 256], P('tm', 'rows'), may hold values from -7.68 to 64
- right_stats: float32 [88, 256, 256], P('tm', 'rows'), may hold values from -7.68 to 64
- left_root: float32 [88, 256, 256], P('tm', 'rows'), may hold values from -0.2 to 1.6
- right_root: float32 [88, 256, 256], P('tm'), may hold values from -0.2 to 1.6
- small_params: float32 [20, 512], replicated, may hold values from -1 to 1.5
- decay_logs: float32 [8, 32], P('tm'), may hold values from -7 to -1.5
- state_mix: float32 [2, 512, 32], P(None, 'tm'), may hold values from -0.6 to 0.6
Outputs:
- layer_out: bfloat16 [48, 1280, 512], P('rows', 'tm')
- grad_features: float32 [48, 1280, 512], P('rows', 'tm')
- grad_state: float32 [48, 512, 32], P('rows', 'tm')
- grad_blocks: float32 [88, 256, 256], P('tm', 'rows')
- new_left: float32 [88, 256, 256], P('tm', 'rows')
- new_right: float32 [88, 256, 256], P('tm', 'rows')
- new_master: float32 [88, 256, 256], P('tm', 'rows')
- new_copy: bfloat16 [88, 256, 256], P('tm', 'rows')
- grad_small: float32 [20, 512], P(None, 'tm')
- new_small: float32 [20, 512], P(None, 'tm')
- grad_decay: float32 [8, 32], P('tm')
- grad_mix: float32 [2, 512, 32], P(None, 'tm')
- new_decay: float32 [8, 32], P('tm')
- new_mix: float32 [2, 512, 32], P(None, 'tm')
Inputs may be any that keep to these rules, and one draw needn't show every extreme that they name: `state_source`: within each aligned block of 6 rows the values are a permutation of 0 to 5.
All inputs are finite; a program needn't handle non-finite values.
Results may differ from a plain program's by a relative error of at most 0.018.
Values may be sent and summed in bfloat16 or wider, within the bound.
A program may use at most 320 MiB of HBM per device.

v0:
```python
from functools import partial
import math

import jax
import jax.numpy as jnp
from jax import lax
from jax.experimental import pallas as pl
from jax.experimental.pallas import tpu as pltpu
from jax.sharding import PartitionSpec as P

D = 512
FF = 2048
NST = 32
KW = 15
BS = 256
HEADS = 8
HALF = 64
LANES = 128
SUB = 16
GROUP = 5
BOTH = 2
PAD = 8
VMEM_BYTES = 60 * 1024 * 1024

rate_blocks = 0.1
rate_small = 0.5
bf16 = jnp.bfloat16
f32 = jnp.float32


def shape(dims, dtype=f32):
    return jax.ShapeDtypeStruct(dims, dtype)


def mm(a, b):
    return jnp.dot(a, b, preferred_element_type=f32)


def mm_nt(a, b):
    return lax.dot_general(a, b, (((1,), (1,)), ((), ())), preferred_element_type=f32)


def mm_tn(a, b):
    return lax.dot_general(a, b, (((0,), (0,)), ((), ())), preferred_element_type=f32)


def sigmoid(v):
    return 0.5 * jnp.tanh(0.5 * v) + 0.5


def norm(v):
    center = v - jnp.mean(v, axis=-1, keepdims=True)
    spread = jnp.mean(center * center, axis=-1, keepdims=True)
    inv = lax.rsqrt(spread + 1e-05)
    return center * inv, inv


def norm_back(hat, inv, scale, incoming):
    scaled = incoming * scale
    mean_one = jnp.mean(scaled, axis=-1, keepdims=True)
    mean_two = jnp.mean(scaled * hat, axis=-1, keepdims=True)
    return inv * (scaled - mean_one - hat * mean_two)


def flat(ref):
    v = ref[...]
    return v.reshape(-1, v.shape[-1])


def put_rows(ref, v):
    ref[...] = v.astype(ref.dtype).reshape(ref.shape)


def fold8(v):
    return jnp.sum(v.reshape(-1, 8, v.shape[-1]), axis=0)


def load_matrices(stack, plan, sem):
    copies = []
    for first, dst in plan:
        down, across = dst.shape[0] // BS, dst.shape[1] // BS
        for i in range(down):
            for j in range(across):
                copies.append(
                    pltpu.make_async_copy(
                        stack.at[first + i * across + j],
                        dst.at[pl.ds(i * BS, BS), pl.ds(j * BS, BS)],
                        sem,
                    )
                )
    for copy in copies:
        copy.start()
    for copy in copies:
        copy.wait()


def store_blocks(plan, scaling, grads, stage, sem):
    copies = []
    for acc, first, transposed in plan:
        rows, cols = acc.shape
        down, across = (cols, rows) if transposed else (rows, cols)
        for i in range(down // BS):
            for j in range(across // BS):
                slot = len(copies)
                if transposed:
                    part = (acc[pl.ds(j * BS, BS), pl.ds(i * BS, BS)] * scaling).T
                else:
                    part = acc[pl.ds(i * BS, BS), pl.ds(j * BS, BS)] * scaling
                stage[slot] = part.astype(bf16)
                copy = pltpu.make_async_copy(
                    stage.at[slot], grads.at[first + i * (across // BS) + j], sem
                )
                copy.start()
                copies.append(copy)
    for copy in copies:
        copy.wait()


def head_mask():
    row = lax.broadcasted_iota(jnp.int32, (HEADS * NST, D), 0) // NST
    col = lax.broadcasted_iota(jnp.int32, (HEADS * NST, D), 1) // HALF
    return (row == col).astype(f32)


def spread_heads(v, mask):
    return (jnp.concatenate([v] * HEADS, axis=0) * mask).astype(bf16)


def local_states(table, v, out):
    frames = table.shape[1]
    first = lax.broadcasted_iota(jnp.int32, (NST, LANES), 1) < HALF
    for b in range(out.shape[0]):
        for g in range(D // LANES):
            here = v[b * frames : (b + 1) * frames, g * LANES : (g + 1) * LANES]
            both = mm(table[pl.ds(2 * NST * g, 2 * NST), :], here)
            picked = jnp.where(first, both[:NST], both[NST:])
            out[b, :, pl.ds(g * LANES, LANES)] = picked.astype(out.dtype)


ANY = pl.BlockSpec(memory_space=pl.ANY)
PARAMS = pltpu.CompilerParams(
    dimension_semantics=("arbitrary",), vmem_limit_bytes=VMEM_BYTES
)


def vm(*dims, dtype=f32):
    return pltpu.VMEM(dims, dtype)


def peers():
    place, row = lax.axis_index("tm"), lax.axis_index("rows")
    return place, row // 2, row % 2


def square(place):
    x, y = place % 2, place // 2
    return 2 * y + 1 - x, 2 * (1 - y) + x, 2 * (1 - y) + 1 - x


def at(place, level, core):
    return {"tm": place, "rows": level * 2 + core}


def remote(src, dst, send, recv, device):
    return pltpu.make_async_remote_copy(
        src_ref=src,
        dst_ref=dst,
        send_sem=send,
        recv_sem=recv,
        device_id=device,
        device_id_type=pl.DeviceIdType.MESH,
    )


def signal(sem, device):
    pl.semaphore_signal(sem, inc=1, device_id=device, device_id_type=pl.DeviceIdType.MESH)


def chunk_ranges(count, chunks):
    edges = [count * c // chunks for c in range(chunks + 1)]
    out = []
    for first, end in zip(edges[:-1], edges[1:]):
        middle = (first + end + 1) // 2
        out.append((first, end, middle))
    return out


class Gather:
    def __init__(self, piece, stack, sems, chunks=1):
        self.piece, self.stack, self.sems = piece, stack, sems
        self.place, self.level, self.core = peers()
        self.xp, self.yp, self.dp = square(self.place)
        self.levels = stack.shape[2]
        self.ranges = chunk_ranges(stack.shape[1], chunks)
        self.all = range(chunks)

    def own(self, c):
        first, end, unused = self.ranges[c]
        n = pl.ds(first, end - first)
        spot = self.stack.at[self.place, n, self.level, self.core]
        return pltpu.make_async_copy(self.piece.at[n], spot, self.sems["own"].at[c])

    def z(self, c, d):
        first, end, unused = self.ranges[c]
        n = pl.ds(first, end - first)
        spot = self.stack.at[self.place, n, self.level, self.core]
        send, recv = self.sems["zs"].at[c, d - 1], self.sems["zr"].at[c, d - 1]
        target = (self.level + d) % self.levels
        return remote(self.piece.at[n], spot, send, recv, at(self.place, target, self.core))

    def z_start(self, c):
        self.own(c).start()
        for d in range(1, self.levels):
            self.z(c, d).start()

    def z_arrive(self, c):
        self.own(c).wait()
        for d in range(1, self.levels):
            self.z(c, d).wait_recv()

    def z_end(self, c):
        for d in range(1, self.levels):
            self.z(c, d).wait_send()

    def part(self, name, c, i, owner, first, end, device):
        spot = self.stack.at[owner, pl.ds(first, end - first), :, self.core]
        send, recv = self.sems[name + "s"].at[c, i], self.sems[name + "r"].at[c, i]
        return remote(spot, spot, send, recv, device)

    def x(self, c, i):
        first, end, mid = self.ranges[c]
        what = ((self.place, first, mid), (self.place, mid, end), (self.yp, mid, end))[i]
        return self.part("x", c, i, *what, at(self.xp, self.level, self.core))

    def y(self, c, i):
        first, end, mid = self.ranges[c]
        what = ((self.place, mid, end), (self.place, first, mid), (self.xp, first, mid))[i]
        return self.part("y", c, i, *what, at(self.yp, self.level, self.core))

    def other(self, c, i):
        first, end, mid = self.ranges[c]
        what = (
            (self.place, first, end),
            (self.xp, first, mid),
            (self.yp, mid, end),
            (self.xp, mid, end),
            (self.yp, first, mid),
            (self.dp, first, mid),
            (self.dp, mid, end),
        )[i]
        return self.part("c", c, i, *what, at(self.place, self.level, 1 - self.core))

    def spread(self, c):
        for copy in (self.x(c, 0), self.y(c, 0), self.x(c, 1), self.y(c, 1), self.other(c, 0)):
            copy.start()

    def forward(self, c):
        self.x(c, 0).wait_recv()
        self.y(c, 2).start()
        self.y(c, 0).wait_recv()
        self.x(c, 2).start()
        self.other(c, 1).start()
        self.other(c, 2).start()
        self.x(c, 1).wait_recv()
        self.other(c, 3).start()
        self.y(c, 1).wait_recv()
        self.other(c, 4).start()

    def finish(self, c):
        self.y(c, 2).wait_recv()
        self.other(c, 5).start()
        self.x(c, 2).wait_recv()
        self.other(c, 6).start()

    def end(self, c):
        for i in range(7):
            self.other(c, i).wait_recv()
        for i in range(7):
            self.other(c, i).wait_send()
        for i in range(3):
            self.x(c, i).wait_send()
            self.y(c, i).wait_send()


Z_SEMS = ("own", "zs", "zr")
XY_SEMS = ("xs", "xr", "ys", "yr", "cs", "cr")


def gather_sems(names, levels, chunks=1):
    width = {"own": (), "z": (levels - 1,), "x": (3,), "y": (3,), "c": (7,)}
    key = lambda name: name if name == "own" else name[0]
    return [pltpu.SemaphoreType.DMA((chunks,) + width[key(name)]) for name in names]


def block_sets():
    ffn, mix = D // BS * (FF // BS), (D // BS) ** 2
    ids = lambda *ranges: [b for first, end in ranges for b in range(first, end)]
    return (
        ids((0, 2 * ffn), (4 * ffn, 4 * ffn + mix)),
        ids((4 * ffn + mix, 4 * ffn + 5 * mix)),
        ids((2 * ffn, 4 * ffn), (4 * ffn + 5 * mix, 4 * ffn + 6 * mix)),
    )


def move_runs(ids, places, count):
    runs, each = [], len(ids) // places
    for index, b in enumerate(ids):
        owner, k, v, j = b // count, b % count, index // each, index % each
        if runs:
            o0, k0, v0, j0, n0 = runs[-1]
            if (o0, v0) == (owner, v) and k0 + n0 == k:
                runs[-1] = (o0, k0, v0, j0, n0 + 1)
                continue
        runs.append((owner, k, v, j, 1))
    return runs


def greet(devices):
    barrier = pltpu.get_barrier_semaphore()
    for device in devices:
        signal(barrier, device)


def met(count):
    pl.semaphore_wait(pltpu.get_barrier_semaphore(), count)


def gather_kernel(
    master, pack, first, pair, rest, pack_all,
    rounded, piece, piece_pair, piece_rest, run_send, run_recv, pk_send, pk_recv, *sems,
):
    place, level, core = peers()
    others = square(place)
    levels = first.shape[2]
    greet([at(other, level, core) for other in others] + [at(place, level, 1 - core)])
    greet([at(place, (level + d) % levels, core) for d in range(1, levels)])
    rounded[...] = master[...].astype(bf16)
    met(3 + levels)
    moves = []
    for ids, target in zip(block_sets(), (piece, piece_pair, piece_rest)):
        for run in move_runs(ids, first.shape[0], master.shape[0]):
            moves.append((len(moves), target) + run)

    def move(index, target, owner, k, v, j, n):
        src, dst = rounded.at[pl.ds(k, n)], target.at[pl.ds(j, n)]
        if owner == v:
            return pltpu.make_async_copy(src, dst, run_send.at[index])
        return remote(src, dst, run_send.at[index], run_recv.at[index], at(v, level, core))

    def arrive(entry):
        index, target, owner, k, v, j, n = entry
        if owner == v:
            pl.when(place == v)(lambda: move(*entry).wait())
        else:
            pl.when(place == v)(lambda: move(*entry).wait_recv())

    for entry in moves:
        pl.when(place == entry[2])(lambda entry=entry: move(*entry).start())
    own_pack = pltpu.make_async_copy(pack, pack_all.at[place], pk_send.at[3])
    own_pack.start()
    packs = [
        remote(pack, pack_all.at[place], pk_send.at[d], pk_recv.at[d], at(other, level, core))
        for d, other in enumerate(others)
    ]
    for copy in packs:
        copy.start()
    for entry in moves:
        if entry[1] is piece:
            arrive(entry)
    names = Z_SEMS + XY_SEMS
    chunks = sems[0].shape[0]
    it = Gather(piece, first, dict(zip(names, sems)), chunks)
    later, sems = [], sems[len(names) :]
    for i, (what, stack) in enumerate(((piece_pair, pair), (piece_rest, rest))):
        later.append(Gather(what, stack, dict(zip(Z_SEMS, sems[3 * i : 3 * i + 3]))))
    it.z_start(0)
    for c in it.all:
        it.z_arrive(c)
        it.spread(c)
        if c == 0:
            for ahead in range(1, chunks):
                it.z_start(ahead)
            for entry in moves:
                if entry[1] is not piece:
                    arrive(entry)
        if c == chunks - 1:
            for other_set in later:
                other_set.z_start(0)
        if c >= 1:
            it.forward(c - 1)
        if c >= 2:
            it.finish(c - 2)
    it.forward(chunks - 1)
    for c in range(max(chunks - 2, 0), chunks):
        it.finish(c)
    for c in it.all:
        it.end(c)
        it.z_end(c)
    for other_set in later:
        other_set.z_arrive(0)
        other_set.z_end(0)
    for entry in moves:
        if entry[2] != entry[4]:
            pl.when(place == entry[2])(lambda entry=entry: move(*entry).wait_send())
    own_pack.wait()
    for copy in packs:
        copy.wait()


def gather_first(master, pack, parts, devices, chunks=3):
    count, slab, cols = master.shape
    levels = devices // 2
    each = [len(ids) // parts for ids in block_sets()]
    runs = sum(len(move_runs(ids, parts, count)) for ids in block_sets())
    dma = lambda *dims: pltpu.SemaphoreType.DMA(dims)
    return pl.pallas_call(
        gather_kernel,
        in_specs=[pl.BlockSpec(memory_space=pltpu.VMEM), ANY],
        out_specs=[ANY] * 4,
        out_shape=[
            shape((parts, each[0], levels, 2, slab, cols), bf16),
            shape((parts, each[1], levels, 2, slab, cols), bf16),
            shape((parts, each[2], levels, 2, slab, cols), bf16),
            shape((parts,) + pack.shape, pack.dtype),
        ],
        scratch_shapes=[
            vm(count, slab, cols, dtype=bf16),
            vm(each[0], slab, cols, dtype=bf16),
            vm(each[1], slab, cols, dtype=bf16),
            vm(each[2], slab, cols, dtype=bf16),
            dma(runs),
            dma(runs),
            dma(4),
            dma(3),
        ]
        + gather_sems(Z_SEMS + XY_SEMS, levels, chunks)
        + gather_sems(Z_SEMS, levels) * 2,
        compiler_params=pltpu.CompilerParams(
            collective_id=1, has_side_effects=True, vmem_limit_bytes=VMEM_BYTES
        ),
        name="gather_first",
    )(master, pack)


def ffa_forward_kernel(feat, small, stack, mfin, *refs):
    step, last = pl.program_id(0), pl.num_programs(0) - 1
    pair = None
    if len(refs) > 9:
        refs, sems = refs[1:7] + refs[7:11], refs[11:]
        pair = Gather(None, refs[5], dict(zip(XY_SEMS, sems)))
        refs = refs[:5] + refs[6:]
    x1_o, inner_o, act_o, u_o, f_o, wi, wo, wu, sem = refs

    @pl.when(step == 0)
    def _():
        if pair is not None:
            place, level, core = peers()
            greet([at(other, level, core) for other in square(place)])
            greet([at(place, level, 1 - core)])
        ffn, mix = D // BS * (FF // BS), (D // BS) ** 2
        load_matrices(stack, ((0, wi), (ffn, wo), (2 * ffn, wu)), sem)
        if pair is not None:
            met(4)
            pair.spread(0)

    x0 = flat(feat).astype(f32)
    hat, unused = norm(x0)
    inner = mm((hat * small[0:1]).astype(bf16), wi[...])
    act = (inner * sigmoid(inner)).astype(bf16)
    put_rows(inner_o, inner)
    put_rows(act_o, act)
    x1 = x0 + 0.5 * mm(act, wo[...])
    put_rows(x1_o, x1)
    hat, unused = norm(x1)
    u = mm((hat * small[1:2]).astype(bf16), wu[...]).astype(bf16)
    put_rows(u_o, u)
    local_states(mfin, u, f_o)
    if pair is not None:
        pl.when(step == last - 1)(lambda: pair.forward(0))

        @pl.when(step == last)
        def _():
            pair.finish(0)
            pair.end(0)


def pack_heads(ref, rows):
    first = lax.broadcasted_iota(jnp.int32, (ref.shape[1], LANES), 1) < HALF
    low, high = [], []
    for p in range(rows // 2):
        a, b = ref[2 * p].astype(f32), ref[2 * p + 1].astype(f32)
        low.append(jnp.where(first, a, pltpu.roll(b, HALF, 1)).astype(bf16))
        high.append(jnp.where(first, pltpu.roll(a, HALF, 1), b).astype(bf16))
    return jnp.concatenate(low, axis=1), jnp.concatenate(high, axis=1)


def pack_params(v, rows):
    first = lax.broadcasted_iota(jnp.int32, v.shape, 1) < HALF
    rolled = pltpu.roll(v, HALF, 1)
    low = jnp.where(first, v, rolled)
    high = jnp.where(first, rolled, v)
    return (
        jnp.concatenate([low] * (rows // 2), axis=1),
        jnp.concatenate([high] * (rows // 2), axis=1),
    )


def unpack_pair(low, high, p):
    low = low[:, p * LANES : (p + 1) * LANES]
    high = high[:, p * LANES : (p + 1) * LANES]
    first = lax.broadcasted_iota(jnp.int32, low.shape, 1) < HALF
    return (
        jnp.where(first, low, pltpu.roll(high, HALF, 1)),
        jnp.where(first, pltpu.roll(low, HALF, 1), high),
    )


def swap_states(mine, whole, first_step, last_step, own_sem, send, recv, pair=None):
    place, level, core = peers()
    parts = whole.shape[0]
    others = [(place + d) % parts for d in range(1, parts)]

    def copies():
        return [
            remote(mine, whole.at[place], send.at[d], recv.at[d], at(other, level, core))
            for d, other in enumerate(others)
        ]

    own = lambda: pltpu.make_async_copy(mine, whole.at[place], own_sem)

    @pl.when(first_step)
    def _():
        barrier = pltpu.get_barrier_semaphore()
        for other in others:
            signal(barrier, at(other, level, core))
        if pair is not None:
            signal(barrier, at(place, level, 1 - core))
        own().start()

    def end():
        @pl.when(first_step)
        def _():
            met(parts - 1 + (pair is not None))
            for copy in copies():
                copy.start()
            if pair is not None:
                pair.spread(0)

        if pair is not None:
            step = pl.program_id(0)

            @pl.when(step == pl.num_programs(0) - 2)
            def _():
                pair.forward(0)

            @pl.when(last_step)
            def _():
                pair.finish(0)
                pair.end(0)

        @pl.when(last_step)
        def _():
            own().wait()
            for copy in copies():
                copy.wait()

    return end


def tile_lanes(v, width):
    return jnp.concatenate([v] * (width // LANES), axis=1)


def conv_forward_kernel(u, ends, tab_a, tab_b, power, coup, taps, *refs):
    step = pl.program_id(0)
    pair = None
    if len(refs) > 6:
        refs, sems = refs[1:7] + refs[7:8], refs[8:]
        pair = Gather(None, refs[2], dict(zip(XY_SEMS, sems)), 2)
        refs = refs[:2] + refs[3:]
    y_o, ends_all, pad, own_sem, send, recv = refs
    end_swap = swap_states(
        ends, ends_all, step == 0, step == pl.num_programs(0) - 1, own_sem, send, recv, pair
    )
    rows, frames = u.shape[0], u.shape[1]
    span = GROUP * SUB
    coup_both = pack_params(coup[...], rows)
    packed = pack_heads(u, rows)
    width = packed[0].shape[1]
    results = []
    for h in range(2):
        scale = [tile_lanes(power[h, i], width) for i in range(GROUP)]
        carry = None
        outs = []
        for g in range(frames // span):
            local = mm(tab_a[h, 0], packed[h][g * span : (g + 1) * span])
            parts = [local[i * NST : (i + 1) * NST] for i in range(GROUP)]
            if carry is None:
                states = [jnp.zeros_like(parts[0])] + parts[:-1]
                carry = parts[-1]
            else:
                states = [carry] + [parts[i] + scale[i] * carry for i in range(GROUP - 1)]
                carry = parts[-1] + scale[-1] * carry
            scaled = jnp.concatenate([v * coup_both[h] for v in states], axis=0)
            outs.append(mm(tab_b[h, 1], scaled.astype(bf16)))
        results.append(jnp.concatenate(outs, axis=0))
    for p in range(rows // 2):
        one, two = unpack_pair(results[0], results[1], p)
        y_o[2 * p] = one
        y_o[2 * p + 1] = two
    pad[0:SUB] = jnp.zeros((SUB, LANES), f32)
    chunk = frames // 5

    def one_row(i, carry):
        pad[pl.ds(SUB, frames)] = u[i].astype(f32)
        for r in range(0, frames, chunk):
            acc = y_o[i, pl.ds(r, chunk)].reshape(-1, SUB, LANES)
            for d in range(SUB):
                piece = pad[pl.ds(SUB + r - d, chunk)].reshape(-1, SUB, LANES)
                acc = acc + piece * taps[d][None]
            y_o[i, pl.ds(r, chunk)] = acc.reshape(chunk, LANES)
        return carry

    lax.fori_loop(0, rows, one_row, 0)
    end_swap()


def edge_sender(edges, low_all, high_all, zeros, send, recv, zero_sem, step, per, rest=None):
    place, level, core = peers()
    parts = lax.axis_size("tm")
    steps = edges.shape[0]
    not_first, not_last = place > 0, place < parts - 1
    after = (place + 1) % parts
    before = (place + parts - 1) % parts

    def up(i):
        return remote(
            edges.at[i, 1], low_all.at[i], send.at[0, i], recv.at[0, i], at(after, level, core)
        )

    def down(i):
        return remote(
            edges.at[i, 0], high_all.at[i], send.at[1, i], recv.at[1, i], at(before, level, core)
        )

    def blank(ref, i, k):
        return pltpu.make_async_copy(zeros, ref.at[i], zero_sem.at[k])

    @pl.when(step == 0)
    def _():
        if rest is None:
            pl.when(not_last)(lambda: greet([at(after, level, core)]))
            pl.when(not_first)(lambda: greet([at(before, level, core)]))
        else:
            greet([at(other, level, core) for other in square(place)])
            greet([at(place, level, 1 - core)])
        zeros[...] = jnp.zeros_like(zeros)

        @pl.when(place == 0)
        def _():
            for i in range(steps):
                blank(low_all, i, 0).start()

        @pl.when(place == parts - 1)
        def _():
            for i in range(steps):
                blank(high_all, i, 1).start()

    def put(v):
        @pl.when(step == 0)
        def _():
            below = (place + parts - 1) // parts
            above = (2 * parts - 2 - place) // parts
            met(below + above if rest is None else parts)
            if rest is not None:
                rest.spread(1)

        if rest is not None:
            pl.when(step == steps // per // 2)(lambda: rest.forward(1))
            pl.when(step == steps // per - 1)(lambda: rest.finish(1))

        frames = v.shape[0] // per
        for b in range(per):
            row = step * per + b
            edges[row, 0] = v[b * frames : b * frames + PAD]
            edges[row, 1] = v[(b + 1) * frames - PAD : (b + 1) * frames]
            pl.when(not_last)(lambda row=row: up(row).start())
            pl.when(not_first)(lambda row=row: down(row).start())

        @pl.when(step == steps // per - 1)
        def _():
            for i in range(steps):
                pl.when(not_last)(lambda i=i: up(i).wait_send())
                pl.when(not_first)(lambda i=i: down(i).wait_send())
                pl.when(not_first)(lambda i=i: up(i).wait_recv())
                pl.when(not_last)(lambda i=i: down(i).wait_recv())

            if rest is not None:
                rest.end(1)

            @pl.when(place == 0)
            def _():
                for i in range(steps):
                    blank(low_all, i, 0).wait()

            @pl.when(place == parts - 1)
            def _():
                for i in range(steps):
                    blank(high_all, i, 1).wait()

    return put


def mixer_out_kernel(
    y, ends_all, starts, weigh, coup, x1, small, stack, pfull, *refs
):
    step = pl.program_id(0)
    rest = None
    if len(refs) > 16:
        refs, sems = refs[1:8] + refs[8:18], refs[18:]
        rest = Gather(None, refs[7], dict(zip(XY_SEMS, sems)), 2)
        refs = refs[:7] + refs[8:]
    ys_o, gated_o, x2_o, pw_o, g_o, low_o, high_o, wo, wp, mask, sem = refs[:11]
    edges, zeros, send, recv, zero_sem = refs[11:]
    put = edge_sender(edges, low_o, high_o, zeros, send, recv, zero_sem, step, 1, rest)

    @pl.when(step == 0)
    def _():
        ffn, mix = D // BS * (FF // BS), (D // BS) ** 2
        load_matrices(stack, ((0, wo), (2 * mix, wp)), sem)
        mask[...] = head_mask()

    came = weigh[0] * ends_all[0, 0].astype(f32)
    for i in range(1, ends_all.shape[0]):
        came = came + weigh[i] * ends_all[i, 0].astype(f32)
    zin = coup[...] * came + weigh[ends_all.shape[0]] * starts[0]
    ys = (y[0] + mm(pfull[...], spread_heads(zin, mask[...]))).astype(bf16)
    ys_o[0] = ys
    gated = mm(ys, wo[...])
    gated_o[0] = gated.astype(bf16)
    x2 = x1[0] + gated[:, :D] * sigmoid(gated[:, D:])
    x2_o[0] = x2
    hat, unused = norm(x2)
    pw = mm((hat * small[2:3]).astype(bf16), wp[...])
    pw_o[0] = pw.astype(bf16)
    g = (pw[:, :D] * sigmoid(pw[:, D:])).astype(bf16)
    g_o[0] = g
    put(g)


def fill_pad(pad, low, body, high):
    frames = body.shape[0]
    for g in range(D // LANES):
        lanes = slice(g * LANES, (g + 1) * LANES)
        pad[g, 0:PAD] = low[:, lanes].astype(f32)
        pad[g, pl.ds(PAD, frames)] = body[:, lanes].astype(f32)
        pad[g, pl.ds(PAD + frames, PAD)] = high[:, lanes].astype(f32)


def ffb_kernel(
    scale, g, low, high, x2, cot, small, stack,
    out_o, dx3_o, dq_o, grads, gain_o, low_o, high_o,
    wi, wo, wq, acc_in, acc_out, acc_q, pad, q_s, stage, k_act, k_din, k_n, k_dp, k_a, k_dpq, sem,
    edges, zeros, send, recv, zero_sem,
):
    step = pl.program_id(0)
    frames = g.shape[1]
    put = edge_sender(edges, low_o, high_o, zeros, send, recv, zero_sem, step, 1)

    @pl.when(step == 0)
    def _():
        ffn, mix = D // BS * (FF // BS), (D // BS) ** 2
        load_matrices(stack, ((0, wi), (ffn, wo), (2 * ffn, wq)), sem)
        acc_in[...] = jnp.zeros_like(acc_in)
        acc_out[...] = jnp.zeros_like(acc_out)
        acc_q[...] = jnp.zeros_like(acc_q)
        gain_o[...] = jnp.zeros_like(gain_o)

    fill_pad(pad, low[0], g[0], high[0])
    chunk = frames // 5
    for c in range(D // LANES):
        lanes = slice(c * LANES, (c + 1) * LANES)
        for r in range(0, frames, chunk):
            acc = small[5:6, lanes] * pad[c, pl.ds(r + PAD - 7, chunk)]
            for j in range(1, KW):
                acc = acc + small[5 + j : 6 + j, lanes] * pad[c, pl.ds(r + j + PAD - 7, chunk)]
            q_s[pl.ds(r, chunk), lanes] = acc
    q = q_s[...]
    sig_q = sigmoid(q)
    act_q = q * sig_q
    a3 = act_q.astype(bf16)
    x3 = x2[0] + mm(a3, wq[...])
    hat3, inv3 = norm(x3)
    n3 = (hat3 * small[3:4]).astype(bf16)
    inner = mm(n3, wi[...])
    sig = sigmoid(inner)
    act = inner * sig
    b4 = act.astype(bf16)
    x4 = x3 + 0.5 * mm(b4, wo[...])
    hat4, inv4 = norm(x4)
    out_o[0] = (hat4 * small[4:5]).astype(bf16)
    c4 = cot[0].astype(f32)
    gain_o[1] += fold8(c4 * hat4)
    dx4 = norm_back(hat4, inv4, small[4:5], c4)
    dp = (0.5 * dx4).astype(bf16)
    dact = mm_nt(dp, wo[...])
    dinner = ((sig + act * (1.0 - sig)) * dact).astype(bf16)
    group = k_n.shape[0] // frames
    keep = pl.ds(pl.multiple_of(step % group * frames, frames), frames)
    k_act[keep] = b4
    k_din[keep] = dinner
    k_n[keep] = n3
    k_dp[keep] = dp
    k_a[keep] = a3
    dn3 = mm_nt(dinner, wi[...])
    gain_o[0] += fold8(dn3 * hat3)
    dx3 = dx4 + norm_back(hat3, inv3, small[3:4], dn3)
    dx3_o[0] = dx3
    dpq = dx3.astype(bf16)
    k_dpq[keep] = dpq
    da3 = mm_nt(dpq, wq[...])
    dq = ((sig_q + act_q * (1.0 - sig_q)) * da3).astype(bf16)
    dq_o[0] = dq
    put(dq)

    @pl.when(step % group == group - 1)
    def _():
        acc_out[...] += mm_tn(k_dp[...], k_act[...])
        acc_in[...] += mm_tn(k_n[...], k_din[...])
        acc_q[...] += mm_tn(k_a[...], k_dpq[...])

    @pl.when(step == pl.num_programs(0) - 1)
    def _():
        ffn, mix = D // BS * (FF // BS), (D // BS) ** 2
        plan = (
            (acc_in, 2 * ffn, False),
            (acc_out, 3 * ffn, True),
            (acc_q, 4 * ffn + 5 * mix, False),
        )
        store_blocks(plan, scale, grads, stage, sem)


def mixer_back_kernel(
    scale, dq, dlow, dhigh, g, glow, ghigh, pw, x2, gated, ys, dx3, small, stack, pfull_t, grads_in,
    dx2_o, dy_o, gst_o, grads, gain_o, dk_o,
    wo, wp, acc_p, acc_o, dpad, gpad, dg_s, dk_s, stage, k_n, k_dpw, k_ys, k_dg, sem,
):
    step = pl.program_id(0)
    frames = dq.shape[1]

    @pl.when(step == 0)
    def _():
        ffn, mix = D // BS * (FF // BS), (D // BS) ** 2
        load_matrices(stack, ((0, wo), (2 * mix, wp)), sem)
        acc_p[...] = jnp.zeros_like(acc_p)
        acc_o[...] = jnp.zeros_like(acc_o)
        gain_o[...] = jnp.zeros_like(gain_o)
        dk_s[...] = jnp.zeros_like(dk_s)

    fill_pad(dpad, dlow[0], dq[0], dhigh[0])
    fill_pad(gpad, glow[0], g[0], ghigh[0])
    chunk = frames // 5
    for c in range(D // LANES):
        lanes = slice(c * LANES, (c + 1) * LANES)
        for r in range(0, frames, chunk):
            here = dpad[c, pl.ds(r + PAD, chunk)]
            acc = small[5:6, lanes] * dpad[c, pl.ds(r + PAD + 7, chunk)]
            for j in range(1, KW):
                acc = acc + small[5 + j : 6 + j, lanes] * dpad[c, pl.ds(r - j + PAD + 7, chunk)]
            dg_s[pl.ds(r, chunk), lanes] = acc
            for j in range(KW):
                dk_s[j, :, lanes] += fold8(here * gpad[c, pl.ds(r + j + PAD - 7, chunk)])
    dg = dg_s[...]
    value = pw[0, :, :D].astype(f32)
    gate = sigmoid(pw[0, :, D:].astype(f32))
    dvalue = (dg * gate).astype(bf16)
    dgate = (dg * value * gate * (1.0 - gate)).astype(bf16)
    dpw = jnp.concatenate([dvalue, dgate], axis=1)
    hat2, inv2 = norm(x2[0])
    n2 = (hat2 * small[2:3]).astype(bf16)
    group = k_n.shape[0] // frames
    keep = pl.ds(pl.multiple_of(step % group * frames, frames), frames)
    k_n[keep] = n2
    k_dpw[keep] = dpw
    k_ys[keep] = ys[0]
    dn2 = mm_nt(dpw, wp[...])
    gain_o[...] += fold8(dn2 * hat2)
    dx2 = dx3[0] + norm_back(hat2, inv2, small[2:3], dn2)
    dx2_o[0] = dx2
    value = gated[0, :, :D].astype(f32)
    gate = sigmoid(gated[0, :, D:].astype(f32))
    dvalue = (dx2 * gate).astype(bf16)
    dgate = (dx2 * value * gate * (1.0 - gate)).astype(bf16)
    dgated = jnp.concatenate([dvalue, dgate], axis=1)
    k_dg[keep] = dgated
    dy = mm_nt(dgated, wo[...]).astype(bf16)
    dy_o[0] = dy
    local_states(pfull_t, dy, gst_o)

    @pl.when(step % group == group - 1)
    def _():
        acc_p[...] += mm_tn(k_n[...], k_dpw[...])
        acc_o[...] += mm_tn(k_ys[...], k_dg[...])

    @pl.when(step == pl.num_programs(0) - 1)
    def _():
        ffn, mix = D // BS * (FF // BS), (D // BS) ** 2
        plan = ((acc_o, 4 * ffn + mix, False), (acc_p, 4 * ffn + 3 * mix, False))
        store_blocks(plan, scale, grads, stage, sem)
        for j in range(KW):
            dk_o[j : j + 1] = jnp.sum(dk_s[j], axis=0, keepdims=True)


def conv_back_kernel(
    u, dy, back_ends, tab_a, tab_b, power, coup, taps,
    du_o, t1_o, t2_o, fp_o, gp_o, dk_o, back_all,
    upad, dpad, acc_s, own_sem, send, recv,
):
    step = pl.program_id(0)
    end_swap = swap_states(
        back_ends, back_all, step == 0, step == pl.num_programs(0) - 1, own_sem, send, recv
    )
    rows, frames = u.shape[0], u.shape[1]
    span = GROUP * SUB
    coup_both = pack_params(coup[...], rows)
    u_both = pack_heads(u, rows)
    d_both = pack_heads(dy, rows)
    width = u_both[0].shape[1]
    du, first_sum, second_sum, end_u, end_d = [], [], [], [], []
    for h in range(2):
        scale = [tile_lanes(power[h, i], width) for i in range(GROUP)]
        aged = [scale[i] * float(SUB * (i + 1)) for i in range(GROUP)]
        zero = jnp.zeros((NST, width), f32)
        carry, carry_w = zero, zero
        states, states_w = [], []
        for g in range(frames // span):
            here = u_both[h][g * span : (g + 1) * span]
            local = mm(tab_a[h, 0], here)
            local_w = mm(tab_a[h, 1], here)
            parts = [local[i * NST : (i + 1) * NST] for i in range(GROUP)]
            parts_w = [local_w[i * NST : (i + 1) * NST] for i in range(GROUP)]
            states.append([carry] + [parts[i] + scale[i] * carry for i in range(GROUP - 1)])
            states_w.append(
                [carry_w]
                + [parts_w[i] + scale[i] * carry_w + aged[i] * carry for i in range(GROUP - 1)]
            )
            carry_w = parts_w[-1] + scale[-1] * carry_w + aged[-1] * carry
            carry = parts[-1] + scale[-1] * carry
        end_u.append(carry_w)
        later, later_w = zero, zero
        one, two = zero, zero
        outs = []
        for g in reversed(range(frames // span)):
            here = d_both[h][g * span : (g + 1) * span]
            back = mm(tab_a[h, 2], here)
            back_w = mm(tab_a[h, 3], here)
            parts = [back[i * NST : (i + 1) * NST] for i in range(GROUP)]
            parts_w = [back_w[i * NST : (i + 1) * NST] for i in range(GROUP)]
            into = jnp.concatenate([v * coup_both[h] for v in parts[1:] + [later]], axis=0)
            outs.append(mm(tab_b[h, 0], into.astype(bf16)))
            for i in range(GROUP):
                one = one + parts[i] * states[g][i]
                two = two + (parts_w[i] * states[g][i] + parts[i] * states_w[g][i])
            new, new_w = parts[0], parts_w[0]
            for i in range(GROUP - 1):
                new = new + scale[i] * parts[i + 1]
                new_w = new_w + (scale[i] * parts_w[i + 1] + aged[i] * parts[i + 1])
            later_w = new_w + scale[-1] * later_w + aged[-1] * later
            later = new + scale[-1] * later
        end_d.append(later_w)
        first_sum.append(one)
        second_sum.append(two)
        du.append(jnp.concatenate(outs[::-1], axis=0))
    first = lax.broadcasted_iota(jnp.int32, (NST, LANES), 1) < HALF
    for sums, out in ((first_sum, t1_o), (second_sum, t2_o)):
        both = []
        for v in sums:
            total = v[:, :LANES]
            for p in range(1, rows // 2):
                total = total + v[:, p * LANES : (p + 1) * LANES]
            both.append(total + pltpu.roll(total, HALF, 1))
        out[...] = jnp.where(first, both[0], both[1])
    for p in range(rows // 2):
        for pair, out in ((du, du_o), (end_u, fp_o), (end_d, gp_o)):
            one, two = unpack_pair(pair[0], pair[1], p)
            out[2 * p] = one
            out[2 * p + 1] = two
    chunk = frames // 5
    upad[0:SUB] = jnp.zeros((SUB, LANES), f32)
    dpad[pl.ds(frames, SUB)] = jnp.zeros((SUB, LANES), f32)
    acc_s[...] = jnp.zeros_like(acc_s)

    def one_row(i, carry):
        upad[pl.ds(SUB, frames)] = u[i].astype(f32)
        dpad[pl.ds(0, frames)] = dy[i].astype(f32)
        for r in range(0, frames, chunk):
            acc = du_o[i, pl.ds(r, chunk)].reshape(-1, SUB, LANES)
            here = dpad[pl.ds(r, chunk)]
            for d in range(SUB):
                piece = dpad[pl.ds(r + d, chunk)].reshape(-1, SUB, LANES)
                acc = acc + piece * taps[d][None]
                product = (here * upad[pl.ds(SUB + r - d, chunk)]).reshape(-1, SUB, LANES)
                acc_s[d] += jnp.sum(product, axis=0)
            du_o[i, pl.ds(r, chunk)] = acc.reshape(chunk, LANES)
        return carry

    lax.fori_loop(0, rows, one_row, 0)
    spot = lax.broadcasted_iota(jnp.int32, (SUB, LANES), 0)
    for d in range(SUB):
        kept = jnp.where(spot >= d, acc_s[d], 0.0)
        dk_o[d : d + 1] = jnp.sum(kept, axis=0, keepdims=True)
    end_swap()


def ffa_back_kernel(
    scale, du_loc, back_all, ends_all, back_ends, ends_w, back_w, starts, weigh, coup,
    x1, feat, inner_r, act_r, dx2, small, stack, mfin_t, grads_in,
    dx0_o, grads, gain_o, sums_o,
    wi, wo, wu, acc_in, acc_out, acc_u, mask, stage, k_act, k_din, k_n, k_dp, k_m, k_du, sem,
):
    step = pl.program_id(0)

    @pl.when(step == 0)
    def _():
        ffn, mix = D // BS * (FF // BS), (D // BS) ** 2
        load_matrices(stack, ((0, wi), (ffn, wo), (2 * ffn, wu)), sem)
        mask[...] = head_mask()
        acc_in[...] = jnp.zeros_like(acc_in)
        acc_out[...] = jnp.zeros_like(acc_out)
        acc_u[...] = jnp.zeros_like(acc_u)
        gain_o[...] = jnp.zeros_like(gain_o)
        sums_o[...] = jnp.zeros_like(sums_o)

    frames = feat.shape[1]
    group = k_n.shape[0] // frames
    keep = pl.ds(pl.multiple_of(step % group * frames, frames), frames)
    parts = ends_all.shape[0]
    came, came_w, later = 0.0, 0.0, 0.0
    for i in range(parts):
        end = ends_all[i, 0].astype(f32)
        came = came + weigh[0, i] * end
        came_w = came_w + weigh[1, i] * end
        later = later + weigh[2, i] * back_all[i, 0].astype(f32)
    mine = back_ends[0].astype(f32)
    sums_o[0] += mine * came
    sums_o[1] += starts[0] * mine
    sums_o[2] += starts[0] * back_w[0]
    sums_o[3] += back_w[0] * came + mine * came_w + later * ends_w[0]
    du = (du_loc[0] + mm(mfin_t[...], spread_heads(coup[...] * later, mask[...]))).astype(bf16)
    hat1, inv1 = norm(x1[0])
    n1 = (hat1 * small[1:2]).astype(bf16)
    k_m[keep] = n1
    k_du[keep] = du
    dn1 = mm_nt(du, wu[...])
    gain_o[1] += fold8(dn1 * hat1)
    dx1 = dx2[0] + norm_back(hat1, inv1, small[1:2], dn1)
    dp = (0.5 * dx1).astype(bf16)
    dact = mm_nt(dp, wo[...])
    inner = inner_r[0].astype(f32)
    sig = sigmoid(inner)
    dinner = ((sig + inner * sig * (1.0 - sig)) * dact).astype(bf16)
    hat0, inv0 = norm(feat[0].astype(f32))
    n0 = (hat0 * small[0:1]).astype(bf16)
    k_act[keep] = act_r[0]
    k_din[keep] = dinner
    k_n[keep] = n0
    k_dp[keep] = dp
    dn0 = mm_nt(dinner, wi[...])
    gain_o[0] += fold8(dn0 * hat0)
    dx0_o[0] = dx1 + norm_back(hat0, inv0, small[0:1], dn0)

    @pl.when(step % group == group - 1)
    def _():
        acc_out[...] += mm_tn(k_dp[...], k_act[...])
        acc_in[...] += mm_tn(k_n[...], k_din[...])
        acc_u[...] += mm_tn(k_m[...], k_du[...])

    @pl.when(step == pl.num_programs(0) - 1)
    def _():
        ffn, mix = D // BS * (FF // BS), (D // BS) ** 2
        plan = ((acc_in, 0, False), (acc_out, ffn, True), (acc_u, 4 * ffn, False))
        store_blocks(plan, scale, grads, stage, sem)


def shampoo_kernel(
    pick, owned, full, left, right, lroot, rroot, master, nl_o, nr_o, nm_o, nc_o, own_o
):
    for i in range(full.shape[0]):
        whole = full[i]
        mine = owned[i]
        own_o[i] = mine.astype(f32)
        nl_o[i] = 0.5 * left[i] + 0.5 * mm_nt(mine, whole)
        columns = mm_nt(pick[...], whole).astype(bf16)
        nr_o[i] = 0.5 * right[i] + 0.5 * mm(columns, whole)
        side = mm(lroot[i].astype(bf16), whole)
        step = mm(side.astype(bf16), rroot[i].astype(bf16))
        new = master[i] - rate_blocks * step
        nm_o[i] = new
        nc_o[i] = new.astype(bf16)


def reduce_kernel(
    sizes, grads, small, full, owned, small_sum,
    mine, came, from_x, from_y, red, near_in, far_in, s_tm, s_core, s_z,
    load_sem, c_send, c_recv, x_send, x_recv, y_send, y_recv,
    z_send, z_recv, f_send, f_recv, s_send, s_recv, put_sem,
):
    place, level, core = peers()
    low, high = level % 2, level // 2
    near, far = level + 1 - 2 * low, level + 2 - 4 * high
    xp, yp, dp = others = square(place)
    greet([at(other, level, core) for other in others])
    greet([at(place, level, 1 - core), at(place, near, core), at(place, far, core)])
    diagonal = 2 * (1 - high) + 1 - low
    greet([at(place, diagonal, core)])
    edges = [sum(sizes[:c]) for c in range(len(sizes) + 1)]
    ranges = [(a, b, (a + b + 1) // 2) for a, b in zip(edges[:-1], edges[1:])]
    sends = []

    def go(copy):
        copy.start()
        sends.append(copy)
        return copy

    loads, core_in = [], []
    for c, (first, end, unused) in enumerate(ranges):
        n = pl.ds(first, end - first)
        load = pltpu.make_async_copy(grads.at[:, n, :, core], mine.at[:, n], load_sem.at[c])
        load.start()
        loads.append(load)
    met(7)
    for c, (first, end, unused) in enumerate(ranges):
        n = pl.ds(first, end - first)
        core_in.append(
            go(
                remote(
                    grads.at[:, n, :, 1 - core], came.at[:, n], c_send.at[c], c_recv.at[c],
                    at(place, level, 1 - core),
                )
            )
        )

    small_in = [
        go(remote(small.at[other], s_tm.at[d], s_send.at[d], s_recv.at[d], at(other, level, core)))
        for d, other in enumerate(others)
    ]

    def add(owner, first, end):
        def one(k, carry):
            mine[owner, k] = mine[owner, k] + came[owner, k]
            return carry

        lax.fori_loop(first, end, one, 0)

    def add_into(owner, ref, first, end):
        def one(k, carry):
            mine[owner, k] = mine[owner, k] + ref[0, k]
            return carry

        lax.fori_loop(first, end, one, 0)

    def to_x(c, i, owner, slot, first, end):
        n = pl.ds(first, end - first)
        send, recv = x_send.at[c, i], x_recv.at[c, i]
        return go(
            remote(mine.at[owner, n], from_x.at[slot, n], send, recv, at(xp, level, core))
        )

    def to_y(c, i, owner, slot, first, end):
        n = pl.ds(first, end - first)
        send, recv = y_send.at[c, i], y_recv.at[c, i]
        return go(
            remote(mine.at[owner, n], from_y.at[slot, n], send, recv, at(yp, level, core))
        )

    def begin(c):
        first, end, middle = ranges[c]
        loads[c].wait()
        core_in[c].wait_recv()
        add(dp, first, end)
        x_one = to_x(c, 0, dp, 0, first, middle)
        y_one = to_y(c, 0, dp, 0, middle, end)
        add(xp, first, end)
        x_two = to_x(c, 1, xp, 1, first, middle)
        add(yp, first, end)
        y_two = to_y(c, 1, yp, 1, middle, end)
        add(place, first, end)
        return x_one, y_one, x_two, y_two

    def second(c, copies):
        first, end, middle = ranges[c]
        copies[0].wait_recv()
        add_into(yp, from_x, first, middle)
        y_three = to_y(c, 2, yp, 1, first, middle)
        copies[1].wait_recv()
        add_into(xp, from_y, middle, end)
        x_three = to_x(c, 2, xp, 1, middle, end)
        return copies[2], copies[3], x_three, y_three

    def along(c, copies):
        first, end, unused = ranges[c]
        for copy in copies:
            copy.wait_recv()

        def one(k, carry):
            total = mine[place, k].astype(f32) + from_x[1, k].astype(f32)
            total = (total + from_y[1, k].astype(f32)).astype(bf16)
            red[k] = total.reshape(red.shape[1:])
            return carry

        lax.fori_loop(first, end, one, 0)
        n = pl.ds(first, end - first)
        return go(
            remote(
                red.at[n, :, 1 - low], near_in.at[n], z_send.at[c, 0], z_recv.at[c, 0],
                at(place, near, core),
            )
        )

    def across(c, copy):
        first, end, unused = ranges[c]
        copy.wait_recv()

        def one(k, carry):
            near_in[k] = red[k, :, low] + near_in[k]
            return carry

        lax.fori_loop(first, end, one, 0)
        n = pl.ds(first, end - first)
        return go(
            remote(
                near_in.at[n, 1 - high], far_in.at[n], z_send.at[c, 1], z_recv.at[c, 1],
                at(place, far, core),
            )
        )

    def to_core(c, i, source):
        first, end, unused = ranges[c]
        spot = full.at[pl.ds(first, end - first), source // 2, source % 2, core]
        src = owned.at[pl.ds(first, end - first)] if i == 0 else spot
        return go(
            remote(src, spot, f_send.at[c, i], f_recv.at[c, i], at(place, level, 1 - core))
        )

    def settle(c, copy):
        first, end, unused = ranges[c]
        copy.wait_recv()

        def one(k, carry):
            owned[k] = near_in[k, high] + far_in[k]
            return carry

        lax.fori_loop(first, end, one, 0)
        n = pl.ds(first, end - first)
        spot = full.at[n, high, low, core]
        put = pltpu.make_async_copy(owned.at[n], spot, put_sem.at[c])
        put.start()
        to_far = go(
            remote(owned.at[n], spot, z_send.at[c, 2], z_recv.at[c, 2], at(place, far, core))
        )
        to_near = go(
            remote(owned.at[n], spot, z_send.at[c, 3], z_recv.at[c, 3], at(place, near, core))
        )
        return put, to_far, to_near, to_core(c, 0, level)

    def pass_on(c, state):
        first, end, unused = ranges[c]
        put, to_far, to_near, own = state
        to_far.wait_recv()
        spot = full.at[pl.ds(first, end - first), 1 - high, low, core]
        more = go(
            remote(spot, spot, z_send.at[c, 4], z_recv.at[c, 4], at(place, near, core))
        )
        passed = [own, to_core(c, 1, far)]
        to_near.wait_recv()
        passed.append(to_core(c, 2, near))
        return put, more, passed

    def last(c, state):
        put, more, passed = state
        more.wait_recv()
        passed.append(to_core(c, 3, diagonal))
        return put, passed

    stages = (
        lambda c, state: begin(c), second, along, across, settle, pass_on, last
    )
    chunks = len(ranges)
    state = [None] * chunks
    for tick in range(chunks + len(stages) - 1):
        for index, stage in enumerate(stages):
            c = tick - index
            if 0 <= c < chunks:
                state[c] = stage(c, state[c])
        if tick == 0:
            for copy in small_in:
                copy.wait_recv()
            s_core[0] = small[place] + (s_tm[0] + s_tm[1]) + s_tm[2]
            swap = go(
                remote(
                    s_core.at[0], s_core.at[1], s_send.at[3], s_recv.at[3],
                    at(place, level, 1 - core),
                )
            )
        if tick == 1:
            swap.wait_recv()
            s_z[level] = s_core[0] + s_core[1]
            spot = s_z.at[level]
            small_z = [
                go(
                    remote(spot, spot, s_send.at[4 + d], s_recv.at[4 + d], at(place, target, core))
                )
                for d, target in enumerate((near, far, diagonal))
            ]
    for copy in small_z:
        copy.wait_recv()
    small_sum[...] = (s_z[0] + s_z[1]) + (s_z[2] + s_z[3])
    for put, passed in state:
        put.wait()
        for copy in passed:
            copy.wait_recv()
    for copy in sends:
        copy.wait_send()


def reduce_grads(grads, small, parts, devices, slab):
    levels = devices // 2
    if parts != 4 or levels != 4:
        owned = lax.psum_scatter(grads, "tm", scatter_dimension=0, tiled=True)
        owned = lax.psum_scatter(owned, "rows", scatter_dimension=1, tiled=True)
        full = lax.all_gather(owned, "rows", axis=1, tiled=True)
        small = lax.psum_scatter(small, "tm", scatter_dimension=0, tiled=True)[0]
        return full, owned, lax.psum(small, "rows")
    count = grads.shape[0] // parts
    sizes = (6, 6, 5, 3, 2)
    grads = grads.reshape(parts, count, levels, 2, slab, BS)
    dma = lambda *dims: pltpu.SemaphoreType.DMA(dims)
    vb = lambda *dims: pltpu.VMEM(dims, bf16)
    vmem = pl.BlockSpec(memory_space=pltpu.VMEM)
    part = small.shape[1:]
    chunks = len(sizes)
    full, owned, small_sum = pl.pallas_call(
        partial(reduce_kernel, sizes),
        in_specs=[ANY, vmem],
        out_specs=[ANY, vmem, vmem],
        out_shape=[
            shape((count, 2, 2, 2, slab, BS), bf16),
            shape((count, slab, BS), bf16),
            shape(part),
        ],
        scratch_shapes=[
            vb(parts, count, levels, slab, BS), vb(parts, count, levels, slab, BS),
            vb(2, count, levels, slab, BS), vb(2, count, levels, slab, BS),
            vb(count, 2, 2, slab, BS), vb(count, 2, slab, BS), vb(count, slab, BS),
            vm(3, *part), vm(2, *part), vm(levels, *part),
            dma(chunks), dma(chunks), dma(chunks),
            dma(chunks, 3), dma(chunks, 3), dma(chunks, 3), dma(chunks, 3),
            dma(chunks, 5), dma(chunks, 5), dma(chunks, 4), dma(chunks, 4),
            dma(7), dma(7), dma(chunks),
        ],
        compiler_params=pltpu.CompilerParams(
            collective_id=2, has_side_effects=True, vmem_limit_bytes=VMEM_BYTES
        ),
        name="reduce_grads",
    )(grads, small)
    return full.reshape(count, BS, BS), owned, small_sum


def row_spec(frames, width, per=1):
    return pl.BlockSpec((per, frames, width), lambda i: (i, 0, 0))


def whole_spec(*dims):
    return pl.BlockSpec(dims, lambda i: (0,) * len(dims))


def talking(number):
    return pltpu.CompilerParams(
        dimension_semantics=("arbitrary",),
        vmem_limit_bytes=VMEM_BYTES,
        collective_id=number,
        has_side_effects=True,
    )


def body(
    features,
    cotangent,
    state_bank,
    state_source,
    master,
    left_stats,
    right_stats,
    left_root,
    right_root,
    small_params,
    decay_logs,
    state_mix,
):
    rows, frames, width = features.shape
    tokens = rows * frames
    parts = lax.axis_size("tm")
    place = lax.axis_index("tm")
    scaling = 1.0 / math.sqrt(tokens * parts * lax.axis_size("rows"))
    ffn, mix = D // BS * (FF // BS), (D // BS) ** 2

    own_heads, own_channels = decay_logs.shape[0], state_mix.shape[1]
    starts_own = state_bank[state_source]
    params = jnp.concatenate(
        [decay_logs.reshape(-1), state_mix.reshape(-1), starts_own.reshape(-1)]
    )
    cut_one = own_heads * NST
    cut_two = cut_one + 2 * own_channels * NST
    cut_three = cut_two + rows * own_channels * NST
    params = jnp.pad(params, (0, -cut_three % (8 * LANES))).reshape(-1, LANES)
    devices = lax.axis_size("rows")
    levels = devices // 2
    spread_out = parts == 4
    if spread_out:
        first, pair, rest, packed = gather_first(master, params, parts, devices)
        first = first.reshape(-1, BS, BS)
        pair_out, rest_out = [shape(pair.shape, bf16)], [shape(rest.shape, bf16)]
        any_one, pair_in, rest_in = [ANY], [pair], [rest]
        pair_sems, rest_sems = gather_sems(XY_SEMS, levels), gather_sems(XY_SEMS, levels, 2)
    else:
        stack = lax.all_gather(master.astype(bf16), "rows", axis=1, tiled=True)
        stack = lax.all_gather(stack, "tm", axis=0, tiled=True)
        packed = lax.all_gather(params, "tm", axis=0)
        first, pair, rest = (stack[jnp.array(ids)] for ids in block_sets())
        pair_out = rest_out = any_one = pair_in = rest_in = pair_sems = rest_sems = []

    packed = packed.reshape(parts, -1)
    logs = packed[:, :cut_one].reshape(HEADS, NST)
    mix_all = packed[:, cut_one:cut_two].reshape(parts, 2, own_channels, NST)
    mix_all = mix_all.transpose(1, 3, 0, 2).reshape(2, NST, D)
    starts = packed[:, cut_two:cut_three].reshape(parts, rows, own_channels, NST)
    starts = starts.transpose(1, 3, 0, 2).reshape(rows, NST, D)

    rates = jnp.exp(logs)
    rate_nc = jnp.repeat(rates.T, HALF, axis=1)
    coupling = mix_all[0] * mix_all[1]
    state_row = jnp.arange(GROUP * NST, dtype=jnp.int32)
    part_of = state_row // NST
    rate_row = jnp.tile(rates, (1, GROUP))[:, :, None]
    inner_t = jnp.arange(GROUP * SUB, dtype=jnp.int32)
    age = SUB * (part_of + 1)[:, None] - 1 - inner_t[None, :]
    age_f = jnp.maximum(age, 0).astype(f32)
    tab_in = jnp.where(age >= 0, jnp.exp(-rate_row * age_f), 0.0)
    since = (inner_t % SUB + 1).astype(f32)
    inside = (inner_t // SUB)[None, :] == part_of[:, None]
    tab_out = jnp.where(inside, jnp.exp(-rate_row * since), 0.0)
    tab_a = jnp.stack([tab_in, tab_in * age_f, tab_out, tab_out * since], axis=1).astype(bf16)
    tab_b = jnp.stack([tab_in, tab_out], axis=1).astype(bf16).transpose(0, 1, 3, 2)
    steps_of = SUB * jnp.arange(1, GROUP + 1, dtype=f32)
    power = jnp.exp(-rates[:, None, :, None] * steps_of[None, :, None, None])
    power = jnp.broadcast_to(power, (HEADS, GROUP, NST, LANES))
    time = jnp.arange(frames, dtype=jnp.int32)
    flat_rates = rates.reshape(-1)
    next_t = (time + 1).astype(f32)
    left_t = (frames - 1 - time).astype(f32)
    pfull = jnp.exp(-flat_rates[None, :] * next_t[:, None]).astype(bf16)
    pfull_t = jnp.exp(-flat_rates[:, None] * next_t[None, :]).astype(bf16)
    mfin = jnp.exp(-flat_rates[:, None] * left_t[None, :]).astype(bf16)
    mfin_t = jnp.exp(-flat_rates[None, :] * left_t[:, None]).astype(bf16)
    lag = jnp.arange(SUB, dtype=f32)
    lag_decay = jnp.exp(-rate_nc[None] * lag[:, None, None])
    kernel_lags = jnp.sum(coupling[None] * lag_decay, axis=1)
    slot = jnp.arange(SUB, dtype=jnp.int32)
    taps_f = jnp.where(slot[:, None, None] <= slot[None, :, None], kernel_lags[:, None, :], 0.0)
    taps_b = jnp.where(
        slot[:, None, None] + slot[None, :, None] < SUB, kernel_lags[:, None, :], 0.0
    )

    span = float(frames)
    shard = jnp.arange(parts, dtype=jnp.int32)

    def passing(apart):
        length = jnp.maximum(apart, 0).astype(f32)[:, None, None] * span
        weight = jnp.where(
            (apart >= 0)[:, None, None], jnp.exp(-rate_nc[None] * length), 0.0
        )
        return weight, weight * length

    behind_w, behind_l = passing(place - 1 - shard)
    ahead_w, unused = passing(shard - place - 1)
    begin = place.astype(f32) * span
    begin_w = jnp.exp(-rate_nc * begin)
    weigh_in = jnp.concatenate([behind_w, (mix_all[1] * begin_w)[None]], axis=0)
    weigh_back = jnp.stack([behind_w, behind_l, ahead_w], axis=0)

    mat = lambda r, c: vm(r, c, dtype=bf16)
    dma = pltpu.SemaphoreType.DMA
    group = 3 if rows % 3 == 0 else 1
    small_spec = whole_spec(*small_params.shape)
    state_spec = pl.BlockSpec((1, NST, D), lambda i: (i, 0, 0))
    states_spec = pl.BlockSpec((parts, 1, NST, D), lambda i: (0, i, 0, 0))
    flat_spec = whole_spec(NST, D)
    x1, inner_a, act_a, u, ends, *done = pl.pallas_call(
        ffa_forward_kernel,
        grid=(rows // BOTH,),
        in_specs=[row_spec(frames, D, BOTH), small_spec, ANY, whole_spec(HEADS * NST, frames)]
        + any_one,
        out_specs=[
            row_spec(frames, D, BOTH),
            row_spec(frames, FF, BOTH),
            row_spec(frames, FF, BOTH),
            row_spec(frames, D, BOTH),
            pl.BlockSpec((BOTH, NST, D), lambda i: (i, 0, 0)),
        ]
        + any_one,
        out_shape=[
            shape((rows, frames, D)),
            shape((rows, frames, FF), bf16),
            shape((rows, frames, FF), bf16),
            shape((rows, frames, D), bf16),
            shape((rows, NST, D), bf16),
        ]
        + pair_out,
        scratch_shapes=[mat(D, FF), mat(FF, D), mat(D, D), dma] + pair_sems,
        input_output_aliases={4: 5} if spread_out else {},
        compiler_params=talking(7) if spread_out else PARAMS,
        name="ffa_forward",
    )(features, small_params, first, mfin, *pair_in)
    if spread_out:
        pair = done[0].reshape(-1, BS, BS)

    group_spec = pl.BlockSpec((rows, frames, LANES), lambda i: (0, 0, i))
    tab_a_spec = pl.BlockSpec((2,) + tab_a.shape[1:], lambda i: (i, 0, 0, 0))
    tab_b_spec = pl.BlockSpec((2,) + tab_b.shape[1:], lambda i: (i, 0, 0, 0))
    power_spec = pl.BlockSpec((2,) + power.shape[1:], lambda i: (i, 0, 0, 0))
    coup_spec = pl.BlockSpec((NST, LANES), lambda i: (0, i))
    taps_spec = pl.BlockSpec((SUB, SUB, LANES), lambda i: (0, 0, i))
    swap_scratch = [dma, dma((parts - 1,)), dma((parts - 1,))]
    all_states = shape((parts, rows, NST, D), bf16)
    y_loc, ends_all, *done = pl.pallas_call(
        conv_forward_kernel,
        grid=(D // LANES,),
        in_specs=[group_spec, ANY, tab_a_spec, tab_b_spec, power_spec, coup_spec, taps_spec]
        + any_one,
        out_specs=[group_spec, ANY] + any_one,
        out_shape=[shape((rows, frames, D)), all_states] + rest_out,
        scratch_shapes=[vm(SUB + frames, LANES)] + swap_scratch + rest_sems,
        input_output_aliases={7: 2} if spread_out else {},
        compiler_params=talking(3),
        name="conv_forward",
    )(u, ends, tab_a, tab_b, power, coupling, taps_f, *rest_in)

    edge_spec = pl.BlockSpec((1, PAD, D), lambda i: (i, 0, 0))
    edge_scratch = [
        vm(rows, 2, PAD, D, dtype=bf16),
        vm(PAD, D, dtype=bf16),
        dma((2, rows)),
        dma((2, rows)),
        dma((2,)),
    ]
    edge_shapes = [shape((rows, PAD, D), bf16)] * 2
    ys, gated, x2, pw, g, g_low, g_high, *done = pl.pallas_call(
        mixer_out_kernel,
        grid=(rows,),
        in_specs=[
            row_spec(frames, D),
            states_spec,
            state_spec,
            whole_spec(parts + 1, NST, D),
            flat_spec,
            row_spec(frames, D),
            small_spec,
            ANY,
            whole_spec(frames, HEADS * NST),
        ]
        + any_one,
        out_specs=[
            row_spec(frames, D),
            row_spec(frames, 2 * D),
            row_spec(frames, D),
            row_spec(frames, 2 * D),
            row_spec(frames, D),
            ANY,
            ANY,
        ]
        + any_one,
        out_shape=[
            shape((rows, frames, D), bf16),
            shape((rows, frames, 2 * D), bf16),
            shape((rows, frames, D)),
            shape((rows, frames, 2 * D), bf16),
            shape((rows, frames, D), bf16),
        ]
        + edge_shapes
        + rest_out,
        scratch_shapes=[mat(D, 2 * D), mat(D, 2 * D), vm(HEADS * NST, D), dma]
        + edge_scratch
        + rest_sems,
        input_output_aliases={9: 7} if spread_out else {},
        compiler_params=talking(4),
        name="mixer_out",
    )(y_loc, ends_all, starts, weigh_in, coupling, x1, small_params, pair, pfull, *done)
    if spread_out:
        rest = done[0].reshape(-1, BS, BS)

    kept = lambda *widths: [mat(group * frames, w) for w in widths]
    grad_shape = shape((parts * master.shape[0], BS, BS), bf16)
    layer_out, dx3, dq, grads, gain_b, d_low, d_high = pl.pallas_call(
        partial(ffb_kernel, scaling),
        grid=(rows,),
        in_specs=[
            row_spec(frames, D),
            edge_spec,
            edge_spec,
            row_spec(frames, D),
            row_spec(frames, D),
            small_spec,
            ANY,
        ],
        out_specs=[
            row_spec(frames, D),
            row_spec(frames, D),
            row_spec(frames, D),
            ANY,
            whole_spec(2, 8, D),
            ANY,
            ANY,
        ],
        out_shape=[
            shape((rows, frames, D), bf16),
            shape((rows, frames, D)),
            shape((rows, frames, D), bf16),
            grad_shape,
            shape((2, 8, D)),
        ]
        + edge_shapes,
        scratch_shapes=[
            mat(D, FF),
            mat(FF, D),
            mat(D, D),
            vm(D, FF),
            vm(D, FF),
            vm(D, D),
            vm(D // LANES, frames + 2 * PAD, LANES),
            vm(frames, D),
            vm(2 * ffn + mix, BS, BS, dtype=bf16),
        ]
        + kept(FF, FF, D, D, D, D)
        + [dma]
        + edge_scratch,
        compiler_params=talking(5),
        name="ffb",
    )(g, g_low, g_high, x2, cotangent, small_params, rest)

    dx2, dy, back_ends, grads, gain_c, kernel_grads = pl.pallas_call(
        partial(mixer_back_kernel, scaling),
        grid=(rows,),
        in_specs=[
            row_spec(frames, D),
            edge_spec,
            edge_spec,
            row_spec(frames, D),
            edge_spec,
            edge_spec,
            row_spec(frames, 2 * D),
            row_spec(frames, D),
            row_spec(frames, 2 * D),
            row_spec(frames, D),
            row_spec(frames, D),
            small_spec,
            ANY,
            whole_spec(HEADS * NST, frames),
            ANY,
        ],
        out_specs=[
            row_spec(frames, D),
            row_spec(frames, D),
            state_spec,
            ANY,
            whole_spec(8, D),
            whole_spec(16, D),
        ],
        out_shape=[
            shape((rows, frames, D)),
            shape((rows, frames, D), bf16),
            shape((rows, NST, D), bf16),
            grad_shape,
            shape((8, D)),
            shape((16, D)),
        ],
        scratch_shapes=[
            mat(D, 2 * D),
            mat(D, 2 * D),
            vm(D, 2 * D),
            vm(D, 2 * D),
            vm(D // LANES, frames + 2 * PAD, LANES),
            vm(D // LANES, frames + 2 * PAD, LANES),
            vm(frames, D),
            vm(KW, 8, D),
            vm(4 * mix, BS, BS, dtype=bf16),
        ]
        + kept(D, 2 * D, D, 2 * D)
        + [dma],
        input_output_aliases={14: 3},
        compiler_params=PARAMS,
        name="mixer_back",
    )(
        dq, d_low, d_high, g, g_low, g_high, pw, x2, gated, ys, dx3, small_params, pair,
        pfull_t, grads,
    )

    nst_spec = pl.BlockSpec((rows, NST, LANES), lambda i: (0, 0, i))
    du_loc, t_one, t_two, ends_w, back_w, lag_grads, back_all = pl.pallas_call(
        conv_back_kernel,
        grid=(D // LANES,),
        in_specs=[
            group_spec, group_spec, ANY, tab_a_spec, tab_b_spec, power_spec, coup_spec, taps_spec
        ],
        out_specs=[
            group_spec,
            coup_spec,
            coup_spec,
            nst_spec,
            nst_spec,
            pl.BlockSpec((SUB, LANES), lambda i: (0, i)),
            ANY,
        ],
        out_shape=[
            shape((rows, frames, D)),
            shape((NST, D)),
            shape((NST, D)),
            shape((rows, NST, D)),
            shape((rows, NST, D)),
            shape((SUB, D)),
            all_states,
        ],
        scratch_shapes=[
            vm(SUB + frames, LANES),
            vm(SUB + frames, LANES),
            vm(SUB, SUB, LANES),
        ]
        + swap_scratch,
        compiler_params=talking(6),
        name="conv_back",
    )(u, dy, back_ends, tab_a, tab_b, power, coupling, taps_b)

    grad_zero, grads, gain_a, sums_c = pl.pallas_call(
        partial(ffa_back_kernel, scaling),
        grid=(rows,),
        in_specs=[
            row_spec(frames, D),
            states_spec,
            states_spec,
            state_spec,
            state_spec,
            state_spec,
            state_spec,
            whole_spec(3, parts, NST, D),
            flat_spec,
            row_spec(frames, D),
            row_spec(frames, D),
            row_spec(frames, FF),
            row_spec(frames, FF),
            row_spec(frames, D),
            small_spec,
            ANY,
            whole_spec(frames, HEADS * NST),
            ANY,
        ],
        out_specs=[row_spec(frames, D), ANY, whole_spec(2, 8, D), whole_spec(4, NST, D)],
        out_shape=[
            shape((rows, frames, D)),
            grad_shape,
            shape((2, 8, D)),
            shape((4, NST, D)),
        ],
        scratch_shapes=[
            mat(D, FF),
            mat(FF, D),
            mat(D, D),
            vm(D, FF),
            vm(D, FF),
            vm(D, D),
            vm(HEADS * NST, D),
            vm(2 * ffn + mix, BS, BS, dtype=bf16),
        ]
        + kept(FF, FF, D, D, D, D)
        + [dma],
        input_output_aliases={17: 1},
        compiler_params=PARAMS,
        name="ffa_back",
    )(
        du_loc, back_all, ends_all, back_ends, ends_w, back_w, starts, weigh_back, coupling,
        x1, features, inner_a, act_a, dx2, small_params, first, mfin_t, grads,
    )

    lag_grad_c = jnp.sum(lag_decay * lag_grads[:, None, :], axis=0)
    lag_grad_r = jnp.sum(lag_decay * (lag[:, None] * lag_grads)[:, None, :], axis=0)
    d_coup = t_one + lag_grad_c + sums_c[0]
    start_back = sums_c[1] * begin_w
    d_first = d_coup * mix_all[1]
    d_second = d_coup * mix_all[0] + start_back
    d_rate = coupling * (t_two + lag_grad_r + sums_c[3])
    d_rate = d_rate + mix_all[1] * (begin * start_back + begin_w * sums_c[2])
    small_grads = [
        jnp.sum(gain_a, axis=1),
        jnp.sum(gain_c, axis=0, keepdims=True),
        jnp.sum(gain_b, axis=1),
        kernel_grads[:KW],
    ]
    stacked = jnp.concatenate(small_grads + [d_first, d_second, d_rate], axis=0) * scaling
    stacked = jnp.pad(stacked, ((0, -stacked.shape[0] % 8), (0, 0)))
    own = place * own_channels
    lanes_own = lambda v: lax.dynamic_slice_in_dim(v, own, own_channels, v.ndim - 1)
    stacked = stacked.reshape(-1, parts, own_channels).transpose(1, 0, 2)
    full_grad, owned, sums = reduce_grads(
        grads, stacked, parts, lax.axis_size("rows"), master.shape[1]
    )
    count_small = small_params.shape[0]
    small_sum = sums[:count_small]
    mix_sum = sums[count_small : count_small + 2 * NST]
    mix_sum = mix_sum.reshape(2, NST, own_channels).transpose(0, 2, 1)
    rate_sum = sums[count_small + 2 * NST : count_small + 3 * NST]
    rate_sum = jnp.sum(rate_sum.reshape(NST, own_heads, HALF), axis=2)
    decay_sum = -rate_sum.T * jnp.exp(decay_logs)
    new_small = lanes_own(small_params) - rate_small * small_sum
    new_decay = decay_logs - rate_small * decay_sum
    new_mix = state_mix - rate_small * mix_sum

    shard_w = jnp.exp(-lanes_own(rate_nc)[None] * (shard.astype(f32) * span)[:, None, None])
    start_grad = jnp.sum(lanes_own(back_all).astype(f32) * shard_w[:, None], axis=0) * lanes_own(mix_all[1])
    start_grad = start_grad.transpose(0, 2, 1)
    chosen = (state_source[None, :] == jnp.arange(rows, dtype=jnp.int32)[:, None]).astype(f32)
    grad_state = jnp.sum(chosen[:, :, None, None] * start_grad[None], axis=1)

    count, slice_rows = owned.shape[0], owned.shape[1]
    mine = lax.axis_index("rows") * slice_rows
    pick = (
        jnp.arange(slice_rows, dtype=jnp.int32)[:, None] + mine
        == jnp.arange(BS, dtype=jnp.int32)[None, :]
    ).astype(bf16)
    group = 11 if count % 11 == 0 else 1
    part_spec = pl.BlockSpec((group, slice_rows, BS), lambda i: (i, 0, 0))
    full_spec = pl.BlockSpec((group, BS, BS), lambda i: (i, 0, 0))
    new_left, new_right, new_master, new_copy, grad_blocks = pl.pallas_call(
        shampoo_kernel,
        grid=(count // group,),
        in_specs=[
            whole_spec(slice_rows, BS),
            part_spec,
            full_spec,
            part_spec,
            part_spec,
            part_spec,
            full_spec,
            part_spec,
        ],
        out_specs=[part_spec] * 5,
        out_shape=[
            shape(owned.shape),
            shape(owned.shape),
            shape(owned.shape),
            shape(owned.shape, bf16),
            shape(owned.shape),
        ],
        compiler_params=PARAMS,
        name="shampoo",
    )(pick, owned, full_grad, left_stats, right_stats, left_root, right_root, master)
    return (
        layer_out,
        grad_zero,
        grad_state,
        grad_blocks,
        new_left,
        new_right,
        new_master,
        new_copy,
        small_sum,
        new_small,
        decay_sum,
        mix_sum,
        new_decay,
        new_mix,
    )


def solution(mesh):
    return jax.shard_map(
        body,
        mesh=mesh,
        in_specs=(
            P("rows", "tm", None),
            P("rows", "tm", None),
            P("rows", "tm", None),
            P("rows"),
            P("tm", "rows", None),
            P("tm", "rows", None),
            P("tm", "rows", None),
            P("tm", "rows", None),
            P("tm", None, None),
            P(),
            P("tm", None),
            P(None, "tm", None),
        ),
        out_specs=(
            P("rows", "tm", None),
            P("rows", "tm", None),
            P("rows", "tm", None),
            P("tm", "rows", None),
            P("tm", "rows", None),
            P("tm", "rows", None),
            P("tm", "rows", None),
            P("tm", "rows", None),
            P(None, "tm"),
            P(None, "tm"),
            P("tm", None),
            P(None, "tm", None),
            P("tm", None),
            P(None, "tm", None),
        ),
        check_vma=False,
    )
```

profile of v0, /device:TPU:0, one launch (start us, length us, event | category | flops | bytes accessed | tf_op | source)
XLA Modules:
  0.0 399.2 jit_solution(10292815331133843594)
XLA Ops:
  0.7 0.7 compare_select_fusion
  2.4 0.9 copy.63
  4.3 41.7 %gather_first.1 = (bf16[4,9,4,2,32,256]{5,4,3,2,1,0:T(8,128)(2,1)}, bf16[4,4,4,2,32,256]{5,4,3,2,1,0:T(8,128)(2,1)}, bf16[4,9,4,2,32,256]{5,4,3,2,1,0:T(8,128)(2,1)}, f32[4,264,128]{2,1,0:T(8,128)}) custom-call(f32[22,32,256]{2,1,0:T(8,128)} %master.3, f32[264,128]{1,0:T(8,128)} %pad_bitcast_fusion.1.pack), custom_call_target="tpu_custom_call" | custom-call | tf_op jit(solution)/shard_map/gather_first/pallas_call | solution.py:416
  46.0 1.2 copy.93
  48.1 2.1 copy.68.tab_a
  50.2 0.9 maximum_bitcast_fusion.tab_b
  52.3 1.1 broadcast_select_fusion
  53.5 0.9 exponential_convert_fusion
  54.4 22.5 %ffa_forward.1 = (f32[6,320,512]{2,1,0:T(8,128)}, bf16[6,320,2048]{2,1,0:T(8,128)(2,1)}, bf16[6,320,2048]{2,1,0:T(8,128)(2,1)}, bf16[6,320,512]{2,1,0:T(8,128)(2...) custom-call(bf16[6,320,512]{2,1,0:T(8,128)(2,1)} %feat.3, ...), custom_call_target="tpu_custom_call", output_to_operand_aliasing={{5}: (4, {})} | custom-call | tf_op jit(solution)/shard_map/ffa_forward/pallas_call | solution.py:1498
  77.0 1.1 broadcast_in_dim.123.power
  78.1 27.5 %conv_forward.1 = (f32[6,320,512]{2,1,0:T(8,128)}, bf16[4,6,32,512]{3,2,1,0:T(8,128)(2,1)}, bf16[4,9,4,2,32,256]{5,4,3,2,1,0:T(8,128)(2,1)}) custom-call(bf16[6,320,512]{2,1,0:T(8,128)(2,1)} %get-tuple-element.70.u, bf16[6,32,512]{2,1,0:T(8,128)(2,1)} %get-tuple-element.71.ends, ...), custom_call_target="tpu_custom_call", output_to_operand_aliasing={{2}: (7, {})} | custom-call | tf_op jit(solution)/shard_map/conv_forward/pallas_call | solution.py:1535
  106.1 0.7 pad_maximum_fusion.2.weigh
  106.9 0.9 exponential_convert_fusion.2
  109.0 0.9 reshape.417.starts
  109.9 24.2 %mixer_out.1 = (bf16[6,320,512]{2,1,0:T(8,128)(2,1)}, bf16[6,320,1024]{2,1,0:T(8,128)(2,1)}, f32[6,320,512]{2,1,0:T(8,128)}, bf16[6,320,1024]{2,1,0:T(8,128)(2,1...) custom-call(f32[6,320,512]{2,1,0:T(8,128)} %get-tuple-element.73.y, ...), custom_call_target="tpu_custom_call", output_to_operand_aliasing={{7}: (9, {})} | custom-call | tf_op jit(solution)/shard_map/mixer_out/pallas_call | solution.py:1557
  134.1 54.0 %ffb.1 = (bf16[6,320,512]{2,1,0:T(8,128)(2,1)}, f32[6,320,512]{2,1,0:T(8,128)}, bf16[6,320,512]{2,1,0:T(8,128)(2,1)}, bf16[88,256,256]{2,1,0:T(8,128)(2,1)}, f32...) custom-call(bf16[6,320,512]{2,1,0:T(8,128)(2,1)} %get-tuple-element.78.g, ...), custom_call_target="tpu_custom_call" | custom-call | tf_op jit(solution)/shard_map/ffb/pallas_call | solution.py:1603
  188.1 30.8 %mixer_back.1 = (f32[6,320,512]{2,1,0:T(8,128)}, bf16[6,320,512]{2,1,0:T(8,128)(2,1)}, bf16[6,32,512]{2,1,0:T(8,128)(2,1)}, bf16[88,256,256]{2,1,0:T(8,128)(2,1)}, f32[8,512]{1,0:T(8,128)}, /*index=5*/f32[16,512]{1,0:T(8,128)}) custom-call(bf16[6,320,512]{2,1,0:T(8,128)(2,1)} %get-tuple-element.84.dq, ...), custom_call_target="tpu_custom_call", output_to_operand_aliasing={{3}: (14, {})} | custom-call | tf_op jit(solution)/shard_map/mixer_back/pallas_call | solution.py:1650
  218.9 23.3 %conv_back.1 = (f32[6,320,512]{2,1,0:T(8,128)}, f32[32,512]{1,0:T(8,128)}, f32[32,512]{1,0:T(8,128)}, f32[6,32,512]{2,1,0:T(8,128)}, f32[6,32,512]{2,1,0:T(8,128...) custom-call(bf16[6,320,512]{2,1,0:T(8,128)(2,1)} %get-tuple-element.70.u, ...), custom_call_target="tpu_custom_call" | custom-call | tf_op jit(solution)/shard_map/conv_back/pallas_call | solution.py:1708
  242.3 0.8 iota_multiply_fusion
  243.0 1.0 multiply_reduce_fusion
  244.2 1.0 pad_maximum_fusion.1.weigh
  245.2 37.6 %ffa_back.1 = (f32[6,320,512]{2,1,0:T(8,128)}, bf16[88,256,256]{2,1,0:T(8,128)(2,1)}, f32[2,8,512]{2,1,0:T(8,128)}, f32[4,32,512]{2,1,0:T(8,128)}) custom-call(f32[6,320,512]{2,1,0:T(8,128)} %get-tuple-element.94.du_loc, bf16[4,6,32,512]{3,2,1,0:T(8,128)(2,1)} %get-tuple-element.95.back_all, ...), custom_call_target="tpu_custom_call", output_to_operand_aliasing={{1}: (17, {})} | custom-call | tf_op jit(solution)/shard_map/ffa_back/pallas_call | solution.py:1742
  282.8 1.0 fusion.5
  283.8 0.8 reduce_sum.87
  285.3 0.7 bitcast_bitcast_fusion.small
  286.0 94.9 %reduce_grads.1 = (bf16[22,2,2,2,32,256]{5,4,3,2,1,0:T(8,128)(2,1)}, bf16[22,32,256]{2,1,0:T(8,128)(2,1)}, f32[120,128]{1,0:T(8,128)}) custom-call(bf16[4,22,4,2,32,256]{5,4,3,2,1,0:T(8,128)(2,1)} %bitcast.76, f32[4,120,128]{2,1,0:T(8,128)} %bitcast_bitcast_fusion.small), custom_call_target="tpu_custom_call" | custom-call | tf_op jit(solution)/shard_map/reduce_grads/pallas_call | solution.py:1342
  381.0 0.7 fusion.7.pick
  381.7 10.5 %shampoo.1 = (f32[22,32,256]{2,1,0:T(8,128)}, f32[22,32,256]{2,1,0:T(8,128)}, f32[22,32,256]{2,1,0:T(8,128)}, bf16[22,32,256]{2,1,0:T(8,128)(2,1)}, f32[22,32,256]{2,1,0:T(8,128)}) custom-call(bf16[32,256]{1,0:T(8,128)(2,1)} %fusion.7.pick, bf16[22,32,256]{2,1,0:T(8,128)(2,1)} %get-tuple-element.112.owned, bf16[22,256,256]{2,1,0:T(8,128)(2,1)} %bitcast.83, ...), custom_call_target="tpu_custom_call" | custom-call | tf_op jit(solution)/shard_map/shampoo/pallas_call | solution.py:1840
  394.5 1.3 multiply_subtract_fusion.2
  395.9 1.0 multiply_reduce_fusion.4
  396.9 0.8 multiply_reduce_fusion.3
  397.7 1.3 copy.101
  (99 shorter events, 9.1 us)
Async XLA Ops:
  0.6 0.9 copy-start
  0.7 2.7 copy-start.12
  51.8 25.2 %copy-start.3 = (f32[32,512]{1,0:T(8,128)}, f32[32,512]{1,0:T(8,128)S(1)}, u32[]{:S(2)}) copy-start(f32[32,512]{1,0:T(8,128)S(1)} %fusion.15.coup) | copy-start | bytes 196612
  245.2 37.6 %copy-start.6 = (f32[32,512]{1,0:T(8,128)S(1)}, f32[32,512]{1,0:T(8,128)}, u32[]{:S(2)}) copy-start(f32[32,512]{1,0:T(8,128)} %get-tuple-element.108) | copy-start | bytes 196612
  245.2 37.6 %copy-start.7 = (f32[32,512]{1,0:T(8,128)S(1)}, f32[32,512]{1,0:T(8,128)}, u32[]{:S(2)}) copy-start(f32[32,512]{1,0:T(8,128)} %get-tuple-element.111) | copy-start | bytes 196612
  245.2 39.4 %copy-start.11 = (f32[8,512]{1,0:T(8,128)S(1)}, f32[8,512]{1,0:T(8,128)}, u32[]{:S(2)}) copy-start(f32[8,512]{1,0:T(8,128)} %get-tuple-element.105) | copy-start | bytes 49156
  245.2 39.5 %copy-start.9 = (f32[2,8,512]{2,1,0:T(8,128)S(1)}, f32[2,8,512]{2,1,0:T(8,128)}, u32[]{:S(2)}) copy-start(f32[2,8,512]{2,1,0:T(8,128)} %get-tuple-element.106) | copy-start | bytes 98308
  245.2 39.5 %copy-start.10 = (f32[16,512]{1,0:T(8,128)S(1)}, f32[16,512]{1,0:T(8,128)}, u32[]{:S(2)}) copy-start(f32[16,512]{1,0:T(8,128)} %get-tuple-element.107) | copy-start | bytes 98308
  381.7 10.5 %copy-start.8 = (f32[120,128]{1,0:T(8,128)S(1)}, f32[120,128]{1,0:T(8,128)}, u32[]{:S(2)}) copy-start(f32[120,128]{1,0:T(8,128)} %get-tuple-element.119) | copy-start | bytes 184324
  381.7 12.2 %copy-start.4 = (f32[2,128,32]{1,2,0:T(8,128)S(1)}, f32[2,128,32]{1,2,0:T(8,128)}, u32[]{:S(2)}) copy-start(f32[2,128,32]{1,2,0:T(8,128)} %param.23) | copy-start | bytes 98308
  381.7 15.3 %copy-start.13 = (s32[6]{0:T(128)S(1)}, s32[6]{0:T(128)}, u32[]{:S(2)}) copy-start(s32[6]{0:T(128)} %param.15) | copy-start | bytes 76
  381.7 16.0 %copy-start.2 = (bf16[6,320,512]{2,1,0:T(8,128)(2,1)S(1)}, bf16[6,320,512]{2,1,0:T(8,128)(2,1)}, u32[]{:S(2)}) copy-start(bf16[6,320,512]{2,1,0:T(8,128)(2,1)} %get-tuple-element.204) | copy-start | bytes 5898244
  393.8 5.1 %copy-start.5 = (f32[64,128]{1,0:T(8,128)}, f32[64,128]{1,0:T(8,128)S(1)}, u32[]{:S(2)}) copy-start(f32[64,128]{1,0:T(8,128)S(1)} %slice.58) | copy-start | bytes 98308
  396.9 2.1 copy-start.1
where the time goes:
time: 403 us; the launch traced here: 399 us
  Pallas kernels  367 us (91%)
  other arithmetic  15.9 us (4%)
  local copies, waits for them, and re-layouts  14.9 us (4%)
    pallas_call x1, Pallas kernels, reduce_grads(): pl.pallas_call(partial(reduce_kernel, sizes), in_specs=[ANY, vmem], out_s...  94.9 us
    pallas_call x1, Pallas kernels, body(): pl.pallas_call(partial(ffb_kernel, scaling), grid=(rows,), in_specs=[row_...  54 us
    pallas_call x1, Pallas kernels, gather_first(): pl.pallas_call(gather_kernel, in_specs=[pl.BlockSpec(memory_space=pltpu.V...  41.7 us
    pallas_call x1, Pallas kernels, body(): pl.pallas_call(partial(ffa_back_kernel, scaling), grid=(rows,), in_specs=...  37.6 us
    pallas_call x1, Pallas kernels, body(): pl.pallas_call(partial(mixer_back_kernel, scaling), grid=(rows,), in_spec...  30.8 us
    pallas_call x1, Pallas kernels, body(): pl.pallas_call(conv_forward_kernel, grid=(D // LANES,), in_specs=[group_s...  27.5 us
    pallas_call x1, Pallas kernels, body(): pl.pallas_call(mixer_out_kernel, grid=(rows,), in_specs=[row_spec(frames,...  24.2 us
    pallas_call x1, Pallas kernels, body(): pl.pallas_call(conv_back_kernel, grid=(D // LANES,), in_specs=[group_spec...  23.3 us

commit v1 on v0

--- a/solution.py
+++ b/solution.py
@@ -442,6 +442,172 @@
     )(master, pack)
 
 
+R_XY = ("load", "cs", "cr", "xs", "xr", "ys", "yr")
+R_Z = ("zs", "zr")
+
+
+def reduce_sems(names, chunks=1):
+    width = {"x": (3,), "y": (3,), "z": (2,)}
+    dims = lambda name: width.get(name[0], ())
+    return [pltpu.SemaphoreType.DMA((chunks,) + dims(name)) for name in names]
+
+
+def square_bufs(m, parts, levels, slab):
+    vb = lambda *dims: pltpu.VMEM(dims + (slab, BS), bf16)
+    return [vb(parts, m, levels)] * 2 + [vb(2, m, levels)] * 2
+
+
+def level_bufs(m, slab):
+    vb = lambda *dims: pltpu.VMEM(dims + (slab, BS), bf16)
+    return [vb(m, 2), vb(m)]
+
+
+class Reduce:
+    def __init__(self, sizes, sems, grads=None, square_refs=None, red=None, level_refs=None, out=None):
+        self.sems, self.grads, self.red, self.out = sems, grads, red, out
+        if square_refs is not None:
+            self.mine, self.came, self.from_x, self.from_y = square_refs
+        if level_refs is not None:
+            self.near_in, self.far_in = level_refs
+        self.place, self.level, self.core = peers()
+        self.xp, self.yp, self.dp = square(self.place)
+        self.low, self.high = self.level % 2, self.level // 2
+        self.near_by = self.level + 1 - 2 * self.low
+        self.far_off = self.level + 2 - 4 * self.high
+        edges = [sum(sizes[:c]) for c in range(len(sizes) + 1)]
+        self.ranges = [(a, b, (a + b + 1) // 2) for a, b in zip(edges[:-1], edges[1:])]
+        self.all = range(len(sizes))
+
+    def n(self, c):
+        first, end, unused = self.ranges[c]
+        return pl.ds(first, end - first)
+
+    def load(self, c):
+        src = self.grads.at[:, self.n(c), :, self.core]
+        return pltpu.make_async_copy(src, self.mine.at[:, self.n(c)], self.sems["load"].at[c])
+
+    def swap(self, c):
+        return remote(
+            self.grads.at[:, self.n(c), :, 1 - self.core],
+            self.came.at[:, self.n(c)],
+            self.sems["cs"].at[c],
+            self.sems["cr"].at[c],
+            at(self.place, self.level, 1 - self.core),
+        )
+
+    def side(self, c, i, name, into, device, what):
+        owner, slot, first, end = what
+        n = pl.ds(first, end - first)
+        send, recv = self.sems[name + "s"].at[c, i], self.sems[name + "r"].at[c, i]
+        return remote(self.mine.at[owner, n], into.at[slot, n], send, recv, device)
+
+    def x(self, c, i):
+        first, end, mid = self.ranges[c]
+        what = ((self.dp, 0, first, mid), (self.xp, 1, first, mid), (self.xp, 1, mid, end))[i]
+        return self.side(c, i, "x", self.from_x, at(self.xp, self.level, self.core), what)
+
+    def y(self, c, i):
+        first, end, mid = self.ranges[c]
+        what = ((self.dp, 0, mid, end), (self.yp, 1, mid, end), (self.yp, 1, first, mid))[i]
+        return self.side(c, i, "y", self.from_y, at(self.yp, self.level, self.core), what)
+
+    def add(self, owner, first, end, ref, slot):
+        def one(k, carry):
+            self.mine[owner, k] = self.mine[owner, k] + ref[slot, k]
+            return carry
+
+        lax.fori_loop(first, end, one, 0)
+
+    def start(self, c):
+        self.load(c).start()
+        self.swap(c).start()
+
+    def begin(self, c):
+        first, end, unused = self.ranges[c]
+        self.load(c).wait()
+        self.swap(c).wait_recv()
+        self.add(self.dp, first, end, self.came, self.dp)
+        self.x(c, 0).start()
+        self.y(c, 0).start()
+        self.add(self.xp, first, end, self.came, self.xp)
+        self.x(c, 1).start()
+        self.add(self.yp, first, end, self.came, self.yp)
+        self.y(c, 1).start()
+        self.add(self.place, first, end, self.came, self.place)
+
+    def second(self, c):
+        first, end, mid = self.ranges[c]
+        self.x(c, 0).wait_recv()
+        self.add(self.yp, first, mid, self.from_x, 0)
+        self.y(c, 2).start()
+        self.y(c, 0).wait_recv()
+        self.add(self.xp, mid, end, self.from_y, 0)
+        self.x(c, 2).start()
+
+    def combine(self, c):
+        first, end, unused = self.ranges[c]
+        for i in (1, 2):
+            self.x(c, i).wait_recv()
+            self.y(c, i).wait_recv()
+
+        def one(k, carry):
+            total = self.mine[self.place, k].astype(f32) + self.from_x[1, k].astype(f32)
+            total = (total + self.from_y[1, k].astype(f32)).astype(bf16)
+            self.red[k] = total.reshape(self.red.shape[1:])
+            return carry
+
+        lax.fori_loop(first, end, one, 0)
+
+    def square_end(self, c):
+        self.swap(c).wait_send()
+        for i in range(3):
+            self.x(c, i).wait_send()
+            self.y(c, i).wait_send()
+
+    def near(self, c):
+        return remote(
+            self.red.at[self.n(c), :, 1 - self.low],
+            self.near_in.at[self.n(c)],
+            self.sems["zs"].at[c, 0],
+            self.sems["zr"].at[c, 0],
+            at(self.place, self.near_by, self.core),
+        )
+
+    def far(self, c):
+        return remote(
+            self.near_in.at[self.n(c), 1 - self.high],
+            self.far_in.at[self.n(c)],
+            self.sems["zs"].at[c, 1],
+            self.sems["zr"].at[c, 1],
+            at(self.place, self.far_off, self.core),
+        )
+
+    def across(self, c):
+        first, end, unused = self.ranges[c]
+        self.near(c).wait_recv()
+
+        def one(k, carry):
+            self.near_in[k] = self.red[k, :, self.low] + self.near_in[k]
+            return carry
+
+        lax.fori_loop(first, end, one, 0)
+        self.far(c).start()
+
+    def settle(self, c):
+        first, end, unused = self.ranges[c]
+        self.far(c).wait_recv()
+
+        def one(k, carry):
+            self.out[k] = self.near_in[k, self.high] + self.far_in[k]
+            return carry
+
+        lax.fori_loop(first, end, one, 0)
+
+    def levels_end(self, c):
+        self.near(c).wait_send()
+        self.far(c).wait_send()
+
+
 def ffa_forward_kernel(feat, small, stack, mfin, *refs):
     step, last = pl.program_id(0), pl.num_programs(0) - 1
     pair = None
@@ -833,25 +999,39 @@
     def _():
         ffn, mix = D // BS * (FF // BS), (D // BS) ** 2
         plan = (
-            (acc_in, 2 * ffn, False),
-            (acc_out, 3 * ffn, True),
-            (acc_q, 4 * ffn + 5 * mix, False),
+            (acc_in, 0, False),
+            (acc_out, ffn, True),
+            (acc_q, 2 * ffn, False),
         )
         store_blocks(plan, scale, grads, stage, sem)
 
 
 def mixer_back_kernel(
-    scale, dq, dlow, dhigh, g, glow, ghigh, pw, x2, gated, ys, dx3, small, stack, pfull_t, grads_in,
-    dx2_o, dy_o, gst_o, grads, gain_o, dk_o,
-    wo, wp, acc_p, acc_o, dpad, gpad, dg_s, dk_s, stage, k_n, k_dpw, k_ys, k_dg, sem,
+    scale, dq, dlow, dhigh, g, glow, ghigh, pw, x2, gated, ys, dx3, small, stack, pfull_t, *refs
 ):
-    step = pl.program_id(0)
+    step, last = pl.program_id(0), pl.num_programs(0) - 1
     frames = dq.shape[1]
+    rest = None
+    if len(refs) > 20:
+        grads_rest, refs = refs[0], refs[1:]
+        red, bufs, sems = refs[6], refs[21:25], refs[25:]
+        half = (red.shape[0] + 1) // 2
+        rest = Reduce((half, red.shape[0] - half), dict(zip(R_XY, sems)), grads_rest, bufs, red)
+        refs = refs[:6] + refs[7:21]
+    dx2_o, dy_o, gst_o, grads, gain_o, dk_o, wo, wp, acc_p, acc_o, dpad, gpad = refs[:12]
+    dg_s, dk_s, stage, k_n, k_dpw, k_ys, k_dg, sem = refs[12:]
 
     @pl.when(step == 0)
     def _():
         ffn, mix = D // BS * (FF // BS), (D // BS) ** 2
+        if rest is not None:
+            greet([at(other, rest.level, rest.core) for other in (rest.xp, rest.yp, rest.dp)])
+            greet([at(rest.place, rest.level, 1 - rest.core)])
         load_matrices(stack, ((0, wo), (2 * mix, wp)), sem)
+        if rest is not None:
+            met(4)
+            for c in rest.all:
+                rest.start(c)
         acc_p[...] = jnp.zeros_like(acc_p)
         acc_o[...] = jnp.zeros_like(acc_o)
         gain_o[...] = jnp.zeros_like(gain_o)
@@ -897,6 +1077,11 @@
     dy_o[0] = dy
     local_states(pfull_t, dy, gst_o)
 
+    if rest is not None:
+        for c in rest.all:
+            pl.when(step == 0)(lambda c=c: rest.begin(c))
+            pl.when(step == last - 3 + 2 * c)(lambda c=c: rest.second(c))
+
     @pl.when(step % group == group - 1)
     def _():
         acc_p[...] += mm_tn(k_n[...], k_dpw[...])
@@ -905,8 +1090,12 @@
     @pl.when(step == pl.num_programs(0) - 1)
     def _():
         ffn, mix = D // BS * (FF // BS), (D // BS) ** 2
-        plan = ((acc_o, 4 * ffn + mix, False), (acc_p, 4 * ffn + 3 * mix, False))
+        plan = ((acc_o, 0, False), (acc_p, 2 * mix, False))
         store_blocks(plan, scale, grads, stage, sem)
+        if rest is not None:
+            for c in rest.all:
+                rest.combine(c)
+                rest.square_end(c)
         for j in range(KW):
             dk_o[j : j + 1] = jnp.sum(dk_s[j], axis=0, keepdims=True)
 
@@ -1014,16 +1203,39 @@
 
 def ffa_back_kernel(
     scale, du_loc, back_all, ends_all, back_ends, ends_w, back_w, starts, weigh, coup,
-    x1, feat, inner_r, act_r, dx2, small, stack, mfin_t, grads_in,
-    dx0_o, grads, gain_o, sums_o,
-    wi, wo, wu, acc_in, acc_out, acc_u, mask, stage, k_act, k_din, k_n, k_dp, k_m, k_du, sem,
+    x1, feat, inner_r, act_r, dx2, small, stack, mfin_t, *refs
 ):
-    step = pl.program_id(0)
+    step, last = pl.program_id(0), pl.num_programs(0) - 1
+    pair = None
+    if len(refs) > 19:
+        grads_pair, red_in, refs = refs[0], refs[1], refs[2:]
+        out_pair, out_rest = refs[4:6]
+        red_rest, rest_bufs, red_pair, square_refs = refs[21], refs[22:24], refs[24], refs[25:29]
+        pair_bufs, sems = refs[29:31], refs[31:]
+        refs = refs[:4] + refs[6:21]
+        pair = Reduce(
+            out_pair.shape[:1], dict(zip(R_XY + R_Z, sems)), grads_pair, square_refs, red_pair,
+            pair_bufs, out_pair,
+        )
+        rest = Reduce(
+            out_rest.shape[:1], dict(zip(R_Z, sems[9:])), None, None, red_rest, rest_bufs, out_rest
+        )
+    dx0_o, grads, gain_o, sums_o, wi, wo, wu, acc_in, acc_out, acc_u = refs[:10]
+    mask, stage, k_act, k_din, k_n, k_dp, k_m, k_du, sem = refs[10:]
 
     @pl.when(step == 0)
     def _():
         ffn, mix = D // BS * (FF // BS), (D // BS) ** 2
+        if pair is not None:
+            greet([at(other, pair.level, pair.core) for other in (pair.xp, pair.yp, pair.dp)])
+            greet([at(pair.place, other, pair.core) for other in (pair.near_by, pair.far_off)])
+            greet([at(pair.place, pair.level, 1 - pair.core)])
+            red_rest[...] = red_in[...]
         load_matrices(stack, ((0, wi), (ffn, wo), (2 * ffn, wu)), sem)
+        if pair is not None:
+            met(6)
+            pair.start(0)
+            rest.near(0).start()
         mask[...] = head_mask()
         acc_in[...] = jnp.zeros_like(acc_in)
         acc_out[...] = jnp.zeros_like(acc_out)
@@ -1069,6 +1281,30 @@
     gain_o[0] += fold8(dn0 * hat0)
     dx0_o[0] = dx1 + norm_back(hat0, inv0, small[0:1], dn0)
 
+    if pair is not None:
+
+        @pl.when(step == 0)
+        def _():
+            pair.begin(0)
+
+        @pl.when(step == last - 4)
+        def _():
+            rest.across(0)
+
+        @pl.when(step == last - 3)
+        def _():
+            pair.second(0)
+
+        @pl.when(step == last - 2)
+        def _():
+            rest.settle(0)
+            pair.combine(0)
+            pair.near(0).start()
+
+        @pl.when(step == last - 1)
+        def _():
+            pair.across(0)
+
     @pl.when(step % group == group - 1)
     def _():
         acc_out[...] += mm_tn(k_dp[...], k_act[...])
@@ -1078,8 +1314,13 @@
     @pl.when(step == pl.num_programs(0) - 1)
     def _():
         ffn, mix = D // BS * (FF // BS), (D // BS) ** 2
-        plan = ((acc_in, 0, False), (acc_out, ffn, True), (acc_u, 4 * ffn, False))
+        plan = ((acc_in, 0, False), (acc_out, ffn, True), (acc_u, 2 * ffn, False))
         store_blocks(plan, scale, grads, stage, sem)
+        if pair is not None:
+            pair.settle(0)
+            pair.square_end(0)
+            pair.levels_end(0)
+            rest.levels_end(0)
 
 
 def shampoo_kernel(
@@ -1099,270 +1340,234 @@
         nc_o[i] = new.astype(bf16)
 
 
+def deliveries(sizes, parts, count):
+    edges = [sum(sizes[:c]) for c in range(len(sizes) + 1)]
+    runs = []
+    for which, ids in enumerate(block_sets()):
+        for owner, k, v, j, n in move_runs(ids, parts, count):
+            if which:
+                runs.append((0, which, owner, k, v, j, n))
+                continue
+            for c, (a, b) in enumerate(zip(edges[:-1], edges[1:])):
+                low, high = max(a, j), min(b, j + n)
+                if low < high:
+                    runs.append((c + 1, 0, owner, k + low - j, v, low, high - low))
+    groups = []
+    for chunk, unused, owner, k, v, j, n in sorted(runs, key=lambda run: (run[0], run[2], run[3])):
+        if groups and groups[-1][:2] == (chunk, owner) and sum(groups[-1][2:]) == k:
+            groups[-1] = (chunk, owner, groups[-1][2], groups[-1][3] + n)
+        else:
+            groups.append((chunk, owner, k, n))
+    return runs, groups
+
+
 def reduce_kernel(
-    sizes, grads, small, full, owned, small_sum,
-    mine, came, from_x, from_y, red, near_in, far_in, s_tm, s_core, s_z,
-    load_sem, c_send, c_recv, x_send, x_recv, y_send, y_recv,
-    z_send, z_recv, f_send, f_recv, s_send, s_recv, put_sem,
+    sizes, runs, groups, grads, share_pair, share_rest, small, full, owned_o, small_sum,
+    mine, came, from_x, from_y, red, near_in, far_in, share_first, owned, s_tm, s_core, s_z,
+    d_send, d_recv, a_send, a_recv, f_send, f_recv, s_send, s_recv, put_sem, *sems,
 ):
-    place, level, core = peers()
-    low, high = level % 2, level // 2
-    near, far = level + 1 - 2 * low, level + 2 - 4 * high
-    xp, yp, dp = others = square(place)
+    it = Reduce(
+        sizes, dict(zip(R_XY + R_Z, sems)), grads, (mine, came, from_x, from_y), red,
+        (near_in, far_in), share_first,
+    )
+    place, level, core = it.place, it.level, it.core
+    low, high, near, far = it.low, it.high, it.near_by, it.far_off
+    diagonal = 2 * (1 - high) + 1 - low
+    others = (it.xp, it.yp, it.dp)
     greet([at(other, level, core) for other in others])
-    greet([at(place, level, 1 - core), at(place, near, core), at(place, far, core)])
-    diagonal = 2 * (1 - high) + 1 - low
-    greet([at(place, diagonal, core)])
-    edges = [sum(sizes[:c]) for c in range(len(sizes) + 1)]
-    ranges = [(a, b, (a + b + 1) // 2) for a, b in zip(edges[:-1], edges[1:])]
-    sends = []
-
-    def go(copy):
-        copy.start()
-        sends.append(copy)
-        return copy
-
-    loads, core_in = [], []
-    for c, (first, end, unused) in enumerate(ranges):
-        n = pl.ds(first, end - first)
-        load = pltpu.make_async_copy(grads.at[:, n, :, core], mine.at[:, n], load_sem.at[c])
-        load.start()
-        loads.append(load)
+    greet([at(place, other, core) for other in (near, far, diagonal)])
+    greet([at(place, level, 1 - core)])
+    shares = (share_first, share_pair, share_rest)
+
+    def deliver(index):
+        unused, which, owner, k, v, j, n = runs[index]
+        src, dst = shares[which].at[pl.ds(j, n)], owned.at[pl.ds(k, n)]
+        if owner == v:
+            return pltpu.make_async_copy(src, dst, d_send.at[index])
+        return remote(src, dst, d_send.at[index], d_recv.at[index], at(owner, level, core))
+
+    def in_chunk(c):
+        return [i for i, run in enumerate(runs) if run[0] == c]
+
+    def send_out(c):
+        for i in in_chunk(c):
+            pl.when(place == runs[i][4])(lambda i=i: deliver(i).start())
+
+    def come_in(c):
+        for i in in_chunk(c):
+            local = runs[i][2] == runs[i][4]
+            done = (lambda i=i: deliver(i).wait()) if local else (lambda i=i: deliver(i).wait_recv())
+            pl.when(place == runs[i][2])(done)
+
+    def sent_out():
+        for i, run in enumerate(runs):
+            if run[2] != run[4]:
+                pl.when(place == run[4])(lambda i=i: deliver(i).wait_send())
+
+    def spot(g, where):
+        unused, owner, k, n = groups[g]
+        return full.at[pl.ds(k, n), where // 2, where % 2, core]
+
+    def held(g):
+        unused, owner, k, n = groups[g]
+        return owned.at[pl.ds(k, n)]
+
+    def put(g):
+        return pltpu.make_async_copy(held(g), spot(g, level), put_sem.at[g])
+
+    def along(g, i):
+        src = spot(g, far) if i == 2 else held(g)
+        dst = spot(g, far if i == 2 else level)
+        target = at(place, far if i == 0 else near, core)
+        return remote(src, dst, a_send.at[g, i], a_recv.at[g, i], target)
+
+    def to_core(g, i):
+        where = (level, far, near, diagonal)[i]
+        src = held(g) if i == 0 else spot(g, where)
+        target = at(place, level, 1 - core)
+        return remote(src, spot(g, where), f_send.at[g, i], f_recv.at[g, i], target)
+
+    def for_groups(c, act):
+        for g, group in enumerate(groups):
+            if c is None or group[0] == c:
+                pl.when(place == group[1])(lambda g=g: act(g))
+
+    def spread(g):
+        put(g).start()
+        along(g, 0).start()
+        along(g, 1).start()
+        to_core(g, 0).start()
+
+    def pass_on(g):
+        along(g, 0).wait_recv()
+        along(g, 2).start()
+        to_core(g, 1).start()
+        along(g, 1).wait_recv()
+        to_core(g, 2).start()
+
+    def last(g):
+        along(g, 2).wait_recv()
+        to_core(g, 3).start()
+
+    def finish(g):
+        put(g).wait()
+        for i in range(4):
+            to_core(g, i).wait_recv()
+        for i in range(4):
+            to_core(g, i).wait_send()
+        for i in range(3):
+            along(g, i).wait_send()
+
+    def to_place(d):
+        send, recv = s_send.at[d], s_recv.at[d]
+        return remote(small.at[others[d]], s_tm.at[d], send, recv, at(others[d], level, core))
+
+    def to_sibling():
+        target = at(place, level, 1 - core)
+        return remote(s_core.at[0], s_core.at[1], s_send.at[3], s_recv.at[3], target)
+
+    def to_level(d):
+        target = at(place, (near, far, diagonal)[d], core)
+        return remote(s_z.at[level], s_z.at[level], s_send.at[4 + d], s_recv.at[4 + d], target)
+
+    def reduced(c):
+        it.combine(c)
+        it.near(c).start()
+
+    def settled(c):
+        it.settle(c)
+        send_out(c + 1)
+
+    def arrived(c):
+        come_in(c + 1)
+        for_groups(c + 1, spread)
+
     met(7)
-    for c, (first, end, unused) in enumerate(ranges):
-        n = pl.ds(first, end - first)
-        core_in.append(
-            go(
-                remote(
-                    grads.at[:, n, :, 1 - core], came.at[:, n], c_send.at[c], c_recv.at[c],
-                    at(place, level, 1 - core),
-                )
-            )
-        )
-
-    small_in = [
-        go(remote(small.at[other], s_tm.at[d], s_send.at[d], s_recv.at[d], at(other, level, core)))
-        for d, other in enumerate(others)
-    ]
-
-    def add(owner, first, end):
-        def one(k, carry):
-            mine[owner, k] = mine[owner, k] + came[owner, k]
-            return carry
-
-        lax.fori_loop(first, end, one, 0)
-
-    def add_into(owner, ref, first, end):
-        def one(k, carry):
-            mine[owner, k] = mine[owner, k] + ref[0, k]
-            return carry
-
-        lax.fori_loop(first, end, one, 0)
-
-    def to_x(c, i, owner, slot, first, end):
-        n = pl.ds(first, end - first)
-        send, recv = x_send.at[c, i], x_recv.at[c, i]
-        return go(
-            remote(mine.at[owner, n], from_x.at[slot, n], send, recv, at(xp, level, core))
-        )
-
-    def to_y(c, i, owner, slot, first, end):
-        n = pl.ds(first, end - first)
-        send, recv = y_send.at[c, i], y_recv.at[c, i]
-        return go(
-            remote(mine.at[owner, n], from_y.at[slot, n], send, recv, at(yp, level, core))
-        )
-
-    def begin(c):
-        first, end, middle = ranges[c]
-        loads[c].wait()
-        core_in[c].wait_recv()
-        add(dp, first, end)
-        x_one = to_x(c, 0, dp, 0, first, middle)
-        y_one = to_y(c, 0, dp, 0, middle, end)
-        add(xp, first, end)
-        x_two = to_x(c, 1, xp, 1, first, middle)
-        add(yp, first, end)
-        y_two = to_y(c, 1, yp, 1, middle, end)
-        add(place, first, end)
-        return x_one, y_one, x_two, y_two
-
-    def second(c, copies):
-        first, end, middle = ranges[c]
-        copies[0].wait_recv()
-        add_into(yp, from_x, first, middle)
-        y_three = to_y(c, 2, yp, 1, first, middle)
-        copies[1].wait_recv()
-        add_into(xp, from_y, middle, end)
-        x_three = to_x(c, 2, xp, 1, middle, end)
-        return copies[2], copies[3], x_three, y_three
-
-    def along(c, copies):
-        first, end, unused = ranges[c]
-        for copy in copies:
-            copy.wait_recv()
-
-        def one(k, carry):
-            total = mine[place, k].astype(f32) + from_x[1, k].astype(f32)
-            total = (total + from_y[1, k].astype(f32)).astype(bf16)
-            red[k] = total.reshape(red.shape[1:])
-            return carry
-
-        lax.fori_loop(first, end, one, 0)
-        n = pl.ds(first, end - first)
-        return go(
-            remote(
-                red.at[n, :, 1 - low], near_in.at[n], z_send.at[c, 0], z_recv.at[c, 0],
-                at(place, near, core),
-            )
-        )
-
-    def across(c, copy):
-        first, end, unused = ranges[c]
-        copy.wait_recv()
-
-        def one(k, carry):
-            near_in[k] = red[k, :, low] + near_in[k]
-            return carry
-
-        lax.fori_loop(first, end, one, 0)
-        n = pl.ds(first, end - first)
-        return go(
-            remote(
-                near_in.at[n, 1 - high], far_in.at[n], z_send.at[c, 1], z_recv.at[c, 1],
-                at(place, far, core),
-            )
-        )
-
-    def to_core(c, i, source):
-        first, end, unused = ranges[c]
-        spot = full.at[pl.ds(first, end - first), source // 2, source % 2, core]
-        src = owned.at[pl.ds(first, end - first)] if i == 0 else spot
-        return go(
-            remote(src, spot, f_send.at[c, i], f_recv.at[c, i], at(place, level, 1 - core))
-        )
-
-    def settle(c, copy):
-        first, end, unused = ranges[c]
-        copy.wait_recv()
-
-        def one(k, carry):
-            owned[k] = near_in[k, high] + far_in[k]
-            return carry
-
-        lax.fori_loop(first, end, one, 0)
-        n = pl.ds(first, end - first)
-        spot = full.at[n, high, low, core]
-        put = pltpu.make_async_copy(owned.at[n], spot, put_sem.at[c])
-        put.start()
-        to_far = go(
-            remote(owned.at[n], spot, z_send.at[c, 2], z_recv.at[c, 2], at(place, far, core))
-        )
-        to_near = go(
-            remote(owned.at[n], spot, z_send.at[c, 3], z_recv.at[c, 3], at(place, near, core))
-        )
-        return put, to_far, to_near, to_core(c, 0, level)
-
-    def pass_on(c, state):
-        first, end, unused = ranges[c]
-        put, to_far, to_near, own = state
-        to_far.wait_recv()
-        spot = full.at[pl.ds(first, end - first), 1 - high, low, core]
-        more = go(
-            remote(spot, spot, z_send.at[c, 4], z_recv.at[c, 4], at(place, near, core))
-        )
-        passed = [own, to_core(c, 1, far)]
-        to_near.wait_recv()
-        passed.append(to_core(c, 2, near))
-        return put, more, passed
-
-    def last(c, state):
-        put, more, passed = state
-        more.wait_recv()
-        passed.append(to_core(c, 3, diagonal))
-        return put, passed
-
+    for c in it.all:
+        it.start(c)
+    send_out(0)
+    for d in range(3):
+        to_place(d).start()
     stages = (
-        lambda c, state: begin(c), second, along, across, settle, pass_on, last
+        it.begin, it.second, reduced, it.across, settled, arrived,
+        lambda c: for_groups(c + 1, pass_on), lambda c: for_groups(c + 1, last),
     )
-    chunks = len(ranges)
-    state = [None] * chunks
+    chunks = len(sizes)
     for tick in range(chunks + len(stages) - 1):
         for index, stage in enumerate(stages):
-            c = tick - index
-            if 0 <= c < chunks:
-                state[c] = stage(c, state[c])
+            if 0 <= tick - index < chunks:
+                stage(tick - index)
         if tick == 0:
-            for copy in small_in:
-                copy.wait_recv()
+            come_in(0)
+            for_groups(0, spread)
+            for d in range(3):
+                to_place(d).wait_recv()
             s_core[0] = small[place] + (s_tm[0] + s_tm[1]) + s_tm[2]
-            swap = go(
-                remote(
-                    s_core.at[0], s_core.at[1], s_send.at[3], s_recv.at[3],
-                    at(place, level, 1 - core),
-                )
-            )
+            to_sibling().start()
         if tick == 1:
-            swap.wait_recv()
+            to_sibling().wait_recv()
             s_z[level] = s_core[0] + s_core[1]
-            spot = s_z.at[level]
-            small_z = [
-                go(
-                    remote(spot, spot, s_send.at[4 + d], s_recv.at[4 + d], at(place, target, core))
-                )
-                for d, target in enumerate((near, far, diagonal))
-            ]
-    for copy in small_z:
-        copy.wait_recv()
+            for d in range(3):
+                to_level(d).start()
+        if tick == 2:
+            for_groups(0, pass_on)
+        if tick == 3:
+            for_groups(0, last)
+    for d in range(3):
+        to_level(d).wait_recv()
     small_sum[...] = (s_z[0] + s_z[1]) + (s_z[2] + s_z[3])
-    for put, passed in state:
-        put.wait()
-        for copy in passed:
-            copy.wait_recv()
-    for copy in sends:
-        copy.wait_send()
-
-
-def reduce_grads(grads, small, parts, devices, slab):
+    owned_o[...] = owned[...]
+    for_groups(None, finish)
+    for c in it.all:
+        it.square_end(c)
+        it.levels_end(c)
+    sent_out()
+    for d in range(3):
+        to_place(d).wait_send()
+        to_level(d).wait_send()
+    to_sibling().wait_send()
+
+
+def reduce_grads(first, pair, rest, small, parts, devices, slab):
     levels = devices // 2
+    ffn, mix = D // BS * (FF // BS), (D // BS) ** 2
     if parts != 4 or levels != 4:
-        owned = lax.psum_scatter(grads, "tm", scatter_dimension=0, tiled=True)
+        grads = [first[: 2 * ffn], rest[: 2 * ffn], first[2 * ffn :], pair, rest[2 * ffn :]]
+        owned = jnp.concatenate(grads, axis=0)
+        owned = lax.psum_scatter(owned, "tm", scatter_dimension=0, tiled=True)
         owned = lax.psum_scatter(owned, "rows", scatter_dimension=1, tiled=True)
         full = lax.all_gather(owned, "rows", axis=1, tiled=True)
         small = lax.psum_scatter(small, "tm", scatter_dimension=0, tiled=True)[0]
         return full, owned, lax.psum(small, "rows")
-    count = grads.shape[0] // parts
-    sizes = (6, 6, 5, 3, 2)
-    grads = grads.reshape(parts, count, levels, 2, slab, BS)
+    sizes = (3, 3, 3)
+    m, chunks = first.shape[1], len(sizes)
+    count = sum(len(ids) for ids in block_sets()) // parts
+    runs, groups = deliveries(sizes, parts, count)
     dma = lambda *dims: pltpu.SemaphoreType.DMA(dims)
-    vb = lambda *dims: pltpu.VMEM(dims, bf16)
+    vb = lambda *dims: pltpu.VMEM(dims + (slab, BS), bf16)
     vmem = pl.BlockSpec(memory_space=pltpu.VMEM)
     part = small.shape[1:]
-    chunks = len(sizes)
     full, owned, small_sum = pl.pallas_call(
-        partial(reduce_kernel, sizes),
-        in_specs=[ANY, vmem],
+        partial(reduce_kernel, sizes, runs, groups),
+        in_specs=[ANY, vmem, vmem, vmem],
         out_specs=[ANY, vmem, vmem],
         out_shape=[
             shape((count, 2, 2, 2, slab, BS), bf16),
             shape((count, slab, BS), bf16),
             shape(part),
         ],
-        scratch_shapes=[
-            vb(parts, count, levels, slab, BS), vb(parts, count, levels, slab, BS),
-            vb(2, count, levels, slab, BS), vb(2, count, levels, slab, BS),
-            vb(count, 2, 2, slab, BS), vb(count, 2, slab, BS), vb(count, slab, BS),
-            vm(3, *part), vm(2, *part), vm(levels, *part),
-            dma(chunks), dma(chunks), dma(chunks),
-            dma(chunks, 3), dma(chunks, 3), dma(chunks, 3), dma(chunks, 3),
-            dma(chunks, 5), dma(chunks, 5), dma(chunks, 4), dma(chunks, 4),
-            dma(7), dma(7), dma(chunks),
-        ],
+        scratch_shapes=square_bufs(m, parts, levels, slab)
+        + [vb(m, 2, 2)]
+        + level_bufs(m, slab)
+        + [vb(m), vb(count), vm(3, *part), vm(2, *part), vm(levels, *part)]
+        + [dma(len(runs)), dma(len(runs)), dma(len(groups), 3), dma(len(groups), 3)]
+        + [dma(len(groups), 4), dma(len(groups), 4), dma(7), dma(7), dma(len(groups))]
+        + reduce_sems(R_XY + R_Z, chunks),
         compiler_params=pltpu.CompilerParams(
             collective_id=2, has_side_effects=True, vmem_limit_bytes=VMEM_BYTES
         ),
         name="reduce_grads",
-    )(grads, small)
+    )(first, pair, rest, small)
     return full.reshape(count, BS, BS), owned, small_sum
 
 
@@ -1599,8 +1804,16 @@
         rest = done[0].reshape(-1, BS, BS)
 
     kept = lambda *widths: [mat(group * frames, w) for w in widths]
-    grad_shape = shape((parts * master.shape[0], BS, BS), bf16)
-    layer_out, dx3, dq, grads, gain_b, d_low, d_high = pl.pallas_call(
+    slab = master.shape[1]
+    spread_back = spread_out and levels == 4
+    sizes = [len(ids) // parts for ids in block_sets()]
+    if spread_back:
+        grad_shapes = [shape((parts, n, levels, 2, slab, BS), bf16) for n in sizes]
+        flat_shapes = [shape((parts * n, BS, BS), bf16) for n in sizes]
+    else:
+        flat_shapes = [shape((len(ids), BS, BS), bf16) for ids in block_sets()]
+    unflat = lambda v, k: v.reshape(grad_shapes[k].shape) if spread_back else v
+    layer_out, dx3, dq, grads_rest, gain_b, d_low, d_high = pl.pallas_call(
         partial(ffb_kernel, scaling),
         grid=(rows,),
         in_specs=[
@@ -1625,7 +1838,7 @@
             shape((rows, frames, D), bf16),
             shape((rows, frames, D)),
             shape((rows, frames, D), bf16),
-            grad_shape,
+            flat_shapes[2],
             shape((2, 8, D)),
         ]
         + edge_shapes,
@@ -1647,7 +1860,7 @@
         name="ffb",
     )(g, g_low, g_high, x2, cotangent, small_params, rest)
 
-    dx2, dy, back_ends, grads, gain_c, kernel_grads = pl.pallas_call(
+    dx2, dy, back_ends, grads_pair, gain_c, kernel_grads, *red_rest = pl.pallas_call(
         partial(mixer_back_kernel, scaling),
         grid=(rows,),
         in_specs=[
@@ -1665,8 +1878,8 @@
             small_spec,
             ANY,
             whole_spec(HEADS * NST, frames),
-            ANY,
-        ],
+        ]
+        + [ANY] * spread_back,
         out_specs=[
             row_spec(frames, D),
             row_spec(frames, D),
@@ -1674,15 +1887,17 @@
             ANY,
             whole_spec(8, D),
             whole_spec(16, D),
-        ],
+        ]
+        + [whole_spec(sizes[2], 2, 2, slab, BS)] * spread_back,
         out_shape=[
             shape((rows, frames, D)),
             shape((rows, frames, D), bf16),
             shape((rows, NST, D), bf16),
-            grad_shape,
+            flat_shapes[1],
             shape((8, D)),
             shape((16, D)),
-        ],
+        ]
+        + [shape((sizes[2], 2, 2, slab, BS), bf16)] * spread_back,
         scratch_shapes=[
             mat(D, 2 * D),
             mat(D, 2 * D),
@@ -1695,13 +1910,13 @@
             vm(4 * mix, BS, BS, dtype=bf16),
         ]
         + kept(D, 2 * D, D, 2 * D)
-        + [dma],
-        input_output_aliases={14: 3},
-        compiler_params=PARAMS,
+        + [dma]
+        + (square_bufs(sizes[2], parts, levels, slab) + reduce_sems(R_XY, 2)) * spread_back,
+        compiler_params=talking(8) if spread_back else PARAMS,
         name="mixer_back",
     )(
         dq, d_low, d_high, g, g_low, g_high, pw, x2, gated, ys, dx3, small_params, pair,
-        pfull_t, grads,
+        pfull_t, *[unflat(grads_rest, 2)] * spread_back,
     )
 
     nst_spec = pl.BlockSpec((rows, NST, LANES), lambda i: (0, 0, i))
@@ -1739,7 +1954,7 @@
         name="conv_back",
     )(u, dy, back_ends, tab_a, tab_b, power, coupling, taps_b)
 
-    grad_zero, grads, gain_a, sums_c = pl.pallas_call(
+    grad_zero, grads_first, gain_a, sums_c, *shares = pl.pallas_call(
         partial(ffa_back_kernel, scaling),
         grid=(rows,),
         in_specs=[
@@ -1760,15 +1975,17 @@
             small_spec,
             ANY,
             whole_spec(frames, HEADS * NST),
-            ANY,
-        ],
-        out_specs=[row_spec(frames, D), ANY, whole_spec(2, 8, D), whole_spec(4, NST, D)],
+        ]
+        + [ANY, whole_spec(sizes[2], 2, 2, slab, BS)] * spread_back,
+        out_specs=[row_spec(frames, D), ANY, whole_spec(2, 8, D), whole_spec(4, NST, D)]
+        + [whole_spec(n, slab, BS) for n in sizes[1:]] * spread_back,
         out_shape=[
             shape((rows, frames, D)),
-            grad_shape,
+            flat_shapes[0],
             shape((2, 8, D)),
             shape((4, NST, D)),
-        ],
+        ]
+        + [shape((n, slab, BS), bf16) for n in sizes[1:]] * spread_back,
         scratch_shapes=[
             mat(D, FF),
             mat(FF, D),
@@ -1780,13 +1997,22 @@
             vm(2 * ffn + mix, BS, BS, dtype=bf16),
         ]
         + kept(FF, FF, D, D, D, D)
-        + [dma],
-        input_output_aliases={17: 1},
-        compiler_params=PARAMS,
+        + [dma]
+        + (
+            [vm(sizes[2], 2, 2, slab, BS, dtype=bf16)]
+            + level_bufs(sizes[2], slab)
+            + [vm(sizes[1], 2, 2, slab, BS, dtype=bf16)]
+            + square_bufs(sizes[1], parts, levels, slab)
+            + level_bufs(sizes[1], slab)
+            + reduce_sems(R_XY + R_Z + R_Z)
+        )
+        * spread_back,
+        compiler_params=talking(9) if spread_back else PARAMS,
         name="ffa_back",
     )(
         du_loc, back_all, ends_all, back_ends, ends_w, back_w, starts, weigh_back, coupling,
-        x1, features, inner_a, act_a, dx2, small_params, first, mfin_t, grads,
+        x1, features, inner_a, act_a, dx2, small_params, first, mfin_t,
+        *([unflat(grads_pair, 1)] + red_rest) * spread_back,
     )
 
     lag_grad_c = jnp.sum(lag_decay * lag_grads[:, None, :], axis=0)
@@ -1809,7 +2035,12 @@
     lanes_own = lambda v: lax.dynamic_slice_in_dim(v, own, own_channels, v.ndim - 1)
     stacked = stacked.reshape(-1, parts, own_channels).transpose(1, 0, 2)
     full_grad, owned, sums = reduce_grads(
-        grads, stacked, parts, lax.axis_size("rows"), master.shape[1]
+        unflat(grads_first, 0),
+        *(shares if spread_back else (grads_pair, grads_rest)),
+        stacked,
+        parts,
+        devices,
+        slab,
     )
     count_small = small_params.shape[0]
     small_sum = sums[:count_small]

time: 403 us -> 392 us (0.973)
  Pallas kernels: 367 us -> 353 us
    pallas_call x1, Pallas kernels: 94.9 us -> 73.7 us  [reduce_grads(): pl.pallas_call(partial(reduce_kernel, sizes, runs, groups), in_specs=[ANY...]
    pallas_call x1, Pallas kernels: 37.6 us -> 43.2 us  [body(): pl.pallas_call(partial(ffa_back_kernel, scaling), grid=(rows,), in_specs=...]
where the time goes in v1:
time: 392 us; the launch traced here: 388 us
  Pallas kernels  353 us (90%)
  local copies, waits for them, and re-layouts  17.3 us (4%)
  other arithmetic  15.9 us (4%)
    pallas_call x1, Pallas kernels, reduce_grads(): pl.pallas_call(partial(reduce_kernel, sizes, runs, groups), in_specs=[ANY...  73.7 us
    pallas_call x1, Pallas kernels, body(): pl.pallas_call(partial(ffb_kernel, scaling), grid=(rows,), in_specs=[row_...  53.9 us
    pallas_call x1, Pallas kernels, body(): pl.pallas_call(partial(ffa_back_kernel, scaling), grid=(rows,), in_specs=...  43.2 us
    pallas_call x1, Pallas kernels, gather_first(): pl.pallas_call(gather_kernel, in_specs=[pl.BlockSpec(memory_space=pltpu.V...  41.7 us
    pallas_call x1, Pallas kernels, body(): pl.pallas_call(partial(mixer_back_kernel, scaling), grid=(rows,), in_spec...  32.7 us
    pallas_call x1, Pallas kernels, body(): pl.pallas_call(conv_forward_kernel, grid=(D // LANES,), in_specs=[group_s...  27.4 us
    pallas_call x1, Pallas kernels, body(): pl.pallas_call(mixer_out_kernel, grid=(rows,), in_specs=[row_spec(frames,...  24.2 us
    pallas_call x1, Pallas kernels, body(): pl.pallas_call(conv_back_kernel, grid=(D // LANES,), in_specs=[group_spec...  23.3 us

profile of v1, /device:TPU:0, one launch (start us, length us, event | category | flops | bytes accessed | tf_op | source)
XLA Modules:
  0.0 387.9 jit_solution(7126332534997841978)
XLA Ops:
  2.4 0.9 copy.61
  4.3 41.7 %gather_first.1 = (bf16[4,9,4,2,32,256]{5,4,3,2,1,0:T(8,128)(2,1)}, bf16[4,4,4,2,32,256]{5,4,3,2,1,0:T(8,128)(2,1)}, bf16[4,9,4,2,32,256]{5,4,3,2,1,0:T(8,128)(2,1)}, f32[4,264,128]{2,1,0:T(8,128)}) custom-call(f32[22,32,256]{2,1,0:T(8,128)} %master.3, f32[264,128]{1,0:T(8,128)} %pad_bitcast_fusion.1.pack), custom_call_target="tpu_custom_call" | custom-call | tf_op jit(solution)/shard_map/gather_first/pallas_call | solution.py:416
  46.0 1.2 copy.91
  48.1 1.7 copy.66.tab_a
  49.9 0.9 maximum_bitcast_fusion.tab_b
  52.0 1.1 broadcast_select_fusion
  53.2 0.9 exponential_convert_fusion
  54.1 22.7 %ffa_forward.1 = (f32[6,320,512]{2,1,0:T(8,128)}, bf16[6,320,2048]{2,1,0:T(8,128)(2,1)}, bf16[6,320,2048]{2,1,0:T(8,128)(2,1)}, bf16[6,320,512]{2,1,0:T(8,128)(2...) custom-call(bf16[6,320,512]{2,1,0:T(8,128)(2,1)} %feat.3, ...), custom_call_target="tpu_custom_call", output_to_operand_aliasing={{5}: (4, {})} | custom-call | tf_op jit(solution)/shard_map/ffa_forward/pallas_call | solution.py:1703
  76.9 1.1 broadcast_in_dim.123.power
  78.0 27.4 %conv_forward.1 = (f32[6,320,512]{2,1,0:T(8,128)}, bf16[4,6,32,512]{3,2,1,0:T(8,128)(2,1)}, bf16[4,9,4,2,32,256]{5,4,3,2,1,0:T(8,128)(2,1)}) custom-call(bf16[6,320,512]{2,1,0:T(8,128)(2,1)} %get-tuple-element.73.u, bf16[6,32,512]{2,1,0:T(8,128)(2,1)} %get-tuple-element.74.ends, ...), custom_call_target="tpu_custom_call", output_to_operand_aliasing={{2}: (7, {})} | custom-call | tf_op jit(solution)/shard_map/conv_forward/pallas_call | solution.py:1740
  105.9 0.7 pad_maximum_fusion.2.weigh
  106.6 0.9 exponential_convert_fusion.2
  108.8 0.9 reshape.423.starts
  109.7 24.2 %mixer_out.1 = (bf16[6,320,512]{2,1,0:T(8,128)(2,1)}, bf16[6,320,1024]{2,1,0:T(8,128)(2,1)}, f32[6,320,512]{2,1,0:T(8,128)}, bf16[6,320,1024]{2,1,0:T(8,128)(2,1...) custom-call(f32[6,320,512]{2,1,0:T(8,128)} %get-tuple-element.76.y, ...), custom_call_target="tpu_custom_call", output_to_operand_aliasing={{7}: (9, {})} | custom-call | tf_op jit(solution)/shard_map/mixer_out/pallas_call | solution.py:1762
  133.9 53.9 %ffb.1 = (bf16[6,320,512]{2,1,0:T(8,128)(2,1)}, f32[6,320,512]{2,1,0:T(8,128)}, bf16[6,320,512]{2,1,0:T(8,128)(2,1)}, bf16[36,256,256]{2,1,0:T(8,128)(2,1)}, f32...) custom-call(bf16[6,320,512]{2,1,0:T(8,128)(2,1)} %get-tuple-element.81.g, ...), custom_call_target="tpu_custom_call" | custom-call | tf_op jit(solution)/shard_map/ffb/pallas_call | solution.py:1816
  187.8 32.7 %mixer_back.1 = (f32[6,320,512]{2,1,0:T(8,128)}, bf16[6,320,512]{2,1,0:T(8,128)(2,1)}, bf16[6,32,512]{2,1,0:T(8,128)(2,1)}, bf16[16,256,256]{2,1,0:T(8,128)(2,1)...) custom-call(bf16[6,320,512]{2,1,0:T(8,128)(2,1)} %get-tuple-element.87.dq, ...), custom_call_target="tpu_custom_call" | custom-call | tf_op jit(solution)/shard_map/mixer_back/pallas_call | solution.py:1863
  220.6 23.3 %conv_back.1 = (f32[6,320,512]{2,1,0:T(8,128)}, f32[32,512]{1,0:T(8,128)}, f32[32,512]{1,0:T(8,128)}, f32[6,32,512]{2,1,0:T(8,128)}, f32[6,32,512]{2,1,0:T(8,128...) custom-call(bf16[6,320,512]{2,1,0:T(8,128)(2,1)} %get-tuple-element.73.u, ...), custom_call_target="tpu_custom_call" | custom-call | tf_op jit(solution)/shard_map/conv_back/pallas_call | solution.py:1923
  243.9 0.8 iota_multiply_fusion
  244.7 1.0 multiply_reduce_fusion
  245.9 1.0 pad_maximum_fusion.1.weigh
  246.9 43.2 %ffa_back.1 = (f32[6,320,512]{2,1,0:T(8,128)}, bf16[36,256,256]{2,1,0:T(8,128)(2,1)}, f32[2,8,512]{2,1,0:T(8,128)}, f32[4,32,512]{2,1,0:T(8,128)}, bf16[4,32,256...) custom-call(f32[6,320,512]{2,1,0:T(8,128)} %get-tuple-element.97.du_loc, bf16[4,6,32,512]{3,2,1,0:T(8,128)(2,1)} %get-tuple-element.98.back_all, ...), custom_call_target="tpu_custom_call" | custom-call | tf_op jit(solution)/shard_map/ffa_back/pallas_call | solution.py:1957
  290.1 1.0 fusion.5
  291.1 0.8 reduce_sum.87
  292.6 0.7 bitcast_bitcast_fusion.small
  293.3 73.7 %reduce_grads.1 = (bf16[22,2,2,2,32,256]{5,4,3,2,1,0:T(8,128)(2,1)}, bf16[22,32,256]{2,1,0:T(8,128)(2,1)}, f32[120,128]{1,0:T(8,128)}) custom-call(bf16[4,9,4,2,32,256]{5,4,3,2,1,0:T(8,128)(2,1)} %bitcast.84, bf16[4,32,256]{2,1,0:T(8,128)(2,1)} %get-tuple-element.108.share_pair, bf16[9,32,256]{2,1,0:T(8,128)(2,1)} %get-tuple-element.109.share_rest, ...), custom_call_target="tpu_custom_call" | custom-call | tf_op jit(solution)/shard_map/reduce_grads/pallas_call | solution.py:1550
  367.7 10.5 %shampoo.1 = (f32[22,32,256]{2,1,0:T(8,128)}, f32[22,32,256]{2,1,0:T(8,128)}, f32[22,32,256]{2,1,0:T(8,128)}, bf16[22,32,256]{2,1,0:T(8,128)(2,1)}, f32[22,32,256]{2,1,0:T(8,128)}) custom-call(bf16[32,256]{1,0:T(8,128)(2,1)} %fusion.7.pick, bf16[22,32,256]{2,1,0:T(8,128)(2,1)} %get-tuple-element.118.owned, bf16[22,256,256]{2,1,0:T(8,128)(2,1)} %bitcast.86, ...), custom_call_target="tpu_custom_call" | custom-call | tf_op jit(solution)/shard_map/shampoo/pallas_call | solution.py:2071
  380.5 1.3 multiply_subtract_fusion.2
  381.9 1.0 multiply_reduce_fusion.4
  383.0 0.8 multiply_reduce_fusion.3
  383.7 1.3 copy.98
  385.0 0.8 copy-done.2
  385.8 1.9 copy.99
  (102 shorter events, 10.5 us)
Async XLA Ops:
  0.6 0.9 copy-start
  0.7 2.7 copy-start.13
  51.4 25.4 %copy-start.4 = (f32[32,512]{1,0:T(8,128)}, f32[32,512]{1,0:T(8,128)S(1)}, u32[]{:S(2)}) copy-start(f32[32,512]{1,0:T(8,128)S(1)} %fusion.15.coup) | copy-start | bytes 196612
  246.8 43.2 %copy-start.7 = (f32[32,512]{1,0:T(8,128)S(1)}, f32[32,512]{1,0:T(8,128)}, u32[]{:S(2)}) copy-start(f32[32,512]{1,0:T(8,128)} %get-tuple-element.114) | copy-start | bytes 196612
  246.8 43.2 %copy-start.8 = (f32[32,512]{1,0:T(8,128)S(1)}, f32[32,512]{1,0:T(8,128)}, u32[]{:S(2)}) copy-start(f32[32,512]{1,0:T(8,128)} %get-tuple-element.117) | copy-start | bytes 196612
  246.9 45.0 %copy-start.12 = (f32[8,512]{1,0:T(8,128)S(1)}, f32[8,512]{1,0:T(8,128)}, u32[]{:S(2)}) copy-start(f32[8,512]{1,0:T(8,128)} %get-tuple-element.111) | copy-start | bytes 49156
  246.9 45.0 %copy-start.10 = (f32[2,8,512]{2,1,0:T(8,128)S(1)}, f32[2,8,512]{2,1,0:T(8,128)}, u32[]{:S(2)}) copy-start(f32[2,8,512]{2,1,0:T(8,128)} %get-tuple-element.112) | copy-start | bytes 98308
  246.9 45.1 %copy-start.11 = (f32[16,512]{1,0:T(8,128)S(1)}, f32[16,512]{1,0:T(8,128)}, u32[]{:S(2)}) copy-start(f32[16,512]{1,0:T(8,128)} %get-tuple-element.113) | copy-start | bytes 98308
  367.7 10.5 %copy-start.9 = (f32[120,128]{1,0:T(8,128)S(1)}, f32[120,128]{1,0:T(8,128)}, u32[]{:S(2)}) copy-start(f32[120,128]{1,0:T(8,128)} %get-tuple-element.125) | copy-start | bytes 184324
  367.7 12.2 %copy-start.5 = (f32[2,128,32]{1,2,0:T(8,128)S(1)}, f32[2,128,32]{1,2,0:T(8,128)}, u32[]{:S(2)}) copy-start(f32[2,128,32]{1,2,0:T(8,128)} %param.23) | copy-start | bytes 98308
  367.7 15.2 %copy-start.14 = (s32[6]{0:T(128)S(1)}, s32[6]{0:T(128)}, u32[]{:S(2)}) copy-start(s32[6]{0:T(128)} %param.15) | copy-start | bytes 76
  367.7 16.0 %copy-start.3 = (bf16[6,320,512]{2,1,0:T(8,128)(2,1)S(1)}, bf16[6,320,512]{2,1,0:T(8,128)(2,1)}, u32[]{:S(2)}) copy-start(bf16[6,320,512]{2,1,0:T(8,128)(2,1)} %get-tuple-element.210) | copy-start | bytes 5898244
  379.9 5.1 %copy-start.6 = (f32[64,128]{1,0:T(8,128)}, f32[64,128]{1,0:T(8,128)S(1)}, u32[]{:S(2)}) copy-start(f32[64,128]{1,0:T(8,128)S(1)} %slice.58) | copy-start | bytes 98308
  383.0 2.9 copy-start.2
  383.7 4.0 %copy-start.1 = (f32[6,128,32]{1,2,0:T(8,128)S(1)}, f32[6,128,32]{1,2,0:T(8,128)}, u32[]{:S(2)}) copy-start(f32[6,128,32]{1,2,0:T(8,128)} %param.14) | copy-start | bytes 294916

commit v2 on v1

--- a/solution.py
+++ b/solution.py
@@ -126,15 +126,82 @@
     return (jnp.concatenate([v] * HEADS, axis=0) * mask).astype(bf16)
 
 
+def join_lanes(ref):
+    return jnp.concatenate([ref[i] for i in range(ref.shape[0])], axis=1)
+
+
+def rate_rows(logs):
+    own = logs.shape[2] // HALF
+    places = range(logs.shape[0])
+    return [jnp.exp(logs[p, j : j + 1, 0:NST]) for p in places for j in range(own)]
+
+
+def as_column(row):
+    down = lax.broadcasted_iota(jnp.int32, (NST, NST), 0)
+    across = lax.broadcasted_iota(jnp.int32, (NST, NST), 1)
+    return jnp.sum(jnp.where(down == across, row, 0.0), axis=1, keepdims=True)
+
+
+def channel_rates(logs):
+    first = lax.broadcasted_iota(jnp.int32, (NST, LANES), 1) < HALF
+    columns = [as_column(row) for row in rate_rows(logs)]
+    pairs = zip(columns[0::2], columns[1::2])
+    return jnp.concatenate([jnp.where(first, a, b) for a, b in pairs], axis=1)
+
+
+def frame_decay(logs, table, to_end):
+    frames = table.shape[0]
+    rates = jnp.concatenate(rate_rows(logs), axis=1)
+    time = lax.broadcasted_iota(jnp.int32, table.shape, 0)
+    length = frames - 1 - time if to_end else time + 1
+    table[...] = jnp.exp(-rates * length.astype(f32)).astype(bf16)
+
+
+def passing(rates, apart, frames):
+    length = (apart * frames).astype(f32)
+    weight = jnp.where(apart >= 0, jnp.exp(-rates * jnp.maximum(length, 0.0)), 0.0)
+    return weight, weight * length
+
+
 def local_states(table, v, out):
-    frames = table.shape[1]
+    frames = table.shape[0]
     first = lax.broadcasted_iota(jnp.int32, (NST, LANES), 1) < HALF
     for b in range(out.shape[0]):
-        for g in range(D // LANES):
-            here = v[b * frames : (b + 1) * frames, g * LANES : (g + 1) * LANES]
-            both = mm(table[pl.ds(2 * NST * g, 2 * NST), :], here)
-            picked = jnp.where(first, both[:NST], both[NST:])
-            out[b, :, pl.ds(g * LANES, LANES)] = picked.astype(out.dtype)
+        for q in range(D // (2 * LANES)):
+            here = v[b * frames : (b + 1) * frames, 2 * q * LANES : 2 * (q + 1) * LANES]
+            four = mm_tn(table[:, q * LANES : (q + 1) * LANES], here)
+            for i in range(2):
+                both = four[2 * i * NST : 2 * (i + 1) * NST, i * LANES : (i + 1) * LANES]
+                picked = jnp.where(first, both[:NST], both[NST:])
+                out[b, :, pl.ds((2 * q + i) * LANES, LANES)] = picked.astype(out.dtype)
+
+
+def chunk_tables(row):
+    column = as_column(row)
+    span = GROUP * SUB
+    time = lax.broadcasted_iota(jnp.int32, (NST, span), 1)
+    since = (time % SUB + 1).astype(f32)
+    into, into_w, out, out_w, power = [], [], [], [], []
+    for i in range(GROUP):
+        age = SUB * (i + 1) - 1 - time
+        age_f = jnp.maximum(age, 0).astype(f32)
+        value = jnp.where(age >= 0, jnp.exp(-column * age_f), 0.0)
+        into.append(value)
+        into_w.append(value * age_f)
+        value = jnp.where(time // SUB == i, jnp.exp(-column * since), 0.0)
+        out.append(value)
+        out_w.append(value * since)
+        power.append(jnp.exp(-column * float(SUB * (i + 1))))
+    join = lambda parts: jnp.concatenate(parts, axis=0).astype(bf16)
+    return join(into), join(into_w), join(out), join(out_w), power
+
+
+def lag_taps(rates, coup, taps, backward):
+    place = lax.broadcasted_iota(jnp.int32, (SUB, LANES), 0)
+    for d in range(SUB):
+        lag = jnp.sum(coup * jnp.exp(-rates * float(d)), axis=0, keepdims=True)
+        inside = place + d < SUB if backward else place >= d
+        taps[d] = jnp.where(inside, lag, 0.0)
 
 
 ANY = pl.BlockSpec(memory_space=pl.ANY)
@@ -326,8 +393,8 @@
 
 
 def gather_kernel(
-    master, pack, first, pair, rest, pack_all,
-    rounded, piece, piece_pair, piece_rest, run_send, run_recv, pk_send, pk_recv, *sems,
+    source, master, bank, mix_terms, logs, first, pair, rest, pack_all,
+    pack, rounded, piece, piece_pair, piece_rest, run_send, run_recv, pk_send, pk_recv, *sems,
 ):
     place, level, core = peers()
     others = square(place)
@@ -335,6 +402,13 @@
     greet([at(other, level, core) for other in others] + [at(place, level, 1 - core)])
     greet([at(place, (level + d) % levels, core) for d in range(1, levels)])
     rounded[...] = master[...].astype(bf16)
+    count = bank.shape[0]
+    for i in range(count):
+        pack[i * NST : (i + 1) * NST] = bank[source[i]]
+    for i in range(2):
+        pack[(count + i) * NST : (count + i + 1) * NST] = mix_terms[i]
+    pack[(count + 2) * NST :] = jnp.zeros((8, pack.shape[1]), f32)
+    pack[(count + 2) * NST : (count + 2) * NST + logs.shape[0], 0:NST] = logs[...]
     met(3 + levels)
     moves = []
     for ids, target in zip(block_sets(), (piece, piece_pair, piece_rest)):
@@ -407,23 +481,26 @@
         copy.wait()
 
 
-def gather_first(master, pack, parts, devices, chunks=3):
+def gather_first(master, bank, mix_terms, logs, source, parts, devices, chunks=3):
     count, slab, cols = master.shape
     levels = devices // 2
     each = [len(ids) // parts for ids in block_sets()]
     runs = sum(len(move_runs(ids, parts, count)) for ids in block_sets())
     dma = lambda *dims: pltpu.SemaphoreType.DMA(dims)
+    pack = ((bank.shape[0] + 2) * NST + 8, bank.shape[2])
     return pl.pallas_call(
         gather_kernel,
-        in_specs=[pl.BlockSpec(memory_space=pltpu.VMEM), ANY],
+        in_specs=[pl.BlockSpec(memory_space=pltpu.SMEM)]
+        + [pl.BlockSpec(memory_space=pltpu.VMEM)] * 4,
         out_specs=[ANY] * 4,
         out_shape=[
             shape((parts, each[0], levels, 2, slab, cols), bf16),
             shape((parts, each[1], levels, 2, slab, cols), bf16),
             shape((parts, each[2], levels, 2, slab, cols), bf16),
-            shape((parts,) + pack.shape, pack.dtype),
+            shape((parts,) + pack),
         ],
         scratch_shapes=[
+            vm(*pack),
             vm(count, slab, cols, dtype=bf16),
             vm(each[0], slab, cols, dtype=bf16),
             vm(each[1], slab, cols, dtype=bf16),
@@ -439,7 +516,7 @@
             collective_id=1, has_side_effects=True, vmem_limit_bytes=VMEM_BYTES
         ),
         name="gather_first",
-    )(master, pack)
+    )(source, master, bank, mix_terms, logs)
 
 
 R_XY = ("load", "cs", "cr", "xs", "xr", "ys", "yr")
@@ -608,14 +685,14 @@
         self.far(c).wait_send()
 
 
-def ffa_forward_kernel(feat, small, stack, mfin, *refs):
+def ffa_forward_kernel(feat, small, stack, logs, *refs):
     step, last = pl.program_id(0), pl.num_programs(0) - 1
     pair = None
-    if len(refs) > 9:
-        refs, sems = refs[1:7] + refs[7:11], refs[11:]
+    if len(refs) > 10:
+        refs, sems = refs[1:12], refs[12:]
         pair = Gather(None, refs[5], dict(zip(XY_SEMS, sems)))
         refs = refs[:5] + refs[6:]
-    x1_o, inner_o, act_o, u_o, f_o, wi, wo, wu, sem = refs
+    x1_o, inner_o, act_o, u_o, f_o, wi, wo, wu, table, sem = refs
 
     @pl.when(step == 0)
     def _():
@@ -628,6 +705,7 @@
         if pair is not None:
             met(4)
             pair.spread(0)
+        frame_decay(logs, table, True)
 
     x0 = flat(feat).astype(f32)
     hat, unused = norm(x0)
@@ -640,7 +718,7 @@
     hat, unused = norm(x1)
     u = mm((hat * small[1:2]).astype(bf16), wu[...]).astype(bf16)
     put_rows(u_o, u)
-    local_states(mfin, u, f_o)
+    local_states(table, u, f_o)
     if pair is not None:
         pl.when(step == last - 1)(lambda: pair.forward(0))
 
@@ -681,7 +759,7 @@
     )
 
 
-def swap_states(mine, whole, first_step, last_step, own_sem, send, recv, pair=None):
+def swap_states(mine, whole, first_step, last_step, own_sem, send, recv, rest=None):
     place, level, core = peers()
     parts = whole.shape[0]
     others = [(place + d) % parts for d in range(1, parts)]
@@ -696,70 +774,68 @@
 
     @pl.when(first_step)
     def _():
-        barrier = pltpu.get_barrier_semaphore()
-        for other in others:
-            signal(barrier, at(other, level, core))
-        if pair is not None:
-            signal(barrier, at(place, level, 1 - core))
+        greet([at(other, level, core) for other in others])
+        if rest is not None:
+            greet([at(place, level, 1 - core)])
         own().start()
 
-    def end():
+    def begin():
         @pl.when(first_step)
         def _():
-            met(parts - 1 + (pair is not None))
+            met(parts - 1 + (rest is not None))
             for copy in copies():
                 copy.start()
-            if pair is not None:
-                pair.spread(0)
-
-        if pair is not None:
-            step = pl.program_id(0)
-
-            @pl.when(step == pl.num_programs(0) - 2)
-            def _():
-                pair.forward(0)
-
-            @pl.when(last_step)
-            def _():
-                pair.finish(0)
-                pair.end(0)
+            if rest is not None:
+                rest.spread(0)
+
+    def end():
+        if rest is not None:
+            pl.when(pl.program_id(0) == pl.num_programs(0) - 2)(lambda: rest.forward(0))
 
         @pl.when(last_step)
         def _():
+            if rest is not None:
+                rest.finish(0)
+                rest.end(0)
             own().wait()
             for copy in copies():
                 copy.wait()
 
-    return end
+    return begin, end
 
 
 def tile_lanes(v, width):
     return jnp.concatenate([v] * (width // LANES), axis=1)
 
 
-def conv_forward_kernel(u, ends, tab_a, tab_b, power, coup, taps, *refs):
+def conv_forward_kernel(u, ends, logs, mix_one, mix_two, *refs):
     step = pl.program_id(0)
     pair = None
-    if len(refs) > 6:
-        refs, sems = refs[1:7] + refs[7:8], refs[8:]
+    if len(refs) > 7:
+        refs, sems = refs[1:9], refs[9:]
         pair = Gather(None, refs[2], dict(zip(XY_SEMS, sems)), 2)
         refs = refs[:2] + refs[3:]
-    y_o, ends_all, pad, own_sem, send, recv = refs
-    end_swap = swap_states(
+    y_o, ends_all, pad, taps, own_sem, send, recv = refs
+    begin_swap, end_swap = swap_states(
         ends, ends_all, step == 0, step == pl.num_programs(0) - 1, own_sem, send, recv, pair
     )
     rows, frames = u.shape[0], u.shape[1]
     span = GROUP * SUB
-    coup_both = pack_params(coup[...], rows)
+    coup = join_lanes(mix_one) * join_lanes(mix_two)
+    lag_taps(channel_rates(logs), coup, taps, False)
+    coup_both = pack_params(coup, rows)
+    heads = rate_rows(logs)
     packed = pack_heads(u, rows)
     width = packed[0].shape[1]
+    begin_swap()
     results = []
     for h in range(2):
-        scale = [tile_lanes(power[h, i], width) for i in range(GROUP)]
+        into, unused, out, unused, power = chunk_tables(heads[h])
+        scale = [jnp.broadcast_to(v, (NST, width)) for v in power]
         carry = None
         outs = []
         for g in range(frames // span):
-            local = mm(tab_a[h, 0], packed[h][g * span : (g + 1) * span])
+            local = mm(into, packed[h][g * span : (g + 1) * span])
             parts = [local[i * NST : (i + 1) * NST] for i in range(GROUP)]
             if carry is None:
                 states = [jnp.zeros_like(parts[0])] + parts[:-1]
@@ -768,7 +844,7 @@
                 states = [carry] + [parts[i] + scale[i] * carry for i in range(GROUP - 1)]
                 carry = parts[-1] + scale[-1] * carry
             scaled = jnp.concatenate([v * coup_both[h] for v in states], axis=0)
-            outs.append(mm(tab_b[h, 1], scaled.astype(bf16)))
+            outs.append(mm_tn(out, scaled.astype(bf16)))
         results.append(jnp.concatenate(outs, axis=0))
     for p in range(rows // 2):
         one, two = unpack_pair(results[0], results[1], p)
@@ -817,9 +893,6 @@
         if rest is None:
             pl.when(not_last)(lambda: greet([at(after, level, core)]))
             pl.when(not_first)(lambda: greet([at(before, level, core)]))
-        else:
-            greet([at(other, level, core) for other in square(place)])
-            greet([at(place, level, 1 - core)])
         zeros[...] = jnp.zeros_like(zeros)
 
         @pl.when(place == 0)
@@ -837,9 +910,8 @@
         def _():
             below = (place + parts - 1) // parts
             above = (2 * parts - 2 - place) // parts
-            met(below + above if rest is None else parts)
-            if rest is not None:
-                rest.spread(1)
+            if rest is None:
+                met(below + above)
 
         if rest is not None:
             pl.when(step == steps // per // 2)(lambda: rest.forward(1))
@@ -878,29 +950,45 @@
 
 
 def mixer_out_kernel(
-    y, ends_all, starts, weigh, coup, x1, small, stack, pfull, *refs
+    y, ends_all, starts, mix_one, mix_two, logs, x1, small, stack, *refs
 ):
     step = pl.program_id(0)
     rest = None
-    if len(refs) > 16:
-        refs, sems = refs[1:8] + refs[8:18], refs[18:]
+    if len(refs) > 19:
+        refs, sems = refs[1:21], refs[21:]
         rest = Gather(None, refs[7], dict(zip(XY_SEMS, sems)), 2)
         refs = refs[:7] + refs[8:]
     ys_o, gated_o, x2_o, pw_o, g_o, low_o, high_o, wo, wp, mask, sem = refs[:11]
-    edges, zeros, send, recv, zero_sem = refs[11:]
+    table, weigh, coup, edges, zeros, send, recv, zero_sem = refs[11:]
+    parts = ends_all.shape[0]
     put = edge_sender(edges, low_o, high_o, zeros, send, recv, zero_sem, step, 1, rest)
 
     @pl.when(step == 0)
     def _():
         ffn, mix = D // BS * (FF // BS), (D // BS) ** 2
+        if rest is not None:
+            greet([at(other, rest.level, rest.core) for other in (rest.xp, rest.yp, rest.dp)])
+            greet([at(rest.place, rest.level, 1 - rest.core)])
         load_matrices(stack, ((0, wo), (2 * mix, wp)), sem)
+        if rest is not None:
+            met(4)
+            rest.spread(1)
         mask[...] = head_mask()
+        place = lax.axis_index("tm")
+        frames = table.shape[0]
+        frame_decay(logs, table, False)
+        rates = channel_rates(logs)
+        for i in range(parts):
+            weigh[i], unused = passing(rates, place - 1 - i, frames)
+        two = join_lanes(mix_two)
+        weigh[parts] = two * passing(rates, place, frames)[0]
+        coup[...] = join_lanes(mix_one) * two
 
     came = weigh[0] * ends_all[0, 0].astype(f32)
-    for i in range(1, ends_all.shape[0]):
+    for i in range(1, parts):
         came = came + weigh[i] * ends_all[i, 0].astype(f32)
-    zin = coup[...] * came + weigh[ends_all.shape[0]] * starts[0]
-    ys = (y[0] + mm(pfull[...], spread_heads(zin, mask[...]))).astype(bf16)
+    zin = coup[...] * came + weigh[parts] * join_lanes(starts)
+    ys = (y[0] + mm(table[...], spread_heads(zin, mask[...]))).astype(bf16)
     ys_o[0] = ys
     gated = mm(ys, wo[...])
     gated_o[0] = gated.astype(bf16)
@@ -1007,19 +1095,19 @@
 
 
 def mixer_back_kernel(
-    scale, dq, dlow, dhigh, g, glow, ghigh, pw, x2, gated, ys, dx3, small, stack, pfull_t, *refs
+    scale, dq, dlow, dhigh, g, glow, ghigh, pw, x2, gated, ys, dx3, small, stack, logs, *refs
 ):
     step, last = pl.program_id(0), pl.num_programs(0) - 1
     frames = dq.shape[1]
     rest = None
-    if len(refs) > 20:
+    if len(refs) > 21:
         grads_rest, refs = refs[0], refs[1:]
-        red, bufs, sems = refs[6], refs[21:25], refs[25:]
+        red, bufs, sems = refs[6], refs[22:26], refs[26:]
         half = (red.shape[0] + 1) // 2
         rest = Reduce((half, red.shape[0] - half), dict(zip(R_XY, sems)), grads_rest, bufs, red)
-        refs = refs[:6] + refs[7:21]
+        refs = refs[:6] + refs[7:22]
     dx2_o, dy_o, gst_o, grads, gain_o, dk_o, wo, wp, acc_p, acc_o, dpad, gpad = refs[:12]
-    dg_s, dk_s, stage, k_n, k_dpw, k_ys, k_dg, sem = refs[12:]
+    dg_s, dk_s, stage, k_n, k_dpw, k_ys, k_dg, table, sem = refs[12:]
 
     @pl.when(step == 0)
     def _():
@@ -1032,6 +1120,7 @@
             met(4)
             for c in rest.all:
                 rest.start(c)
+        frame_decay(logs, table, False)
         acc_p[...] = jnp.zeros_like(acc_p)
         acc_o[...] = jnp.zeros_like(acc_o)
         gain_o[...] = jnp.zeros_like(gain_o)
@@ -1075,7 +1164,7 @@
     k_dg[keep] = dgated
     dy = mm_nt(dgated, wo[...]).astype(bf16)
     dy_o[0] = dy
-    local_states(pfull_t, dy, gst_o)
+    local_states(table, dy, gst_o)
 
     if rest is not None:
         for c in rest.all:
@@ -1101,31 +1190,36 @@
 
 
 def conv_back_kernel(
-    u, dy, back_ends, tab_a, tab_b, power, coup, taps,
-    du_o, t1_o, t2_o, fp_o, gp_o, dk_o, back_all,
-    upad, dpad, acc_s, own_sem, send, recv,
+    u, dy, back_ends, logs, mix_one, mix_two,
+    du_o, t1_o, t2_o, fp_o, gp_o, back_all,
+    upad, dpad, acc_s, taps, own_sem, send, recv,
 ):
     step = pl.program_id(0)
-    end_swap = swap_states(
+    begin_swap, end_swap = swap_states(
         back_ends, back_all, step == 0, step == pl.num_programs(0) - 1, own_sem, send, recv
     )
     rows, frames = u.shape[0], u.shape[1]
     span = GROUP * SUB
-    coup_both = pack_params(coup[...], rows)
+    coup = join_lanes(mix_one) * join_lanes(mix_two)
+    rates = channel_rates(logs)
+    lag_taps(rates, coup, taps, True)
+    coup_both = pack_params(coup, rows)
+    heads = rate_rows(logs)
     u_both = pack_heads(u, rows)
     d_both = pack_heads(dy, rows)
     width = u_both[0].shape[1]
     du, first_sum, second_sum, end_u, end_d = [], [], [], [], []
     for h in range(2):
-        scale = [tile_lanes(power[h, i], width) for i in range(GROUP)]
+        into, into_w, out, out_w, power = chunk_tables(heads[h])
+        scale = [jnp.broadcast_to(v, (NST, width)) for v in power]
         aged = [scale[i] * float(SUB * (i + 1)) for i in range(GROUP)]
         zero = jnp.zeros((NST, width), f32)
         carry, carry_w = zero, zero
         states, states_w = [], []
         for g in range(frames // span):
             here = u_both[h][g * span : (g + 1) * span]
-            local = mm(tab_a[h, 0], here)
-            local_w = mm(tab_a[h, 1], here)
+            local = mm(into, here)
+            local_w = mm(into_w, here)
             parts = [local[i * NST : (i + 1) * NST] for i in range(GROUP)]
             parts_w = [local_w[i * NST : (i + 1) * NST] for i in range(GROUP)]
             states.append([carry] + [parts[i] + scale[i] * carry for i in range(GROUP - 1)])
@@ -1141,12 +1235,12 @@
         outs = []
         for g in reversed(range(frames // span)):
             here = d_both[h][g * span : (g + 1) * span]
-            back = mm(tab_a[h, 2], here)
-            back_w = mm(tab_a[h, 3], here)
+            back = mm(out, here)
+            back_w = mm(out_w, here)
             parts = [back[i * NST : (i + 1) * NST] for i in range(GROUP)]
             parts_w = [back_w[i * NST : (i + 1) * NST] for i in range(GROUP)]
-            into = jnp.concatenate([v * coup_both[h] for v in parts[1:] + [later]], axis=0)
-            outs.append(mm(tab_b[h, 0], into.astype(bf16)))
+            grads = jnp.concatenate([v * coup_both[h] for v in parts[1:] + [later]], axis=0)
+            outs.append(mm_tn(into, grads.astype(bf16)))
             for i in range(GROUP):
                 one = one + parts[i] * states[g][i]
                 two = two + (parts_w[i] * states[g][i] + parts[i] * states_w[g][i])
@@ -1195,24 +1289,31 @@
 
     lax.fori_loop(0, rows, one_row, 0)
     spot = lax.broadcasted_iota(jnp.int32, (SUB, LANES), 0)
+    one, two = t1_o[...], t2_o[...]
     for d in range(SUB):
         kept = jnp.where(spot >= d, acc_s[d], 0.0)
-        dk_o[d : d + 1] = jnp.sum(kept, axis=0, keepdims=True)
+        grad = jnp.exp(-rates * float(d)) * jnp.sum(kept, axis=0, keepdims=True)
+        one = one + grad
+        two = two + float(d) * grad
+    t1_o[...] = one
+    t2_o[...] = two
+    begin_swap()
     end_swap()
 
 
 def ffa_back_kernel(
-    scale, du_loc, back_all, ends_all, back_ends, ends_w, back_w, starts, weigh, coup,
-    x1, feat, inner_r, act_r, dx2, small, stack, mfin_t, *refs
+    scale, du_loc, back_all, ends_all, back_ends, ends_w, back_w, starts, mix_one, mix_two, logs,
+    t_one, t_two, gain_b, gain_c, kernel_grads,
+    x1, feat, inner_r, act_r, dx2, small, stack, *refs
 ):
     step, last = pl.program_id(0), pl.num_programs(0) - 1
     pair = None
-    if len(refs) > 19:
+    if len(refs) > 23:
         grads_pair, red_in, refs = refs[0], refs[1], refs[2:]
-        out_pair, out_rest = refs[4:6]
-        red_rest, rest_bufs, red_pair, square_refs = refs[21], refs[22:24], refs[24], refs[25:29]
-        pair_bufs, sems = refs[29:31], refs[31:]
-        refs = refs[:4] + refs[6:21]
+        out_pair, out_rest = refs[3:5]
+        red_rest, rest_bufs, red_pair, square_refs = refs[25], refs[26:28], refs[28], refs[29:33]
+        pair_bufs, sems = refs[33:35], refs[35:]
+        refs = refs[:3] + refs[5:25]
         pair = Reduce(
             out_pair.shape[:1], dict(zip(R_XY + R_Z, sems)), grads_pair, square_refs, red_pair,
             pair_bufs, out_pair,
@@ -1220,8 +1321,10 @@
         rest = Reduce(
             out_rest.shape[:1], dict(zip(R_Z, sems[9:])), None, None, red_rest, rest_bufs, out_rest
         )
-    dx0_o, grads, gain_o, sums_o, wi, wo, wu, acc_in, acc_out, acc_u = refs[:10]
-    mask, stage, k_act, k_din, k_n, k_dp, k_m, k_du, sem = refs[10:]
+    dx0_o, grads, small_o, wi, wo, wu, acc_in, acc_out, acc_u = refs[:9]
+    mask, stage, k_act, k_din, k_n, k_dp, k_m, k_du, sem = refs[9:18]
+    gain_o, sums_o, table, weigh, coup = refs[18:]
+    place, parts = lax.axis_index("tm"), ends_all.shape[0]
 
     @pl.when(step == 0)
     def _():
@@ -1237,6 +1340,13 @@
             pair.start(0)
             rest.near(0).start()
         mask[...] = head_mask()
+        frames = table.shape[0]
+        frame_decay(logs, table, True)
+        rates = channel_rates(logs)
+        for i in range(parts):
+            weigh[0, i], weigh[1, i] = passing(rates, place - 1 - i, frames)
+            weigh[2, i], unused = passing(rates, i - place - 1, frames)
+        coup[...] = join_lanes(mix_one) * join_lanes(mix_two)
         acc_in[...] = jnp.zeros_like(acc_in)
         acc_out[...] = jnp.zeros_like(acc_out)
         acc_u[...] = jnp.zeros_like(acc_u)
@@ -1246,7 +1356,6 @@
     frames = feat.shape[1]
     group = k_n.shape[0] // frames
     keep = pl.ds(pl.multiple_of(step % group * frames, frames), frames)
-    parts = ends_all.shape[0]
     came, came_w, later = 0.0, 0.0, 0.0
     for i in range(parts):
         end = ends_all[i, 0].astype(f32)
@@ -1254,11 +1363,12 @@
         came_w = came_w + weigh[1, i] * end
         later = later + weigh[2, i] * back_all[i, 0].astype(f32)
     mine = back_ends[0].astype(f32)
+    start = join_lanes(starts)
     sums_o[0] += mine * came
-    sums_o[1] += starts[0] * mine
-    sums_o[2] += starts[0] * back_w[0]
+    sums_o[1] += start * mine
+    sums_o[2] += start * back_w[0]
     sums_o[3] += back_w[0] * came + mine * came_w + later * ends_w[0]
-    du = (du_loc[0] + mm(mfin_t[...], spread_heads(coup[...] * later, mask[...]))).astype(bf16)
+    du = (du_loc[0] + mm(table[...], spread_heads(coup[...] * later, mask[...]))).astype(bf16)
     hat1, inv1 = norm(x1[0])
     n1 = (hat1 * small[1:2]).astype(bf16)
     k_m[keep] = n1
@@ -1314,6 +1424,27 @@
     @pl.when(step == pl.num_programs(0) - 1)
     def _():
         ffn, mix = D // BS * (FF // BS), (D // BS) ** 2
+        one, two = join_lanes(mix_one), join_lanes(mix_two)
+        begin = (place * frames).astype(f32)
+        begin_w = jnp.exp(-channel_rates(logs) * begin)
+        d_coup = t_one[...] + sums_o[0]
+        start_back = sums_o[1] * begin_w
+        d_rate = coup[...] * (t_two[...] + sums_o[3])
+        d_rate = d_rate + two * (begin * start_back + begin_w * sums_o[2])
+        total = lambda v: jnp.sum(v, axis=0, keepdims=True)
+        gains = [total(gain_o[0]), total(gain_o[1]), total(gain_c[...])]
+        gains += [total(gain_b[0]), total(gain_b[1]), kernel_grads[0:KW]]
+        entries = gains + [d_coup * two, d_coup * one + start_back, d_rate]
+        own = small_o.shape[2]
+        small_o[...] = jnp.zeros_like(small_o)
+        row = 0
+        for entry in entries:
+            count = entry.shape[0]
+            if count == NST:
+                row = -(-row // 8) * 8
+            for p in range(parts):
+                small_o[p, row : row + count] = entry[:, p * own : (p + 1) * own] * scale
+            row += count
         plan = ((acc_in, 0, False), (acc_out, ffn, True), (acc_u, 2 * ffn, False))
         store_blocks(plan, scale, grads, stage, sem)
         if pair is not None:
@@ -1324,14 +1455,70 @@
 
 
 def shampoo_kernel(
-    pick, owned, full, left, right, lroot, rroot, master, nl_o, nr_o, nm_o, nc_o, own_o
+    frames, source, owned, full, left, right, lroot, rroot, master, sums, small, logs, mix_terms,
+    back_all, result, slope, nl_o, nr_o, nm_o, nc_o, own_o,
+    small_o, new_small_o, decay_o, mix_o, new_decay_o, new_mix_o, state_o, result_o, slope_o,
 ):
+    step = pl.program_id(0)
+    result_o[...] = result[...]
+    slope_o[...] = slope[...]
+
+    @pl.when(step == 0)
+    def _():
+        place = lax.axis_index("tm")
+        parts, rows, width = back_all.shape[0], back_all.shape[1], state_o.shape[2]
+        columns = [as_column(jnp.exp(logs[j : j + 1])) for j in range(logs.shape[0])]
+        over = [jnp.broadcast_to(column, (NST, HALF)) for column in columns]
+        rates = jnp.concatenate(over, axis=1)
+        decays = [jnp.exp(-rates * float(frames * i)) * mix_terms[1] for i in range(parts)]
+        grads = []
+        for r in range(rows):
+            grad = 0.0
+            for p in range(parts):
+                total = 0.0
+                for i in range(parts):
+                    part = back_all[i, r, :, p * width : (p + 1) * width].astype(f32)
+                    total = total + part * decays[i]
+                grad = grad + jnp.where(place == p, total, 0.0)
+            grads.append(grad)
+        for r in range(rows):
+            total = 0.0
+            for i in range(rows):
+                total = total + jnp.where(source[i] == r, grads[i], 0.0)
+            state_o[r] = total
+
+    @pl.when(step == 0)
+    def _():
+        count = small_o.shape[0]
+        grad = sums[0:count]
+        small_o[...] = grad
+        width = small_o.shape[1]
+        own_small = 0.0
+        for p in range(small.shape[1] // width):
+            part = small[:, p * width : (p + 1) * width]
+            own_small = own_small + jnp.where(lax.axis_index("tm") == p, part, 0.0)
+        new_small_o[...] = own_small - rate_small * grad
+        row = -(-count // 8) * 8
+        for i in range(2):
+            grad = sums[row + i * NST : row + (i + 1) * NST]
+            mix_o[i] = grad
+            new_mix_o[i] = mix_terms[i] - rate_small * grad
+        by_channel = sums[row + 2 * NST : row + 3 * NST].T
+        for j in range(logs.shape[0]):
+            here = jnp.sum(by_channel[j * HALF : (j + 1) * HALF], axis=0, keepdims=True)
+            grad = -here * jnp.exp(logs[j : j + 1])
+            decay_o[j : j + 1] = grad
+            new_decay_o[j : j + 1] = logs[j : j + 1] - rate_small * grad
+
+    slab = owned.shape[1]
+    down = lax.broadcasted_iota(jnp.int32, (slab, BS), 0) + lax.axis_index("rows") * slab
+    pick = (down == lax.broadcasted_iota(jnp.int32, (slab, BS), 1)).astype(f32).astype(bf16)
     for i in range(full.shape[0]):
         whole = full[i]
         mine = owned[i]
         own_o[i] = mine.astype(f32)
         nl_o[i] = 0.5 * left[i] + 0.5 * mm_nt(mine, whole)
-        columns = mm_nt(pick[...], whole).astype(bf16)
+        columns = mm_nt(pick, whole).astype(bf16)
         nr_o[i] = 0.5 * right[i] + 0.5 * mm(columns, whole)
         side = mm(lroot[i].astype(bf16), whole)
         step = mm(side.astype(bf16), rroot[i].astype(bf16))
@@ -1610,19 +1797,15 @@
     ffn, mix = D // BS * (FF // BS), (D // BS) ** 2
 
     own_heads, own_channels = decay_logs.shape[0], state_mix.shape[1]
-    starts_own = state_bank[state_source]
-    params = jnp.concatenate(
-        [decay_logs.reshape(-1), state_mix.reshape(-1), starts_own.reshape(-1)]
-    )
-    cut_one = own_heads * NST
-    cut_two = cut_one + 2 * own_channels * NST
-    cut_three = cut_two + rows * own_channels * NST
-    params = jnp.pad(params, (0, -cut_three % (8 * LANES))).reshape(-1, LANES)
+    mix_t = state_mix.transpose(0, 2, 1)
+    bank_t = state_bank.transpose(0, 2, 1)
     devices = lax.axis_size("rows")
     levels = devices // 2
     spread_out = parts == 4
     if spread_out:
-        first, pair, rest, packed = gather_first(master, params, parts, devices)
+        first, pair, rest, packed = gather_first(
+            master, bank_t, mix_t, decay_logs, state_source, parts, devices
+        )
         first = first.reshape(-1, BS, BS)
         pair_out, rest_out = [shape(pair.shape, bf16)], [shape(rest.shape, bf16)]
         any_one, pair_in, rest_in = [ANY], [pair], [rest]
@@ -1630,68 +1813,22 @@
     else:
         stack = lax.all_gather(master.astype(bf16), "rows", axis=1, tiled=True)
         stack = lax.all_gather(stack, "tm", axis=0, tiled=True)
-        packed = lax.all_gather(params, "tm", axis=0)
+        logs_own = jnp.pad(decay_logs, ((0, 8 - own_heads), (0, own_channels - NST)))
+        params = [bank_t[state_source].reshape(-1, own_channels), mix_t.reshape(-1, own_channels)]
+        packed = lax.all_gather(jnp.concatenate(params + [logs_own], axis=0), "tm", axis=0)
         first, pair, rest = (stack[jnp.array(ids)] for ids in block_sets())
         pair_out = rest_out = any_one = pair_in = rest_in = pair_sems = rest_sems = []
 
-    packed = packed.reshape(parts, -1)
-    logs = packed[:, :cut_one].reshape(HEADS, NST)
-    mix_all = packed[:, cut_one:cut_two].reshape(parts, 2, own_channels, NST)
-    mix_all = mix_all.transpose(1, 3, 0, 2).reshape(2, NST, D)
-    starts = packed[:, cut_two:cut_three].reshape(parts, rows, own_channels, NST)
-    starts = starts.transpose(1, 3, 0, 2).reshape(rows, NST, D)
-
-    rates = jnp.exp(logs)
-    rate_nc = jnp.repeat(rates.T, HALF, axis=1)
-    coupling = mix_all[0] * mix_all[1]
-    state_row = jnp.arange(GROUP * NST, dtype=jnp.int32)
-    part_of = state_row // NST
-    rate_row = jnp.tile(rates, (1, GROUP))[:, :, None]
-    inner_t = jnp.arange(GROUP * SUB, dtype=jnp.int32)
-    age = SUB * (part_of + 1)[:, None] - 1 - inner_t[None, :]
-    age_f = jnp.maximum(age, 0).astype(f32)
-    tab_in = jnp.where(age >= 0, jnp.exp(-rate_row * age_f), 0.0)
-    since = (inner_t % SUB + 1).astype(f32)
-    inside = (inner_t // SUB)[None, :] == part_of[:, None]
-    tab_out = jnp.where(inside, jnp.exp(-rate_row * since), 0.0)
-    tab_a = jnp.stack([tab_in, tab_in * age_f, tab_out, tab_out * since], axis=1).astype(bf16)
-    tab_b = jnp.stack([tab_in, tab_out], axis=1).astype(bf16).transpose(0, 1, 3, 2)
-    steps_of = SUB * jnp.arange(1, GROUP + 1, dtype=f32)
-    power = jnp.exp(-rates[:, None, :, None] * steps_of[None, :, None, None])
-    power = jnp.broadcast_to(power, (HEADS, GROUP, NST, LANES))
-    time = jnp.arange(frames, dtype=jnp.int32)
-    flat_rates = rates.reshape(-1)
-    next_t = (time + 1).astype(f32)
-    left_t = (frames - 1 - time).astype(f32)
-    pfull = jnp.exp(-flat_rates[None, :] * next_t[:, None]).astype(bf16)
-    pfull_t = jnp.exp(-flat_rates[:, None] * next_t[None, :]).astype(bf16)
-    mfin = jnp.exp(-flat_rates[:, None] * left_t[None, :]).astype(bf16)
-    mfin_t = jnp.exp(-flat_rates[None, :] * left_t[:, None]).astype(bf16)
-    lag = jnp.arange(SUB, dtype=f32)
-    lag_decay = jnp.exp(-rate_nc[None] * lag[:, None, None])
-    kernel_lags = jnp.sum(coupling[None] * lag_decay, axis=1)
-    slot = jnp.arange(SUB, dtype=jnp.int32)
-    taps_f = jnp.where(slot[:, None, None] <= slot[None, :, None], kernel_lags[:, None, :], 0.0)
-    taps_b = jnp.where(
-        slot[:, None, None] + slot[None, :, None] < SUB, kernel_lags[:, None, :], 0.0
-    )
-
-    span = float(frames)
-    shard = jnp.arange(parts, dtype=jnp.int32)
-
-    def passing(apart):
-        length = jnp.maximum(apart, 0).astype(f32)[:, None, None] * span
-        weight = jnp.where(
-            (apart >= 0)[:, None, None], jnp.exp(-rate_nc[None] * length), 0.0
-        )
-        return weight, weight * length
-
-    behind_w, behind_l = passing(place - 1 - shard)
-    ahead_w, unused = passing(shard - place - 1)
-    begin = place.astype(f32) * span
-    begin_w = jnp.exp(-rate_nc * begin)
-    weigh_in = jnp.concatenate([behind_w, (mix_all[1] * begin_w)[None]], axis=0)
-    weigh_back = jnp.stack([behind_w, behind_l, ahead_w], axis=0)
+    mix_row = rows
+    logs_row = (rows + 2) * NST // 8
+    per_group = LANES // own_channels
+    wide = lambda at_row: pl.BlockSpec((parts, NST, own_channels), lambda i: (0, at_row, 0))
+    narrow = lambda at_row: pl.BlockSpec((per_group, NST, own_channels), lambda i: (i, at_row, 0))
+    starts_spec = pl.BlockSpec((parts, NST, own_channels), lambda i: (0, i, 0))
+    logs_spec = pl.BlockSpec((parts, 8, own_channels), lambda i: (0, logs_row, 0))
+    logs_part = pl.BlockSpec((per_group, 8, own_channels), lambda i: (i, logs_row, 0))
+    all_params = [wide(mix_row), wide(mix_row + 1), logs_spec]
+    part_params = [logs_part, narrow(mix_row), narrow(mix_row + 1)]
 
     mat = lambda r, c: vm(r, c, dtype=bf16)
     dma = pltpu.SemaphoreType.DMA
@@ -1703,7 +1840,7 @@
     x1, inner_a, act_a, u, ends, *done = pl.pallas_call(
         ffa_forward_kernel,
         grid=(rows // BOTH,),
-        in_specs=[row_spec(frames, D, BOTH), small_spec, ANY, whole_spec(HEADS * NST, frames)]
+        in_specs=[row_spec(frames, D, BOTH), small_spec, ANY, logs_spec]
         + any_one,
         out_specs=[
             row_spec(frames, D, BOTH),
@@ -1721,34 +1858,30 @@
             shape((rows, NST, D), bf16),
         ]
         + pair_out,
-        scratch_shapes=[mat(D, FF), mat(FF, D), mat(D, D), dma] + pair_sems,
+        scratch_shapes=[mat(D, FF), mat(FF, D), mat(D, D), mat(frames, HEADS * NST), dma] + pair_sems,
         input_output_aliases={4: 5} if spread_out else {},
         compiler_params=talking(7) if spread_out else PARAMS,
         name="ffa_forward",
-    )(features, small_params, first, mfin, *pair_in)
+    )(features, small_params, first, packed, *pair_in)
     if spread_out:
         pair = done[0].reshape(-1, BS, BS)
 
     group_spec = pl.BlockSpec((rows, frames, LANES), lambda i: (0, 0, i))
-    tab_a_spec = pl.BlockSpec((2,) + tab_a.shape[1:], lambda i: (i, 0, 0, 0))
-    tab_b_spec = pl.BlockSpec((2,) + tab_b.shape[1:], lambda i: (i, 0, 0, 0))
-    power_spec = pl.BlockSpec((2,) + power.shape[1:], lambda i: (i, 0, 0, 0))
     coup_spec = pl.BlockSpec((NST, LANES), lambda i: (0, i))
-    taps_spec = pl.BlockSpec((SUB, SUB, LANES), lambda i: (0, 0, i))
     swap_scratch = [dma, dma((parts - 1,)), dma((parts - 1,))]
     all_states = shape((parts, rows, NST, D), bf16)
     y_loc, ends_all, *done = pl.pallas_call(
         conv_forward_kernel,
         grid=(D // LANES,),
-        in_specs=[group_spec, ANY, tab_a_spec, tab_b_spec, power_spec, coup_spec, taps_spec]
+        in_specs=[group_spec, ANY] + part_params
         + any_one,
         out_specs=[group_spec, ANY] + any_one,
         out_shape=[shape((rows, frames, D)), all_states] + rest_out,
-        scratch_shapes=[vm(SUB + frames, LANES)] + swap_scratch + rest_sems,
-        input_output_aliases={7: 2} if spread_out else {},
+        scratch_shapes=[vm(SUB + frames, LANES), vm(SUB, SUB, LANES)] + swap_scratch + rest_sems,
+        input_output_aliases={5: 2} if spread_out else {},
         compiler_params=talking(3),
         name="conv_forward",
-    )(u, ends, tab_a, tab_b, power, coupling, taps_f, *rest_in)
+    )(u, ends, packed, packed, packed, *rest_in)
 
     edge_spec = pl.BlockSpec((1, PAD, D), lambda i: (i, 0, 0))
     edge_scratch = [
@@ -1765,14 +1898,10 @@
         in_specs=[
             row_spec(frames, D),
             states_spec,
-            state_spec,
-            whole_spec(parts + 1, NST, D),
-            flat_spec,
-            row_spec(frames, D),
-            small_spec,
-            ANY,
-            whole_spec(frames, HEADS * NST),
+            starts_spec,
         ]
+        + all_params
+        + [row_spec(frames, D), small_spec, ANY]
         + any_one,
         out_specs=[
             row_spec(frames, D),
@@ -1794,12 +1923,13 @@
         + edge_shapes
         + rest_out,
         scratch_shapes=[mat(D, 2 * D), mat(D, 2 * D), vm(HEADS * NST, D), dma]
+        + [mat(frames, HEADS * NST), vm(parts + 1, NST, D), vm(NST, D)]
         + edge_scratch
         + rest_sems,
         input_output_aliases={9: 7} if spread_out else {},
         compiler_params=talking(4),
         name="mixer_out",
-    )(y_loc, ends_all, starts, weigh_in, coupling, x1, small_params, pair, pfull, *done)
+    )(y_loc, ends_all, packed, packed, packed, packed, x1, small_params, pair, *done)
     if spread_out:
         rest = done[0].reshape(-1, BS, BS)
 
@@ -1877,7 +2007,7 @@
             row_spec(frames, D),
             small_spec,
             ANY,
-            whole_spec(HEADS * NST, frames),
+            logs_spec,
         ]
         + [ANY] * spread_back,
         out_specs=[
@@ -1910,29 +2040,26 @@
             vm(4 * mix, BS, BS, dtype=bf16),
         ]
         + kept(D, 2 * D, D, 2 * D)
-        + [dma]
+        + [mat(frames, HEADS * NST), dma]
         + (square_bufs(sizes[2], parts, levels, slab) + reduce_sems(R_XY, 2)) * spread_back,
         compiler_params=talking(8) if spread_back else PARAMS,
         name="mixer_back",
     )(
         dq, d_low, d_high, g, g_low, g_high, pw, x2, gated, ys, dx3, small_params, pair,
-        pfull_t, *[unflat(grads_rest, 2)] * spread_back,
+        packed, *[unflat(grads_rest, 2)] * spread_back,
     )
 
     nst_spec = pl.BlockSpec((rows, NST, LANES), lambda i: (0, 0, i))
-    du_loc, t_one, t_two, ends_w, back_w, lag_grads, back_all = pl.pallas_call(
+    du_loc, t_one, t_two, ends_w, back_w, back_all = pl.pallas_call(
         conv_back_kernel,
         grid=(D // LANES,),
-        in_specs=[
-            group_spec, group_spec, ANY, tab_a_spec, tab_b_spec, power_spec, coup_spec, taps_spec
-        ],
+        in_specs=[group_spec, group_spec, ANY] + part_params,
         out_specs=[
             group_spec,
             coup_spec,
             coup_spec,
             nst_spec,
             nst_spec,
-            pl.BlockSpec((SUB, LANES), lambda i: (0, i)),
             ANY,
         ],
         out_shape=[
@@ -1941,20 +2068,21 @@
             shape((NST, D)),
             shape((rows, NST, D)),
             shape((rows, NST, D)),
-            shape((SUB, D)),
             all_states,
         ],
         scratch_shapes=[
             vm(SUB + frames, LANES),
             vm(SUB + frames, LANES),
             vm(SUB, SUB, LANES),
+            vm(SUB, SUB, LANES),
         ]
         + swap_scratch,
         compiler_params=talking(6),
         name="conv_back",
-    )(u, dy, back_ends, tab_a, tab_b, power, coupling, taps_b)
-
-    grad_zero, grads_first, gain_a, sums_c, *shares = pl.pallas_call(
+    )(u, dy, back_ends, packed, packed, packed)
+
+    small_rows = -(-small_params.shape[0] // 8) * 8 + 3 * NST
+    grad_zero, grads_first, small_all, *shares = pl.pallas_call(
         partial(ffa_back_kernel, scaling),
         grid=(rows,),
         in_specs=[
@@ -1964,9 +2092,15 @@
             state_spec,
             state_spec,
             state_spec,
-            state_spec,
-            whole_spec(3, parts, NST, D),
+            starts_spec,
+        ]
+        + all_params
+        + [
             flat_spec,
+            flat_spec,
+            whole_spec(2, 8, D),
+            whole_spec(8, D),
+            whole_spec(16, D),
             row_spec(frames, D),
             row_spec(frames, D),
             row_spec(frames, FF),
@@ -1974,16 +2108,14 @@
             row_spec(frames, D),
             small_spec,
             ANY,
-            whole_spec(frames, HEADS * NST),
         ]
         + [ANY, whole_spec(sizes[2], 2, 2, slab, BS)] * spread_back,
-        out_specs=[row_spec(frames, D), ANY, whole_spec(2, 8, D), whole_spec(4, NST, D)]
+        out_specs=[row_spec(frames, D), ANY, whole_spec(parts, small_rows, own_channels)]
         + [whole_spec(n, slab, BS) for n in sizes[1:]] * spread_back,
         out_shape=[
             shape((rows, frames, D)),
             flat_shapes[0],
-            shape((2, 8, D)),
-            shape((4, NST, D)),
+            shape((parts, small_rows, own_channels)),
         ]
         + [shape((n, slab, BS), bf16) for n in sizes[1:]] * spread_back,
         scratch_shapes=[
@@ -1997,7 +2129,8 @@
             vm(2 * ffn + mix, BS, BS, dtype=bf16),
         ]
         + kept(FF, FF, D, D, D, D)
-        + [dma]
+        + [dma, vm(2, 8, D), vm(4, NST, D), mat(frames, HEADS * NST)]
+        + [vm(3, parts, NST, D), vm(NST, D)]
         + (
             [vm(sizes[2], 2, 2, slab, BS, dtype=bf16)]
             + level_bufs(sizes[2], slab)
@@ -2010,69 +2143,33 @@
         compiler_params=talking(9) if spread_back else PARAMS,
         name="ffa_back",
     )(
-        du_loc, back_all, ends_all, back_ends, ends_w, back_w, starts, weigh_back, coupling,
-        x1, features, inner_a, act_a, dx2, small_params, first, mfin_t,
+        du_loc, back_all, ends_all, back_ends, ends_w, back_w, packed, packed, packed, packed,
+        t_one, t_two, gain_b, gain_c, kernel_grads,
+        x1, features, inner_a, act_a, dx2, small_params, first,
         *([unflat(grads_pair, 1)] + red_rest) * spread_back,
     )
 
-    lag_grad_c = jnp.sum(lag_decay * lag_grads[:, None, :], axis=0)
-    lag_grad_r = jnp.sum(lag_decay * (lag[:, None] * lag_grads)[:, None, :], axis=0)
-    d_coup = t_one + lag_grad_c + sums_c[0]
-    start_back = sums_c[1] * begin_w
-    d_first = d_coup * mix_all[1]
-    d_second = d_coup * mix_all[0] + start_back
-    d_rate = coupling * (t_two + lag_grad_r + sums_c[3])
-    d_rate = d_rate + mix_all[1] * (begin * start_back + begin_w * sums_c[2])
-    small_grads = [
-        jnp.sum(gain_a, axis=1),
-        jnp.sum(gain_c, axis=0, keepdims=True),
-        jnp.sum(gain_b, axis=1),
-        kernel_grads[:KW],
-    ]
-    stacked = jnp.concatenate(small_grads + [d_first, d_second, d_rate], axis=0) * scaling
-    stacked = jnp.pad(stacked, ((0, -stacked.shape[0] % 8), (0, 0)))
-    own = place * own_channels
-    lanes_own = lambda v: lax.dynamic_slice_in_dim(v, own, own_channels, v.ndim - 1)
-    stacked = stacked.reshape(-1, parts, own_channels).transpose(1, 0, 2)
     full_grad, owned, sums = reduce_grads(
         unflat(grads_first, 0),
         *(shares if spread_back else (grads_pair, grads_rest)),
-        stacked,
+        small_all,
         parts,
         devices,
         slab,
     )
-    count_small = small_params.shape[0]
-    small_sum = sums[:count_small]
-    mix_sum = sums[count_small : count_small + 2 * NST]
-    mix_sum = mix_sum.reshape(2, NST, own_channels).transpose(0, 2, 1)
-    rate_sum = sums[count_small + 2 * NST : count_small + 3 * NST]
-    rate_sum = jnp.sum(rate_sum.reshape(NST, own_heads, HALF), axis=2)
-    decay_sum = -rate_sum.T * jnp.exp(decay_logs)
-    new_small = lanes_own(small_params) - rate_small * small_sum
-    new_decay = decay_logs - rate_small * decay_sum
-    new_mix = state_mix - rate_small * mix_sum
-
-    shard_w = jnp.exp(-lanes_own(rate_nc)[None] * (shard.astype(f32) * span)[:, None, None])
-    start_grad = jnp.sum(lanes_own(back_all).astype(f32) * shard_w[:, None], axis=0) * lanes_own(mix_all[1])
-    start_grad = start_grad.transpose(0, 2, 1)
-    chosen = (state_source[None, :] == jnp.arange(rows, dtype=jnp.int32)[:, None]).astype(f32)
-    grad_state = jnp.sum(chosen[:, :, None, None] * start_grad[None], axis=1)
-
     count, slice_rows = owned.shape[0], owned.shape[1]
-    mine = lax.axis_index("rows") * slice_rows
-    pick = (
-        jnp.arange(slice_rows, dtype=jnp.int32)[:, None] + mine
-        == jnp.arange(BS, dtype=jnp.int32)[None, :]
-    ).astype(bf16)
     group = 11 if count % 11 == 0 else 1
     part_spec = pl.BlockSpec((group, slice_rows, BS), lambda i: (i, 0, 0))
     full_spec = pl.BlockSpec((group, BS, BS), lambda i: (i, 0, 0))
-    new_left, new_right, new_master, new_copy, grad_blocks = pl.pallas_call(
-        shampoo_kernel,
+    small_shape = (small_params.shape[0], own_channels)
+    carry_spec = row_spec(frames, D, rows * group // count)
+    small_outs = [small_shape, small_shape, decay_logs.shape, mix_t.shape]
+    small_outs += [decay_logs.shape, mix_t.shape, bank_t.shape]
+    new_left, new_right, new_master, new_copy, grad_blocks, *others = pl.pallas_call(
+        partial(shampoo_kernel, frames),
         grid=(count // group,),
         in_specs=[
-            whole_spec(slice_rows, BS),
+            pl.BlockSpec(memory_space=pltpu.SMEM),
             part_spec,
             full_spec,
             part_spec,
@@ -2080,18 +2177,35 @@
             part_spec,
             full_spec,
             part_spec,
+            whole_spec(*sums.shape),
+            whole_spec(*small_params.shape),
+            whole_spec(*decay_logs.shape),
+            whole_spec(*mix_t.shape),
+            whole_spec(*back_all.shape),
+            carry_spec,
+            carry_spec,
         ],
-        out_specs=[part_spec] * 5,
+        out_specs=[part_spec] * 5 + [whole_spec(*dims) for dims in small_outs]
+        + [carry_spec] * 2,
         out_shape=[
             shape(owned.shape),
             shape(owned.shape),
             shape(owned.shape),
             shape(owned.shape, bf16),
             shape(owned.shape),
-        ],
+        ]
+        + [shape(dims) for dims in small_outs]
+        + [shape(layer_out.shape, bf16), shape(grad_zero.shape)],
         compiler_params=PARAMS,
         name="shampoo",
-    )(pick, owned, full_grad, left_stats, right_stats, left_root, right_root, master)
+    )(
+        state_source, owned, full_grad, left_stats, right_stats, left_root, right_root, master,
+        sums, small_params, decay_logs, mix_t, back_all, layer_out, grad_zero,
+    )
+    *small_results, grad_state, layer_out, grad_zero = others
+    for i in (3, 5):
+        small_results[i] = small_results[i].transpose(0, 2, 1)
+    grad_state = grad_state.transpose(0, 2, 1)
     return (
         layer_out,
         grad_zero,
@@ -2101,12 +2215,7 @@
         new_right,
         new_master,
         new_copy,
-        small_sum,
-        new_small,
-        decay_sum,
-        mix_sum,
-        new_decay,
-        new_mix,
+        *small_results,
     )
 
 

time: 392 us -> 362 us (0.923)
  local copies, waits for them, and re-layouts: 17.3 us -> 0 us
  other arithmetic: 15.9 us -> 0 us
    unnamed x38 -> x0, local copies, waits for them, and re-layouts: 7.64 us -> none
where the time goes in v2:
time: 362 us; the launch traced here: 355 us
  Pallas kernels  353 us (98%)
    pallas_call x1, Pallas kernels, reduce_grads(): pl.pallas_call(partial(reduce_kernel, sizes, runs, groups), in_specs=[ANY...  73.6 us
    pallas_call x1, Pallas kernels, body(): pl.pallas_call(partial(ffb_kernel, scaling), grid=(rows,), in_specs=[row_...  53.5 us
    pallas_call x1, Pallas kernels, body(): pl.pallas_call(partial(ffa_back_kernel, scaling), grid=(rows,), in_specs=...  43.1 us
    pallas_call x1, Pallas kernels, gather_first(): pl.pallas_call(gather_kernel, in_specs=[pl.BlockSpec(memory_space=pltpu.S...  42 us
    pallas_call x1, Pallas kernels, body(): pl.pallas_call(partial(mixer_back_kernel, scaling), grid=(rows,), in_spec...  32.8 us
    pallas_call x1, Pallas kernels, body(): pl.pallas_call(conv_forward_kernel, grid=(D // LANES,), in_specs=[group_s...  25.6 us
    pallas_call x1, Pallas kernels, body(): pl.pallas_call(conv_back_kernel, grid=(D // LANES,), in_specs=[group_spec...  23.6 us
    pallas_call x1, Pallas kernels, body(): pl.pallas_call(mixer_out_kernel, grid=(rows,), in_specs=[row_spec(frames,...  23.2 us

profile of v2, /device:TPU:0, one launch (start us, length us, event | category | flops | bytes accessed | tf_op | source)
XLA Modules:
  0.0 354.6 jit_solution(10936166547722038028)
XLA Ops:
  0.6 42.0 %gather_first.1 = (bf16[4,9,4,2,32,256]{5,4,3,2,1,0:T(8,128)(2,1)}, bf16[4,4,4,2,32,256]{5,4,3,2,1,0:T(8,128)(2,1)}, bf16[4,9,4,2,32,256]{5,4,3,2,1,0:T(8,128)(2,1)}, f32[4,264,128]{2,1,0:T(8,128)}) custom-call(s32[6]{0:T(128)} %source.3, f32[22,32,256]{2,1,0:T(8,128)} %master.3, f32[6,32,128]{2,1,0:T(8,128)} %bitcast.23, f32[2,32,128]{2,1,0:T(8,128)} %bitcast.21, ...), custom_call_target="tpu_custom_call" | custom-call | tf_op jit(solution)/shard_map/gather_first/pallas_call | solution.py:491
  42.7 22.5 %ffa_forward.1 = (f32[6,320,512]{2,1,0:T(8,128)}, bf16[6,320,2048]{2,1,0:T(8,128)(2,1)}, bf16[6,320,2048]{2,1,0:T(8,128)(2,1)}, bf16[6,320,512]{2,1,0:T(8,128)(2...) custom-call(bf16[6,320,512]{2,1,0:T(8,128)(2,1)} %feat.3, ...), custom_call_target="tpu_custom_call", output_to_operand_aliasing={{5}: (4, {})} | custom-call | tf_op jit(solution)/shard_map/ffa_forward/pallas_call | solution.py:1840
  65.2 25.6 %conv_forward.1 = (f32[6,320,512]{2,1,0:T(8,128)}, bf16[4,6,32,512]{3,2,1,0:T(8,128)(2,1)}, bf16[4,9,4,2,32,256]{5,4,3,2,1,0:T(8,128)(2,1)}) custom-call(bf16[6,320,512]{2,1,0:T(8,128)(2,1)} %get-tuple-element.80.u, bf16[6,32,512]{2,1,0:T(8,128)(2,1)} %get-tuple-element.81.ends, ...), custom_call_target="tpu_custom_call", output_to_operand_aliasing={{2}: (5, {})} | custom-call | tf_op jit(solution)/shard_map/conv_forward/pallas_call | solution.py:1873
  90.8 23.2 %mixer_out.1 = (bf16[6,320,512]{2,1,0:T(8,128)(2,1)}, bf16[6,320,1024]{2,1,0:T(8,128)(2,1)}, f32[6,320,512]{2,1,0:T(8,128)}, bf16[6,320,1024]{2,1,0:T(8,128)(2,1...) custom-call(f32[6,320,512]{2,1,0:T(8,128)} %get-tuple-element.83.y, ...), custom_call_target="tpu_custom_call", output_to_operand_aliasing={{7}: (9, {})} | custom-call | tf_op jit(solution)/shard_map/mixer_out/pallas_call | solution.py:1895
  114.0 53.5 %ffb.1 = (bf16[6,320,512]{2,1,0:T(8,128)(2,1)}, f32[6,320,512]{2,1,0:T(8,128)}, bf16[6,320,512]{2,1,0:T(8,128)(2,1)}, bf16[36,256,256]{2,1,0:T(8,128)(2,1)}, f32...) custom-call(bf16[6,320,512]{2,1,0:T(8,128)(2,1)} %get-tuple-element.88.g, ...), custom_call_target="tpu_custom_call" | custom-call | tf_op jit(solution)/shard_map/ffb/pallas_call | solution.py:1946
  167.6 32.8 %mixer_back.1 = (f32[6,320,512]{2,1,0:T(8,128)}, bf16[6,320,512]{2,1,0:T(8,128)(2,1)}, bf16[6,32,512]{2,1,0:T(8,128)(2,1)}, bf16[16,256,256]{2,1,0:T(8,128)(2,1)...) custom-call(bf16[6,320,512]{2,1,0:T(8,128)(2,1)} %get-tuple-element.93.dq, ...), custom_call_target="tpu_custom_call" | custom-call | tf_op jit(solution)/shard_map/mixer_back/pallas_call | solution.py:1993
  200.4 23.6 %conv_back.1 = (f32[6,320,512]{2,1,0:T(8,128)}, f32[32,512]{1,0:T(8,128)}, f32[32,512]{1,0:T(8,128)}, f32[6,32,512]{2,1,0:T(8,128)}, f32[6,32,512]{2,1,0:T(8,128)}, /*index=5*/bf16[4,6,32,512]{3,2,1,0:T(8,128)(2,1)}) custom-call(bf16[6,320,512]{2,1,0:T(8,128)(2,1)} %get-tuple-element.80.u, bf16[6,320,512]{2,1,0:T(8,128)(2,1)} %get-tuple-element.101.dy, ...), custom_call_target="tpu_custom_call" | custom-call | tf_op jit(solution)/shard_map/conv_back/pallas_call | solution.py:2053
  223.9 43.1 %ffa_back.1 = (f32[6,320,512]{2,1,0:T(8,128)}, bf16[36,256,256]{2,1,0:T(8,128)(2,1)}, f32[4,120,128]{2,1,0:T(8,128)}, bf16[4,32,256]{2,1,0:T(8,128)(2,1)}, bf16[9,32,256]{2,1,0:T(8,128)(2,1)}) custom-call(f32[6,320,512]{2,1,0:T(8,128)} %get-tuple-element.103.du_loc, bf16[4,6,32,512]{3,2,1,0:T(8,128)(2,1)} %get-tuple-element.104.back_all, ...), custom_call_target="tpu_custom_call" | custom-call | tf_op jit(solution)/shard_map/ffa_back/pallas_call | solution.py:2085
  267.0 73.6 %reduce_grads.1 = (bf16[22,2,2,2,32,256]{5,4,3,2,1,0:T(8,128)(2,1)}, bf16[22,32,256]{2,1,0:T(8,128)(2,1)}, f32[120,128]{1,0:T(8,128)}) custom-call(bf16[4,9,4,2,32,256]{5,4,3,2,1,0:T(8,128)(2,1)} %bitcast.18, bf16[4,32,256]{2,1,0:T(8,128)(2,1)} %get-tuple-element.118.share_pair, bf16[9,32,256]{2,1,0:T(8,128)(2,1)} %get-tuple-element.119.share_rest, ...), custom_call_target="tpu_custom_call" | custom-call | tf_op jit(solution)/shard_map/reduce_grads/pallas_call | solution.py:1737
  340.7 13.5 %shampoo.1 = (f32[22,32,256]{2,1,0:T(8,128)}, f32[22,32,256]{2,1,0:T(8,128)}, f32[22,32,256]{2,1,0:T(8,128)}, bf16[22,32,256]{2,1,0:T(8,128)(2,1)}, f32[22,32,25...) custom-call(s32[6]{0:T(128)} %source.3, ...), custom_call_target="tpu_custom_call" | custom-call | tf_op jit(solution)/shard_map/shampoo/pallas_call | solution.py:2168
